TPU v7x, 32 devices: a whole 2x2x4 slice. The times are simulated.
32 devices in a mesh: parts: 2 (over y), row: 16 (over z, x, core).
Axes of the slice: x: 2, y: 2, z: 4, core: 2. Of those that a mesh axis runs over, the one named last changes fastest.
Arguments:
- traces: bfloat16 [256, 2, 12000], P(('parts', 'row')), parts along dimension 0, may hold values from -160 to 160
- valid_mask: int32 [256, 2], P(('parts', 'row')), parts along dimension 0, may hold values 0 or 1
- pair_table: int32 [32, 10], P(('parts', 'row')), parts along dimension 0, may hold values from 0 to 15, as said below
- stack_in: float32 [32, 10, 8, 8, 401], P(('parts', 'row')), parts along dimension 0, may hold values from -6 to 6
Outputs:
- stacks: float32 [32, 10, 8, 8, 401], P(('parts', 'row')), parts along dimension 0
There are 2 independent parts, one for each index of `parts`. A program takes and returns all parts, laid end to end along the dimension named above; each array names one. Nothing has to cross between parts.
Inputs may be any that keep to these rules, and one draw needn't show every extreme that they name: `pair_table`: row i lists the panels (i + k) mod 16 for k = -1 to 8, each once, in an order that varies from row to row.
All inputs are finite; a program needn't handle non-finite values. No bound on the sum of `valid_mask` on one device may be relied on, other than what follows from the above.
Results may differ from a plain program's by a relative error of at most 0.0032.
Values may be sent and summed in bfloat16 or wider, within the bound.
No kernel may reach another device: no remote copies, remote signals or barrier semaphores. Data moves between devices by JAX's collectives and lax.ppermute only.
A program may use at most 128 MiB of HBM per device.

v0:
```python
import math

import jax
import jax.numpy as jnp
from jax import lax
from jax.sharding import PartitionSpec as P

SAMPLES = 12000
FLO = 6
BINS = 595
HALF = 40
LAGS = 401


epsilon = 1e-06


def spectra_of(rows, samples, first_bin, bins):
    length = samples // 8
    freq = first_bin + jnp.arange(bins, dtype=jnp.int32)

    def absorb(totals, block_index):
        first_row = block_index * length
        segment = lax.dynamic_slice_in_dim(rows, first_row, length, 1)
        times = first_row + jnp.arange(length, dtype=jnp.int32)
        angle = (times[:, None] * freq[None, :] % samples).astype(jnp.float32) * (
            2.0 * math.pi / samples
        )
        table = jnp.concatenate([jnp.cos(angle), -jnp.sin(angle)], axis=1).astype(jnp.bfloat16)
        return (totals + jnp.dot(segment, table, preferred_element_type=jnp.float32), None)

    start_total = jnp.zeros((rows.shape[0], 2 * bins), jnp.float32)
    totals, unused = lax.scan(absorb, start_total, jnp.arange(8, dtype=jnp.int32))
    return totals


def whiten_rows(traces, valid_mask, first_bin, bins, half_width):
    chans, minutes, samples = traces.shape
    spectrum = spectra_of(traces.reshape(chans * minutes, samples), samples, first_bin, bins)
    real_part = spectrum[:, :bins]
    imag_part = spectrum[:, bins:]
    power = real_part * real_part + imag_part * imag_part
    positions = jnp.arange(bins, dtype=jnp.int32)
    near = (jnp.abs(positions[:, None] - positions[None, :]) <= half_width).astype(jnp.float32)
    window = near / jnp.sum(near, axis=0, keepdims=True)
    smooth = jnp.dot(power, window, precision=lax.Precision.HIGHEST)
    divisor = jnp.sqrt(smooth + epsilon)
    flags = valid_mask.reshape(-1, 1).astype(jnp.float32)
    whitened = spectrum * flags / jnp.concatenate([divisor, divisor], axis=1)
    return whitened.astype(jnp.bfloat16).reshape(chans, minutes, 2 * bins)


def lag_matrix(first_bin, bins, lags, samples):
    freq = first_bin + jnp.arange(bins, dtype=jnp.int32)
    shifts = jnp.arange(lags, dtype=jnp.int32) - (lags - 1) // 2
    angle = (freq[:, None] * shifts[None, :] % samples).astype(jnp.float32) * (
        2.0 * math.pi / samples
    )
    return jnp.concatenate([jnp.cos(angle), -jnp.sin(angle)], axis=0).astype(jnp.bfloat16)


def tile_corr(own_white, own_flags, partner_white, partner_flags, lag_table):
    bins = lag_table.shape[0] // 2
    own = own_white.astype(jnp.float32)
    partner = partner_white.astype(jnp.float32)
    shape = (partner.shape[0], own.shape[0], partner.shape[1], bins)
    real_sum = jnp.zeros(shape, jnp.float32)
    imag_sum = jnp.zeros(shape, jnp.float32)
    joint_sum = jnp.zeros(shape[:3], jnp.float32)
    for minute in range(own.shape[1]):
        own_real = own[:, minute, :bins][None, :, None, :]
        own_imag = own[:, minute, bins:][None, :, None, :]
        part_real = partner[:, :, minute, :bins][:, None, :, :]
        part_imag = partner[:, :, minute, bins:][:, None, :, :]
        real_sum = real_sum + (own_real * part_real + own_imag * part_imag)
        imag_sum = imag_sum + (own_imag * part_real - own_real * part_imag)
        own_valid = own_flags[:, minute].astype(jnp.float32)[None, :, None]
        part_valid = partner_flags[:, :, minute].astype(jnp.float32)[:, None, :]
        joint_sum = joint_sum + own_valid * part_valid
    inverse = 1.0 / jnp.maximum(joint_sum, 1.0)
    cross = (jnp.concatenate([real_sum, imag_sum], axis=-1) * inverse[..., None]).astype(
        jnp.bfloat16
    )
    corr = jnp.dot(cross.reshape(-1, 2 * bins), lag_table, preferred_element_type=jnp.float32) * (
        1.0 / math.sqrt(bins)
    )
    return corr.reshape(shape[0], shape[1], shape[2], lag_table.shape[1])


def shards(traces, valid_mask, pair_table, stack_in):
    panel_count = lax.axis_size("row")
    chans = traces.shape[0]
    minutes = traces.shape[1]
    whitened = whiten_rows(traces, valid_mask, FLO, BINS, HALF)
    own_flags = valid_mask.astype(jnp.bfloat16)
    lag_table = lag_matrix(FLO, BINS, LAGS, SAMPLES)
    table_row = pair_table[0]
    base_stack = stack_in[0]
    whole_white, whole_flags = (
        lax.all_gather(whitened, "row", axis=0, tiled=True),
        lax.all_gather(own_flags, "row", axis=0, tiled=True),
    )
    panels = whole_white.reshape(panel_count, chans, minutes, whitened.shape[2])
    panel_flags = whole_flags.reshape(panel_count, chans, minutes)
    partner = jnp.take(panels, table_row, axis=0)
    partner_flags = jnp.take(panel_flags, table_row, axis=0)
    result = base_stack + tile_corr(whitened, own_flags, partner, partner_flags, lag_table)
    return result[None]


def solution(mesh):
    in_specs = (
        P(("parts", "row"), None, None),
        P(("parts", "row"), None),
        P(("parts", "row"), None),
        P(("parts", "row"), None, None, None, None),
    )
    out_specs = P(("parts", "row"), None, None, None, None)
    return jax.shard_map(shards, mesh=mesh, in_specs=in_specs, out_specs=out_specs, check_vma=False)
```

profile of v0, /device:TPU:0, one launch (start us, length us, event | category | flops | bytes accessed | tf_op | source)
XLA Modules:
  0.0 214.5 jit_solution(12585721607296174629)
XLA Ops:
  0.0 0.7 compare_and_fusion
  0.7 0.7 fusion.46
  1.3 0.8 fusion.52
  2.1 0.1 copy.33
  2.2 0.1 convert_element_type.89
  2.3 0.1 convert_reduce_fusion
  2.4 23.0 %all-gather = bf16[16,8,2]{1,2,0:T(2,128)(2,1)S(1)} all-gather(bf16[1,8,2]{1,2,0:T(2,128)(2,1)S(1)} %bitcast.50), channel_id=1, replica_groups=mesh['parts'=2,'row'=16] {'row'}, dimensions={0}, use_global_device_ids=true | all-gather | bytes 544 | tf_op jit(solution)/shard_map/all_gather | solution.py:101
  25.4 0.6 gather_fusion.1
  25.9 0.1 copy.34
  26.1 0.1 copy.35
  26.1 0.1 copy.36
  26.2 0.1 maximum_divide_fusion.1
  26.3 0.1 div.25
  26.4 1.3 reshape.162
  27.7 151.3 %while.13 = (s32[]{:T(128)}, f32[16,1190]{1,0:T(8,128)S(1)}, s32[8]{0:T(128)S(1)}, bf16[16,12000]{1,0:T(8,128)(2,1)S(1)}, s32[]{:T(128)}, /*index=5*/s32[1]{0:T(128)}, s32[]{:T(128)}, s32[]{:T(128)}) while((s32[]{:T(128)}, f32[16,1190]{1,0:T(8,128)S(1)}, s32[8]{0:T(128)S(1)}, bf16[16,12000]{1,0:T(8,128)(2,1)S(1)}, s32[]{:T(128)}, ...), condition=%wide.region_1.2_spmd.clone, body=%wide.region_0.1_spmd.clone.sunk | while | flops 75010184 | bytes 7644401 | solution.py:33
  27.7 0.7 dynamic_slice.20
  29.0 16.6 %cosine_convert_fusion.3 = (bf16[1500,595]{1,0:T(8,128)(2,1)S(1)}, bf16[1500,595]{1,0:T(8,128)(2,1)S(1)}) fusion(s32[595]{0:T(1024)S(1)} %iota_add_fusion.6, s32[1500]{0:T(1024)S(1)} %iota_add_fusion.7), kind=kLoop, calls=%fused_computation.11.clone.1 | loop fusion | flops 10710000 | bytes 3578380 | tf_op jit(solution)/shard_map/convert
  45.6 1.0 fusion.58
  46.6 0.6 dynamic_slice.20
  47.9 16.6 %cosine_convert_fusion.3 = (bf16[1500,595]{1,0:T(8,128)(2,1)S(1)}, bf16[1500,595]{1,0:T(8,128)(2,1)S(1)}) fusion(s32[595]{0:T(1024)S(1)} %iota_add_fusion.6, s32[1500]{0:T(1024)S(1)} %iota_add_fusion.7), kind=kLoop, calls=%fused_computation.11.clone.1 | loop fusion | flops 10710000 | bytes 3578380 | tf_op jit(solution)/shard_map/convert
  64.5 1.0 fusion.58
  65.5 0.6 dynamic_slice.20
  66.8 16.6 %cosine_convert_fusion.3 = (bf16[1500,595]{1,0:T(8,128)(2,1)S(1)}, bf16[1500,595]{1,0:T(8,128)(2,1)S(1)}) fusion(s32[595]{0:T(1024)S(1)} %iota_add_fusion.6, s32[1500]{0:T(1024)S(1)} %iota_add_fusion.7), kind=kLoop, calls=%fused_computation.11.clone.1 | loop fusion | flops 10710000 | bytes 3578380 | tf_op jit(solution)/shard_map/convert
  83.4 1.0 fusion.58
  84.4 0.6 dynamic_slice.20
  85.7 16.6 %cosine_convert_fusion.3 = (bf16[1500,595]{1,0:T(8,128)(2,1)S(1)}, bf16[1500,595]{1,0:T(8,128)(2,1)S(1)}) fusion(s32[595]{0:T(1024)S(1)} %iota_add_fusion.6, s32[1500]{0:T(1024)S(1)} %iota_add_fusion.7), kind=kLoop, calls=%fused_computation.11.clone.1 | loop fusion | flops 10710000 | bytes 3578380 | tf_op jit(solution)/shard_map/convert
  102.3 1.0 fusion.58
  103.3 0.6 dynamic_slice.20
  104.6 16.6 %cosine_convert_fusion.3 = (bf16[1500,595]{1,0:T(8,128)(2,1)S(1)}, bf16[1500,595]{1,0:T(8,128)(2,1)S(1)}) fusion(s32[595]{0:T(1024)S(1)} %iota_add_fusion.6, s32[1500]{0:T(1024)S(1)} %iota_add_fusion.7), kind=kLoop, calls=%fused_computation.11.clone.1 | loop fusion | flops 10710000 | bytes 3578380 | tf_op jit(solution)/shard_map/convert
  121.2 1.0 fusion.58
  122.2 0.6 dynamic_slice.20
  123.5 16.6 %cosine_convert_fusion.3 = (bf16[1500,595]{1,0:T(8,128)(2,1)S(1)}, bf16[1500,595]{1,0:T(8,128)(2,1)S(1)}) fusion(s32[595]{0:T(1024)S(1)} %iota_add_fusion.6, s32[1500]{0:T(1024)S(1)} %iota_add_fusion.7), kind=kLoop, calls=%fused_computation.11.clone.1 | loop fusion | flops 10710000 | bytes 3578380 | tf_op jit(solution)/shard_map/convert
  140.1 1.0 fusion.58
  141.1 0.6 dynamic_slice.20
  142.4 16.6 %cosine_convert_fusion.3 = (bf16[1500,595]{1,0:T(8,128)(2,1)S(1)}, bf16[1500,595]{1,0:T(8,128)(2,1)S(1)}) fusion(s32[595]{0:T(1024)S(1)} %iota_add_fusion.6, s32[1500]{0:T(1024)S(1)} %iota_add_fusion.7), kind=kLoop, calls=%fused_computation.11.clone.1 | loop fusion | flops 10710000 | bytes 3578380 | tf_op jit(solution)/shard_map/convert
  159.0 1.0 fusion.58
  160.0 0.6 dynamic_slice.20
  161.3 16.6 %cosine_convert_fusion.3 = (bf16[1500,595]{1,0:T(8,128)(2,1)S(1)}, bf16[1500,595]{1,0:T(8,128)(2,1)S(1)}) fusion(s32[595]{0:T(1024)S(1)} %iota_add_fusion.6, s32[1500]{0:T(1024)S(1)} %iota_add_fusion.7), kind=kLoop, calls=%fused_computation.11.clone.1 | loop fusion | flops 10710000 | bytes 3578380 | tf_op jit(solution)/shard_map/convert
  177.9 1.0 fusion.58
  179.0 0.8 fusion.34
  179.8 0.1 fusion.38
  179.9 0.1 fusion.51
  180.1 19.4 %all_gather.6 = bf16[128,2,1190]{2,1,0:T(2,128)(2,1)S(1)} all-gather(bf16[8,2,1190]{2,1,0:T(2,128)(2,1)S(1)} %reshape.163), channel_id=1, replica_groups=mesh['parts'=2,'row'=16] {'row'}, dimensions={0}, use_global_device_ids=true | all-gather | bytes 647360 | tf_op jit(solution)/shard_map/all_gather | solution.py:100
  199.4 1.4 gather_fusion
  200.9 0.4 fusion.37
  201.3 1.2 fusion.50
  202.6 5.6 %cosine_convert_fusion.1 = (bf16[595,401]{1,0:T(8,128)(2,1)S(1)}, bf16[595,401]{1,0:T(8,128)(2,1)S(1)}) fusion(s32[401]{0:T(512)S(1)} %iota_add_fusion.3, s32[595]{0:T(1024)S(1)} %iota_add_fusion.2), kind=kLoop, calls=%fused_computation.37 | loop fusion | flops 2863140 | bytes 958364 | tf_op jit(solution)/shard_map/convert.6
  208.1 0.8 add_add_fusion
  208.9 2.4 %fusion.22 = f32[640,401]{0,1:T(8,128)} fusion(f32[640,595]{1,0:T(8,128)S(1)} %bitcast.49, f32[640,595]{1,0:T(8,128)S(1)} %bitcast.48, f32[640]{0:T(1024)S(1)} %div.25, bf16[595,401]{1,0:T(8,128)(2,1)S(1)} %get-tuple-element.110, bf16[595,401]{1,0:T(8,128)(2,1)S(1)} %get-tuple-element.109), kind=kOutput, calls=%fused_computation.33 | convolution fusion | flops 615253376 | bytes 5029900 | tf_op jit(solution)/shard_map/dot_general | solution.py:84
  211.3 0.0 copy-start
  211.3 1.7 copy.37
  213.0 0.0 copy-done
  213.1 1.4 add.141
  (29 shorter events, 0.2 us)
Async XLA Ops:
  211.3 1.7 copy-start
where the time goes:
time: 215 us; the launch traced here: 214 us
  other arithmetic  143 us (67%)
  blocking collectives  42.3 us (20%)
  local copies, waits for them, and re-layouts  12.1 us (6%)
  matrix products  11.3 us (5%)
  loops' own time  5.26 us (2%)
    another operation x9, other arithmetic  138 us
    all_gather x1, blocking collectives, shards(): lax.all_gather(own_flags, 'row', axis=0, tiled=True)  23 us
    all_gather x1, blocking collectives, shards(): lax.all_gather(whitened, 'row', axis=0, tiled=True)  19.4 us
    dot_general x8, matrix products, absorb(): jnp.dot(segment, table, preferred_element_type=jnp.float32)  8.12 us
    another operation x1, loops' own time, spectra_of(): lax.scan(absorb, start_total, jnp.arange(8, dtype=jnp.int32))  5.26 us
    dynamic_slice x8, local copies, waits for them, and re-layouts, spectra_of(): lax.scan(absorb, start_total, jnp.arange(8, dtype=jnp.int32))  5.19 us

commit v1 on v0

v1 whole, which is shorter than its diff:
```python
import math

import jax
import jax.numpy as jnp
import ml_dtypes
import numpy as np
from jax import lax
from jax.experimental import pallas as pl
from jax.experimental.pallas import tpu as pltpu
from jax.sharding import PartitionSpec as P

SAMPLES = 12000
FLO = 6
BINS = 595
HALF = 40
LAGS = 401
EPS = 1e-06

FOLD = SAMPLES // 10
LANES = 640
COLS = 512


def lane_bins():
    bins = np.full((LANES,), -1, np.int64)
    for group in range(5):
        for half in range(2):
            mine = [k for k in range(FLO, FLO + BINS) if k % 10 == group + 5 * half]
            start = group * 128 + half * 64
            bins[start : start + len(mine)] = mine
    return bins


BIN_OF = lane_bins()
USED = BIN_OF >= 0


def bf16(a):
    return np.asarray(a, np.float32).astype(ml_dtypes.bfloat16)


def fold_table():
    q = (np.arange(FOLD)[:, None] * BIN_OF[None, :]) % SAMPLES
    angle = 2.0 * np.pi * q / SAMPLES
    cos = np.where(USED, np.cos(angle), 0.0).reshape(FOLD, 5, 1, 128)
    sin = np.where(USED, -np.sin(angle), 0.0).reshape(FOLD, 5, 1, 128)
    table = np.concatenate([cos, sin], axis=2)
    order = [1, 4, 2, 3, 0]
    return bf16(table[:, order].reshape(FOLD, 5 * 256))


def near_table():
    gap = np.abs(BIN_OF[:, None] - BIN_OF[None, :])
    near = (gap <= HALF) & USED[:, None] & USED[None, :]
    count = np.maximum(near.sum(axis=0), 1)
    return bf16(near), (1.0 / count).astype(np.float32)[None, :]


def lag_table():
    tau = np.arange(LAGS) - (LAGS - 1) // 2
    q = (BIN_OF[:, None] * tau[None, :]) % SAMPLES
    angle = 2.0 * np.pi * q / SAMPLES
    table = np.zeros((2 * LANES, COLS), np.float64)
    table[:LANES, :LAGS] = np.where(USED[:, None], np.cos(angle), 0.0)
    table[LANES:, :LAGS] = np.where(USED[:, None], -np.sin(angle), 0.0)
    table[LANES - 1, COLS - 1] = 1.0
    return bf16(table)


C36, C72 = math.cos(math.pi / 5), math.cos(2 * math.pi / 5)
S36, S72 = math.sin(math.pi / 5), math.sin(2 * math.pi / 5)


def ten_point(s):
    e = [s[n] + s[n + 5] for n in range(5)]
    d = [s[n] - s[n + 5] for n in range(5)]
    e14, e23, f14, f23 = e[1] + e[4], e[2] + e[3], e[1] - e[4], e[2] - e[3]
    d14, d23, g14, g23 = d[1] + d[4], d[2] + d[3], d[1] - d[4], d[2] - d[3]
    y0 = e[0] + e14 + e23
    y2 = (e[0] + C72 * e14 - C36 * e23, -(S72 * f14 + S36 * f23))
    y4 = (e[0] - C36 * e14 + C72 * e23, -(S36 * f14 - S72 * f23))
    y1 = (d[0] + C36 * g14 + C72 * g23, -(S36 * d14 + S72 * d23))
    y3 = (d[0] - C72 * g14 - C36 * g23, -(S72 * d14 - S36 * d23))
    y5 = d[0] - g14 + g23
    return y0, y1, y2, y3, y4, y5


def hi_lo(y):
    hi = y.astype(jnp.bfloat16)
    return [hi, (y - hi.astype(jnp.float32)).astype(jnp.bfloat16)]


def whiten_kernel(x_ref, mask_ref, table_hbm, near_hbm, inv_ref, out_ref, table, near, sem):
    rows = x_ref.shape[0]
    parts = ((0, 512), (512, 512), (1024, 256))
    copies = [
        pltpu.make_async_copy(table_hbm.at[:, pl.ds(a, w)], table.at[:, pl.ds(a, w)], sem.at[i])
        for i, (a, w) in enumerate(parts)
    ] + [pltpu.make_async_copy(near_hbm, near, sem.at[3])]
    for c in copies:
        c.start()
    s = [x_ref[:, FOLD * n : FOLD * (n + 1)].astype(jnp.float32) for n in range(10)]
    y0, y1, y2, y3, y4, y5 = ten_point(s)
    lane = lax.broadcasted_iota(jnp.int32, (rows, 128), 1)
    lower = lane < 64
    real = [None] * 5
    imag = [None] * 5

    def product(ys, part):
        copies[part].wait()
        at, width = parts[part]
        left = jnp.concatenate([piece for y in ys for piece in hi_lo(y)], axis=0)
        full = jnp.dot(left, table[:, at : at + width], preferred_element_type=jnp.float32)
        return [
            full[2 * rows * i : 2 * rows * i + rows] + full[2 * rows * i + rows : 2 * rows * (i + 1)]
            for i in range(len(ys))
        ]

    for part, (ya, yb), groups in ((0, (y1, y4), (1, 4)), (1, (y2, y3), (2, 3))):
        pa, qa, pb, qb = product([ya[0], ya[1], yb[0], yb[1]], part)
        first, second = groups
        for group, at, (p0, q0, p1, q1) in ((first, 0, (pa, qa, pb, qb)), (second, 256, (pb, qb, pa, qa))):
            c, n = slice(at, at + 128), slice(at + 128, at + 256)
            real[group] = jnp.where(lower, p0[:, c] - q0[:, n], p1[:, c] + q1[:, n])
            imag[group] = jnp.where(lower, p0[:, n] + q0[:, c], p1[:, n] - q1[:, c])
    p0, p5 = product([y0, y5], 2)
    real[0] = jnp.where(lower, p0[:, :128], p5[:, :128])
    imag[0] = jnp.where(lower, p0[:, 128:], p5[:, 128:])
    re = jnp.concatenate(real, axis=1)
    im = jnp.concatenate(imag, axis=1)
    power = re * re + im * im
    hi, mid = hi_lo(power)
    low = (power - hi.astype(jnp.float32) - mid.astype(jnp.float32)).astype(jnp.bfloat16)
    copies[3].wait()
    sums = jnp.dot(jnp.concatenate([hi, mid, low], axis=0), near[...], preferred_element_type=jnp.float32)
    smooth = (sums[:rows] + sums[rows : 2 * rows] + sums[2 * rows :]) * inv_ref[...]
    chans = mask_ref.shape[1]
    mask = mask_ref[...].astype(jnp.float32)
    spread = jnp.concatenate(
        [jnp.broadcast_to(mask[i : i + 1], (chans, chans)) for i in range(mask_ref.shape[0])], axis=0
    )
    own = lax.broadcasted_iota(jnp.int32, (rows, chans), 0) % chans
    at = lax.broadcasted_iota(jnp.int32, (rows, chans), 1)
    flags = jnp.sum(jnp.where(own == at, spread, 0.0), axis=1, keepdims=True)
    factor = flags * lax.rsqrt(smooth + EPS)
    last = lax.broadcasted_iota(jnp.int32, (rows, LANES), 1) == LANES - 1
    out_ref[:, :LANES] = (re * factor).astype(jnp.bfloat16)
    out_ref[:, LANES:] = jnp.where(last, flags, im * factor).astype(jnp.bfloat16)


def whiten(traces, valid_mask):
    chans, minutes, samples = traces.shape
    rows = chans * minutes
    x = jnp.swapaxes(traces, 0, 1).reshape(rows, samples)
    near, inverse = near_table()
    vmem = pl.BlockSpec(memory_space=pltpu.VMEM)
    hbm = pl.BlockSpec(memory_space=pl.ANY)
    return pl.pallas_call(
        whiten_kernel,
        out_shape=jax.ShapeDtypeStruct((rows, 2 * LANES), jnp.bfloat16),
        in_specs=[vmem, vmem, hbm, hbm, vmem],
        out_specs=vmem,
        scratch_shapes=[
            pltpu.VMEM((FOLD, 5 * 256), jnp.bfloat16),
            pltpu.VMEM((LANES, LANES), jnp.bfloat16),
            pltpu.SemaphoreType.DMA((4,)),
        ],
        name="whiten",
    )(x, valid_mask.T, jnp.asarray(fold_table()), jnp.asarray(near), jnp.asarray(inverse))


def corr_kernel(slots_ref, own_ref, panels_ref, lag_ref, stack_ref, out_ref, cross):
    step = pl.program_id(0)
    count, chans = stack_ref.shape[0], stack_ref.shape[1]
    own = own_ref[...].astype(jnp.float32)
    minutes = own.shape[0] // chans
    for j in range(count):
        at = slots_ref[0, step * count + j]
        part = panels_ref[at].astype(jnp.float32)
        for a in range(0, chans, 2):
            both_re, both_im = [], []
            for channel in (a, a + 1):
                re = im = None
                for m in range(minutes):
                    row = m * chans + channel
                    o_re, o_im = own[row : row + 1, :LANES], own[row : row + 1, LANES:]
                    p_re = part[m * chans : (m + 1) * chans, :LANES]
                    p_im = part[m * chans : (m + 1) * chans, LANES:]
                    r = o_re * p_re + o_im * p_im
                    i = o_im * p_re - o_re * p_im
                    re = r if re is None else re + r
                    im = i if im is None else im + i
                both_re.append(re)
                both_im.append(im)
            rows = slice((j * chans + a) * chans, (j * chans + a + 2) * chans)
            cross[rows, :LANES] = jnp.concatenate(both_re, axis=0).astype(jnp.bfloat16)
            cross[rows, LANES:] = jnp.concatenate(both_im, axis=0).astype(jnp.bfloat16)
    full = jnp.dot(cross[...], lag_ref[...], preferred_element_type=jnp.float32)
    scale = (1.0 / math.sqrt(BINS)) / jnp.maximum(full[:, COLS - 1 :], 1.0)
    corr = (full * scale)[:, :LAGS].reshape(stack_ref.shape)
    out_ref[...] = stack_ref[...] + corr


def correlate(slots, own, panels, stack):
    offsets, chans = stack.shape[0], stack.shape[1]
    chunk = max(d for d in range(1, 7) if offsets % d == 0)
    rows, lanes = own.shape
    block = pl.BlockSpec((chunk, chans, chans, LAGS), lambda i, s: (i, 0, 0, 0))
    whole = pl.BlockSpec(memory_space=pltpu.VMEM)
    return pl.pallas_call(
        corr_kernel,
        out_shape=jax.ShapeDtypeStruct(stack.shape, jnp.float32),
        grid_spec=pltpu.PrefetchScalarGridSpec(
            num_scalar_prefetch=1,
            grid=(offsets // chunk,),
            in_specs=[whole, whole, whole, block],
            out_specs=block,
            scratch_shapes=[pltpu.VMEM((chunk * chans * chans, lanes), jnp.bfloat16)],
        ),
        name="correlate",
    )(slots, own, panels, jnp.asarray(lag_table()), stack)


def shards(traces, valid_mask, pair_table, stack_in):
    own = whiten(traces, valid_mask)
    panels = lax.all_gather(own, "row", axis=0)
    return correlate(pair_table, own, panels, stack_in[0])[None]


def solution(mesh):
    in_specs = (
        P(("parts", "row"), None, None),
        P(("parts", "row"), None),
        P(("parts", "row"), None),
        P(("parts", "row"), None, None, None, None),
    )
    out_specs = P(("parts", "row"), None, None, None, None)
    return jax.shard_map(shards, mesh=mesh, in_specs=in_specs, out_specs=out_specs, check_vma=False)
```

time: 215 us -> 37.9 us (0.18)
  other arithmetic: 143 us -> 0 us
  blocking collectives: 42.3 us -> 26.6 us
  matrix products: 11.3 us -> 0 us
  local copies, waits for them, and re-layouts: 12.1 us -> 1.77 us
  Pallas kernels: 0 us -> 9.37 us
  loops' own time: 5.26 us -> 0 us
    another operation x9 -> x0, other arithmetic: 138 us -> none
    all_gather x2 -> x1, blocking collectives: 42.3 us -> 26.6 us  [shards(): panels = lax.all_gather(own, 'row', axis=0)]
    dot_general x10 -> x0, matrix products: 11.3 us -> none  [the longest x8 8.12 us: absorb(): jnp.dot(segment, table, preferred_element_type=jnp.float32)]
    pallas_call x0 -> x2, Pallas kernels: none -> 9.37 us  [the longest x1 4.97 us: correlate(): pl.pallas_call(corr_kernel, out_shape=jax.ShapeDtypeStruct(stack.shape, j...]
    another operation x1 -> x0, loops' own time: 5.26 us -> none  [spectra_of(): lax.scan(absorb, start_total, jnp.arange(8, dtype=jnp.int32))]
    dynamic_slice x8 -> x0, local copies, waits for them, and re-layouts: 5.19 us -> none  [spectra_of(): lax.scan(absorb, start_total, jnp.arange(8, dtype=jnp.int32))]
    add x19 -> x0, other arithmetic: 2.27 us -> none  [the longest x1 1.44 us: shards(): base_stack + tile_corr(whitened, own_flags, partner, partner_flags, lag_t...]
where the time goes in v1:
time: 37.9 us; the launch traced here: 37.7 us
  blocking collectives  26.6 us (70%)
  Pallas kernels  9.37 us (25%)
  local copies, waits for them, and re-layouts  1.77 us (5%)
    all_gather x1, blocking collectives, shards(): panels = lax.all_gather(own, 'row', axis=0)  26.6 us
    pallas_call x1, Pallas kernels, correlate(): pl.pallas_call(corr_kernel, out_shape=jax.ShapeDtypeStruct(stack.shape, j...  4.97 us
    pallas_call x1, Pallas kernels, whiten(): pl.pallas_call(whiten_kernel, out_shape=jax.ShapeDtypeStruct((rows, 2 * L...  4.41 us
    transpose x1, local copies, waits for them, and re-layouts, whiten(): x = jnp.swapaxes(traces, 0, 1).reshape(rows, samples)  1.77 us

profile of v1, /device:TPU:0, one launch (start us, length us, event | category | flops | bytes accessed | tf_op | source)
XLA Modules:
  0.0 37.7 jit_solution(3994357399921066620)
XLA Ops:
  0.0 1.8 %copy.11 = bf16[2,8,12000]{2,1,0:T(8,128)(2,1)} copy(bf16[2,8,12000]{2,0,1:T(2,128)(2,1)} %bitcast.11) | data formatting | bytes 768000 | tf_op jit(solution)/shard_map/transpose | solution.py:154
  1.8 4.4 %whiten.1.own_ref = bf16[16,1280]{1,0:T(8,128)(2,1)} custom-call(bf16[16,12000]{1,0:T(8,128)(2,1)} %bitcast.9, s32[2,8]{1,0:T(2,128)} %bitcast.12, bf16[1200,1280]{1,0:T(8,128)(2,1)} %constant.8.clone.table_hbm, bf16[640,640]{1,0:T(8,128)(2,1)} %constant.9.clone.near_hbm, f32[1,640]{1,0:T(1,128)} %constant.10.clone.inv_ref), custom_call_target="tpu_custom_call" | custom-call | tf_op jit(solution)/shard_map/whiten/pallas_call | solution.py:158
  6.2 26.6 %all-gather = bf16[256,1280]{1,0:T(8,128)(2,1)} all-gather(bf16[16,1280]{1,0:T(8,128)(2,1)} %whiten.1.own_ref), channel_id=2, replica_groups=mesh['parts'=2,'row'=16] {'row'}, dimensions={0}, use_global_device_ids=true | all-gather | bytes 696320 | tf_op jit(solution)/shard_map/all_gather | solution.py:226
  32.8 5.0 %correlate.1 = f32[10,8,8,401]{3,2,1,0:T(8,128)} custom-call(s32[1,10]{1,0:T(1,128)} %slots_ref.1, bf16[16,1280]{1,0:T(8,128)(2,1)} %whiten.1.own_ref, bf16[16,16,1280]{2,1,0:T(8,128)(2,1)} %bitcast.8, bf16[1280,512]{1,0:T(8,128)(2,1)} %constant.11.clone.lag_ref, f32[10,8,8,401]{3,2,1,0:T(8,128)} %bitcast.10), custom_call_target="tpu_custom_call" | custom-call | tf_op jit(solution)/shard_map/correlate/pallas_call | solution.py:210

commit v2 on v1

--- a/solution.py
+++ b/solution.py
@@ -1,3 +1,4 @@
+import functools
 import math
 
 import jax
@@ -169,13 +170,13 @@
     )(x, valid_mask.T, jnp.asarray(fold_table()), jnp.asarray(near), jnp.asarray(inverse))
 
 
-def corr_kernel(slots_ref, own_ref, panels_ref, lag_ref, stack_ref, out_ref, cross):
+def corr_kernel(pick, slots_ref, own_ref, panels_ref, lag_ref, stack_ref, out_ref, cross):
     step = pl.program_id(0)
     count, chans = stack_ref.shape[0], stack_ref.shape[1]
     own = own_ref[...].astype(jnp.float32)
     minutes = own.shape[0] // chans
     for j in range(count):
-        at = slots_ref[0, step * count + j]
+        at = pick(slots_ref[0, step * count + j])
         part = panels_ref[at].astype(jnp.float32)
         for a in range(0, chans, 2):
             both_re, both_im = [], []
@@ -201,14 +202,14 @@
     out_ref[...] = stack_ref[...] + corr
 
 
-def correlate(slots, own, panels, stack):
+def correlate(pick, slots, own, panels, stack):
     offsets, chans = stack.shape[0], stack.shape[1]
     chunk = max(d for d in range(1, 7) if offsets % d == 0)
     rows, lanes = own.shape
     block = pl.BlockSpec((chunk, chans, chans, LAGS), lambda i, s: (i, 0, 0, 0))
     whole = pl.BlockSpec(memory_space=pltpu.VMEM)
     return pl.pallas_call(
-        corr_kernel,
+        functools.partial(corr_kernel, pick),
         out_shape=jax.ShapeDtypeStruct(stack.shape, jnp.float32),
         grid_spec=pltpu.PrefetchScalarGridSpec(
             num_scalar_prefetch=1,
@@ -221,10 +222,34 @@
     )(slots, own, panels, jnp.asarray(lag_table()), stack)
 
 
+def share(own, panel_count, offsets):
+    chips = panel_count // 2
+    hops = (offsets + 1) // 2
+    if panel_count % 2 or hops > 8 or hops + 2 > chips:
+        return lax.all_gather(own, "row", axis=0), lambda j: j
+
+    def fetch(far):
+        shift = 2 * far
+        return lax.ppermute(own, "row", [((i + shift) % panel_count, i) for i in range(panel_count)])
+
+    mine = jnp.stack([own] + [fetch(far) for far in range(1, hops)] + [fetch(-1)])
+    both = [[2 * c, 2 * c + 1] for c in range(chips)]
+    panels = lax.all_gather(mine, "row", axis=0, tiled=True, axis_index_groups=both)
+
+    def pick(j):
+        base = (lax.axis_index("row") // 2) * 2
+        ahead = lax.rem(j - base + panel_count, panel_count)
+        far = ahead // 2
+        place = jnp.where(far == chips - 1, hops, far)
+        return lax.rem(ahead, 2) * (hops + 1) + place
+
+    return panels, pick
+
+
 def shards(traces, valid_mask, pair_table, stack_in):
     own = whiten(traces, valid_mask)
-    panels = lax.all_gather(own, "row", axis=0)
-    return correlate(pair_table, own, panels, stack_in[0])[None]
+    panels, pick = share(own, lax.axis_size("row"), pair_table.shape[1])
+    return correlate(pick, pair_table, own, panels, stack_in[0])[None]
 
 
 def solution(mesh):

time: 37.9 us -> 27 us (0.71)
  blocking collectives: 26.6 us -> 2.29 us
  starting transfers between devices: 0 us -> 11 us
  waiting for transfers between devices: 0 us -> 1.46 us
  local copies, waits for them, and re-layouts: 1.77 us -> 2.61 us
    all_gather x1, blocking collectives: 26.6 us -> 2.29 us  [share(): lax.all_gather(mine, 'row', axis=0, tiled=True, axis_index_groups=both)]
    ppermute x0 -> x5, starting transfers between devices: none -> 11 us  [fetch(): lax.ppermute(own, 'row', [((i + shift) % panel_count, i) for i in range(p...]
    ppermute x0 -> x5, waiting for transfers between devices: none -> 1.46 us  [fetch(): lax.ppermute(own, 'row', [((i + shift) % panel_count, i) for i in range(p...]
    unnamed x0 -> x5, local copies, waits for them, and re-layouts: none -> 0.83 us
  transfers between devices with their start and end apart: 0 -> 5, of which waited for: 0 -> 1; matrix products, arithmetic and copies ran while one was open for 0% -> 3% of each run, Pallas kernels for 0% -> 0%
where the time goes in v2:
time: 27 us; the launch traced here: 26.7 us
  starting transfers between devices  11 us (41%)
  Pallas kernels  9.33 us (35%)
  local copies, waits for them, and re-layouts  2.61 us (10%)
  blocking collectives  2.29 us (8%)
  waiting for transfers between devices  1.46 us (5%)
    ppermute x5, starting transfers between devices, fetch(): lax.ppermute(own, 'row', [((i + shift) % panel_count, i) for i in range(p...  11 us
    pallas_call x1, Pallas kernels, correlate(): pl.pallas_call(functools.partial(corr_kernel, pick), out_shape=jax.ShapeD...  4.92 us
    pallas_call x1, Pallas kernels, whiten(): pl.pallas_call(whiten_kernel, out_shape=jax.ShapeDtypeStruct((rows, 2 * L...  4.41 us
    all_gather x1, blocking collectives, share(): lax.all_gather(mine, 'row', axis=0, tiled=True, axis_index_groups=both)  2.29 us
    transpose x1, local copies, waits for them, and re-layouts, whiten(): x = jnp.swapaxes(traces, 0, 1).reshape(rows, samples)  1.77 us
    ppermute x5, waiting for transfers between devices, fetch(): lax.ppermute(own, 'row', [((i + shift) % panel_count, i) for i in range(p...  1.46 us
    unnamed x5, local copies, waits for them, and re-layouts  0.83 us
  transfers between devices with their start and end apart: 5, of which 1 were waited for; matrix products, arithmetic and copies ran while one was open for 3% of the time, Pallas kernels for 0%

profile of v2, /device:TPU:0, one launch (start us, length us, event | category | flops | bytes accessed | tf_op | source)
XLA Modules:
  0.0 26.7 jit_solution(5480066540363556491)
XLA Ops:
  0.0 1.8 %copy.12 = bf16[2,8,12000]{2,1,0:T(8,128)(2,1)} copy(bf16[2,8,12000]{2,0,1:T(2,128)(2,1)} %bitcast.21) | data formatting | bytes 768000 | tf_op jit(solution)/shard_map/transpose | solution.py:155
  1.8 4.4 %whiten.1.own_ref = bf16[16,1280]{1,0:T(8,128)(2,1)} custom-call(bf16[16,12000]{1,0:T(8,128)(2,1)} %bitcast.19, s32[2,8]{1,0:T(2,128)} %bitcast.22, bf16[1200,1280]{1,0:T(8,128)(2,1)} %constant.8.clone.table_hbm, bf16[640,640]{1,0:T(8,128)(2,1)} %constant.9.clone.near_hbm, f32[1,640]{1,0:T(1,128)} %constant.10.clone.inv_ref), custom_call_target="tpu_custom_call" | custom-call | tf_op jit(solution)/shard_map/whiten/pallas_call | solution.py:159
  6.2 3.0 %collective-permute-start.4 = (bf16[16,1280]{1,0:T(8,128)(2,1)}, bf16[16,1280]{1,0:T(8,128)(2,1)S(1)}, u32[]{:S(2)}, u32[]{:S(2)}) collective-permute-start(bf16[16,1280]{1,0:T(8,128)(2,1)} %whiten.1.own_ref), channel_id=1, source_target_pairs={{14,0},{15,1},{0,2},{1,3},{2,4},{3,5},{4,6},{5,7},{6,8},{7,9},{8,1... | collective-permute-start | bytes 122888 | tf_op jit(solution)/shard_map/ppermute | solution.py:233
  9.2 2.6 %collective-permute-start.3 = (bf16[16,1280]{1,0:T(8,128)(2,1)}, bf16[16,1280]{1,0:T(8,128)(2,1)S(1)}, u32[]{:S(2)}, u32[]{:S(2)}) collective-permute-start(bf16[16,1280]{1,0:T(8,128)(2,1)} %whiten.1.own_ref), channel_id=1, source_target_pairs={{8,0},{9,1},{10,2},{11,3},{12,4},{13,5},{14,6},{15,7},{0,8},{1,9},... | collective-permute-start | bytes 122888 | tf_op jit(solution)/shard_map/ppermute | solution.py:233
  11.8 1.3 %collective-permute-start.2 = (bf16[16,1280]{1,0:T(8,128)(2,1)}, bf16[16,1280]{1,0:T(8,128)(2,1)S(1)}, u32[]{:S(2)}, u32[]{:S(2)}) collective-permute-start(bf16[16,1280]{1,0:T(8,128)(2,1)} %whiten.1.own_ref), channel_id=1, source_target_pairs={{6,0},{7,1},{8,2},{9,3},{10,4},{11,5},{12,6},{13,7},{14,8},{15,9},... | collective-permute-start | bytes 122888 | tf_op jit(solution)/shard_map/ppermute | solution.py:233
  13.1 2.1 %collective-permute-start.1 = (bf16[16,1280]{1,0:T(8,128)(2,1)}, bf16[16,1280]{1,0:T(8,128)(2,1)S(1)}, u32[]{:S(2)}, u32[]{:S(2)}) collective-permute-start(bf16[16,1280]{1,0:T(8,128)(2,1)} %whiten.1.own_ref), channel_id=1, source_target_pairs={{4,0},{5,1},{6,2},{7,3},{8,4},{9,5},{10,6},{11,7},{12,8},{13,9},{1... | collective-permute-start | bytes 122888 | tf_op jit(solution)/shard_map/ppermute | solution.py:233
  15.2 1.9 %collective-permute-start = (bf16[16,1280]{1,0:T(8,128)(2,1)}, bf16[16,1280]{1,0:T(8,128)(2,1)S(1)}, u32[]{:S(2)}, u32[]{:S(2)}) collective-permute-start(bf16[16,1280]{1,0:T(8,128)(2,1)} %whiten.1.own_ref), channel_id=1, source_target_pairs={{2,0},{3,1},{4,2},{5,3},{6,4},{7,5},{8,6},{9,7},{10,8},{11,9},{12,... | collective-permute-start | bytes 122888 | tf_op jit(solution)/shard_map/ppermute | solution.py:233
  17.2 0.8 %bitcast_dynamic-update-slice_fusion.5 = bf16[6,16,1280]{2,1,0:T(8,128)(2,1)S(1)} fusion(bf16[16,1280]{1,0:T(8,128)(2,1)} %whiten.1.own_ref), kind=kLoop, calls=%fused_computation.6 | loop fusion | bytes 81920
  18.0 1.4 %collective-permute-done = bf16[16,1280]{1,0:T(8,128)(2,1)S(1)} collective-permute-done((bf16[16,1280]{1,0:T(8,128)(2,1)}, bf16[16,1280]{1,0:T(8,128)(2,1)S(1)}, u32[]{:S(2)}, u32[]{:S(2)}) %collective-permute-start) | collective-permute-done | bytes 40992 | tf_op jit(solution)/shard_map/ppermute | solution.py:233
  19.4 0.0 collective-permute-done.1
  19.5 0.0 collective-permute-done.2
  19.5 0.0 collective-permute-done.3
  19.5 0.0 collective-permute-done.4
  19.5 2.3 %all_gather.3.panels_ref = bf16[12,16,1280]{2,1,0:T(8,128)(2,1)} all-gather(bf16[6,16,1280]{2,1,0:T(8,128)(2,1)S(1)} %bitcast_dynamic-update-slice_fusion), channel_id=1, replica_groups={{0,1},{2,3},{4,5},{6,7},{8,9},{10,11},{12,13},{14,15},{16,17},{18,19},{..., dimensions={0}, use_global_device_ids=true | all-gather | bytes 737280 | tf_op jit(solution)/shard_map/all_gather | solution.py:237
  21.8 4.9 %correlate.1 = f32[10,8,8,401]{3,2,1,0:T(8,128)} custom-call(s32[1,10]{1,0:T(1,128)} %slots_ref.1, bf16[16,1280]{1,0:T(8,128)(2,1)} %whiten.1.own_ref, bf16[12,16,1280]{2,1,0:T(8,128)(2,1)} %all_gather.3.panels_ref, bf16[1280,512]{1,0:T(8,128)(2,1)} %constant.11.clone.lag_ref, f32[10,8,8,401]{3,2,1,0:T(8,128)} %bitcast.20), custom_call_target="tpu_custom_call" | custom-call | tf_op jit(solution)/shard_map/correlate/pallas_call | solution.py:211
  (5 shorter events, 0.0 us)
Async XLA Ops:
  6.2 13.3 %collective-permute-start.4 = (bf16[16,1280]{1,0:T(8,128)(2,1)}, bf16[16,1280]{1,0:T(8,128)(2,1)S(1)}, u32[]{:S(2)}, u32[]{:S(2)}) collective-permute-start(bf16[16,1280]{1,0:T(8,128)(2,1)} %whiten.1.own_ref), channel_id=1, source_target_pairs={{14,0},{15,1},{0,2},{1,3},{2,4},{3,5},{4,6},{5,7},{6,8},{7,9},{8,1... | collective-permute-start | bytes 122888 | tf_op jit(solution)/shard_map/ppermute | solution.py:233
  9.2 10.3 %collective-permute-start.3 = (bf16[16,1280]{1,0:T(8,128)(2,1)}, bf16[16,1280]{1,0:T(8,128)(2,1)S(1)}, u32[]{:S(2)}, u32[]{:S(2)}) collective-permute-start(bf16[16,1280]{1,0:T(8,128)(2,1)} %whiten.1.own_ref), channel_id=1, source_target_pairs={{8,0},{9,1},{10,2},{11,3},{12,4},{13,5},{14,6},{15,7},{0,8},{1,9},... | collective-permute-start | bytes 122888 | tf_op jit(solution)/shard_map/ppermute | solution.py:233
  11.8 7.7 %collective-permute-start.2 = (bf16[16,1280]{1,0:T(8,128)(2,1)}, bf16[16,1280]{1,0:T(8,128)(2,1)S(1)}, u32[]{:S(2)}, u32[]{:S(2)}) collective-permute-start(bf16[16,1280]{1,0:T(8,128)(2,1)} %whiten.1.own_ref), channel_id=1, source_target_pairs={{6,0},{7,1},{8,2},{9,3},{10,4},{11,5},{12,6},{13,7},{14,8},{15,9},... | collective-permute-start | bytes 122888 | tf_op jit(solution)/shard_map/ppermute | solution.py:233
  13.1 6.4 %collective-permute-start.1 = (bf16[16,1280]{1,0:T(8,128)(2,1)}, bf16[16,1280]{1,0:T(8,128)(2,1)S(1)}, u32[]{:S(2)}, u32[]{:S(2)}) collective-permute-start(bf16[16,1280]{1,0:T(8,128)(2,1)} %whiten.1.own_ref), channel_id=1, source_target_pairs={{4,0},{5,1},{6,2},{7,3},{8,4},{9,5},{10,6},{11,7},{12,8},{13,9},{1... | collective-permute-start | bytes 122888 | tf_op jit(solution)/shard_map/ppermute | solution.py:233
  15.2 4.2 %collective-permute-start = (bf16[16,1280]{1,0:T(8,128)(2,1)}, bf16[16,1280]{1,0:T(8,128)(2,1)S(1)}, u32[]{:S(2)}, u32[]{:S(2)}) collective-permute-start(bf16[16,1280]{1,0:T(8,128)(2,1)} %whiten.1.own_ref), channel_id=1, source_target_pairs={{2,0},{3,1},{4,2},{5,3},{6,4},{7,5},{8,6},{9,7},{10,8},{11,9},{12,... | collective-permute-start | bytes 122888 | tf_op jit(solution)/shard_map/ppermute | solution.py:233

commit v3 on v2

v3 whole, which is shorter than its diff:
```python
import functools
import math

import jax
import jax.numpy as jnp
import ml_dtypes
import numpy as np
from jax import lax
from jax.experimental import pallas as pl
from jax.experimental.pallas import tpu as pltpu
from jax.sharding import PartitionSpec as P

SAMPLES = 12000
FLO = 6
BINS = 595
HALF = 40
LAGS = 401
EPS = 1e-06
WHITEN_VMEM = 60 << 20
CORR_VMEM = 24 << 20

SPLIT = 20
FOLD = SAMPLES // SPLIT
LANES = 640
RUN = 32
COLS = 512


def bin_at(lane):
    residue = lane // 128 + 5 * (lane % 128 // RUN)
    return residue + SPLIT * (residue < FLO) + SPLIT * (lane % RUN)


BIN_OF = bin_at(np.arange(LANES))
USED = BIN_OF < FLO + BINS
GROUPS = ((1, 4), (2, 3), (0,))


def bf16(a):
    return np.asarray(a, np.float32).astype(ml_dtypes.bfloat16)


def fold_table():
    q = (np.arange(FOLD)[:, None] * BIN_OF[None, :]) % SAMPLES
    angle = 2.0 * np.pi * q / SAMPLES
    cos = np.where(USED, np.cos(angle), 0.0).reshape(FOLD, 5, 1, 128)
    sin = np.where(USED, -np.sin(angle), 0.0).reshape(FOLD, 5, 1, 128)
    table = np.concatenate([cos, sin], axis=2)
    order = [group for some in GROUPS for group in some]
    return bf16(table[:, order].reshape(FOLD, 5 * 256))


def lag_table():
    tau = np.arange(LAGS) - (LAGS - 1) // 2
    q = (BIN_OF[:, None] * tau[None, :]) % SAMPLES
    angle = 2.0 * np.pi * q / SAMPLES
    table = np.zeros((2 * LANES, COLS), np.float64)
    table[:LANES, :LAGS] = np.where(USED[:, None], np.cos(angle), 0.0)
    table[LANES:, :LAGS] = np.where(USED[:, None], -np.sin(angle), 0.0)
    table[LANES - 1, COLS - 1] = 1.0
    return bf16(table)


def cosine(n, of):
    return math.cos(2.0 * math.pi * n / of)


def sine(n, of):
    return math.sin(2.0 * math.pi * n / of)


def ten_point(s):
    e = [s[n] + s[n + 5] for n in range(5)]
    d = [s[n] - s[n + 5] for n in range(5)]
    c1, c2, s1, s2 = cosine(1, 10), cosine(2, 10), sine(1, 10), sine(2, 10)
    e14, e23, f14, f23 = e[1] + e[4], e[2] + e[3], e[1] - e[4], e[2] - e[3]
    d14, d23, g14, g23 = d[1] + d[4], d[2] + d[3], d[1] - d[4], d[2] - d[3]
    y0 = (e[0] + e14 + e23, None)
    y2 = (e[0] + c2 * e14 - c1 * e23, -(s2 * f14 + s1 * f23))
    y4 = (e[0] - c1 * e14 + c2 * e23, -(s1 * f14 - s2 * f23))
    y1 = (d[0] + c1 * g14 + c2 * g23, -(s1 * d14 + s2 * d23))
    y3 = (d[0] - c2 * g14 - c1 * g23, -(s2 * d14 - s1 * d23))
    y5 = (d[0] - g14 + g23, None)
    return [y0, y1, y2, y3, y4, y5]


def twenty_point(s):
    y = [None] * 11
    y[0::2] = ten_point([s[n] + s[n + 10] for n in range(10)])
    d = [s[n] - s[n + 10] for n in range(10)]
    g = [d[n] - d[10 - n] for n in range(1, 5)]
    h = [d[n] + d[10 - n] for n in range(1, 5)]
    for k in (1, 3, 5, 7, 9):
        real, imag = d[0], -sine(5 * k, 20) * d[5]
        for n in range(1, 5):
            real = real + cosine(n * k % 20, 20) * g[n - 1]
            imag = imag - sine(n * k % 20, 20) * h[n - 1]
        y[k] = (real, imag)
    return y


def hi_lo(y):
    hi = y.astype(jnp.bfloat16)
    return [hi, (y - hi.astype(jnp.float32)).astype(jnp.bfloat16)]


def whiten_kernel(x_hbm, mask_hbm, table_hbm, out_ref, x_buf, mask_buf, table, near, sem):
    chans, minutes, samples = x_buf.shape
    rows = chans * minutes
    starts = (0, 512, 1024, 1280)
    fetch_x = pltpu.make_async_copy(x_hbm, x_buf, sem.at[0])
    fetch_mask = pltpu.make_async_copy(mask_hbm, mask_buf, sem.at[1])
    fetch_table = [
        pltpu.make_async_copy(table_hbm.at[:, pl.ds(a, b - a)], table.at[:, pl.ds(a, b - a)], sem.at[2 + i])
        for i, (a, b) in enumerate(zip(starts, starts[1:]))
    ]
    for copy in [fetch_x, fetch_mask] + fetch_table:
        copy.start()

    down = bin_at(lax.broadcasted_iota(jnp.int32, (LANES, 128), 0))
    down = jnp.where(down < FLO + BINS, down, -SAMPLES)
    lanes = bin_at(lax.broadcasted_iota(jnp.int32, (8, LANES), 1))
    for group in range(5):
        across = jnp.broadcast_to(lanes[:1, group * 128 : (group + 1) * 128], (LANES, 128))
        close = (jnp.abs(down - across) <= HALF) & (across < FLO + BINS)
        near[:, group * 128 : (group + 1) * 128] = jnp.where(close, 1.0, 0.0).astype(jnp.bfloat16)
    bins = lanes[:1]
    count = jnp.minimum(bins + HALF, FLO + BINS - 1) - jnp.maximum(bins - HALF, FLO) + 1
    inverse = 1.0 / jnp.maximum(count, 1).astype(jnp.float32)

    fetch_x.wait()
    x = jnp.swapaxes(x_buf[...], 0, 1).reshape(rows, samples)
    y = twenty_point([x[:, FOLD * n : FOLD * (n + 1)].astype(jnp.float32) for n in range(SPLIT)])
    run = lax.broadcasted_iota(jnp.int32, (rows, 128), 1) // RUN
    for copy in [fetch_mask] + fetch_table:
        copy.wait()
    real = [None] * 5
    imag = [None] * 5
    for part, groups in enumerate(GROUPS):
        wanted = sorted({min(k, SPLIT - k) for g in groups for k in range(g, SPLIT, 5)})
        pieces = [(k, i) for k in wanted for i in range(2) if y[k][i] is not None]
        left = jnp.concatenate([p for k, i in pieces for p in hi_lo(y[k][i])], axis=0)
        at = starts[part]
        full = jnp.dot(left, table[:, at : starts[part + 1]], preferred_element_type=jnp.float32)
        got = {
            p: full[2 * rows * i : 2 * rows * i + rows] + full[2 * rows * i + rows : 2 * rows * (i + 1)]
            for i, p in enumerate(pieces)
        }
        for place, group in enumerate(groups):
            cos = slice(place * 256, place * 256 + 128)
            sin = slice(place * 256 + 128, place * 256 + 256)
            re = im = None
            for q in range(4):
                k = group + 5 * q
                same = min(k, SPLIT - k)
                a = got[(same, 0)]
                r, i = a[:, cos], a[:, sin]
                if (same, 1) in got:
                    b = got[(same, 1)] if k == same else -got[(same, 1)]
                    r, i = r - b[:, sin], i + b[:, cos]
                re = r if re is None else jnp.where(run == q, r, re)
                im = i if im is None else jnp.where(run == q, i, im)
            real[group], imag[group] = re, im
    re = jnp.concatenate(real, axis=1)
    im = jnp.concatenate(imag, axis=1)
    power = re * re + im * im
    hi, mid = hi_lo(power)
    low = (power - hi.astype(jnp.float32) - mid.astype(jnp.float32)).astype(jnp.bfloat16)
    sums = jnp.dot(jnp.concatenate([hi, mid, low], axis=0), near[...], preferred_element_type=jnp.float32)
    smooth = (sums[:rows] + sums[rows : 2 * rows] + sums[2 * rows :]) * inverse
    mask = mask_buf[...].astype(jnp.float32)
    spread = jnp.concatenate([jnp.broadcast_to(mask[m : m + 1], (chans, chans)) for m in range(minutes)], axis=0)
    own = lax.broadcasted_iota(jnp.int32, (rows, chans), 0) % chans
    other = lax.broadcasted_iota(jnp.int32, (rows, chans), 1)
    flags = jnp.sum(jnp.where(own == other, spread, 0.0), axis=1, keepdims=True)
    factor = flags * lax.rsqrt(smooth + EPS)
    last = lax.broadcasted_iota(jnp.int32, (rows, LANES), 1) == LANES - 1
    out_ref[:, :LANES] = (re * factor).astype(jnp.bfloat16)
    out_ref[:, LANES:] = jnp.where(last, flags, im * factor).astype(jnp.bfloat16)


def whiten(traces, valid_mask):
    chans, minutes, samples = traces.shape
    rows = chans * minutes
    anywhere = pl.BlockSpec(memory_space=pltpu.HBM)
    return pl.pallas_call(
        whiten_kernel,
        out_shape=jax.ShapeDtypeStruct((rows, 2 * LANES), jnp.bfloat16),
        in_specs=[anywhere] * 3,
        out_specs=pl.BlockSpec(memory_space=pltpu.VMEM),
        scratch_shapes=[
            pltpu.VMEM((chans, minutes, samples), jnp.bfloat16),
            pltpu.VMEM((minutes, chans), jnp.int32),
            pltpu.VMEM((FOLD, 5 * 256), jnp.bfloat16),
            pltpu.VMEM((LANES, LANES), jnp.bfloat16),
            pltpu.SemaphoreType.DMA((5,)),
        ],
        compiler_params=pltpu.CompilerParams(vmem_limit_bytes=WHITEN_VMEM),
        name="whiten",
    )(traces, valid_mask.T, jnp.asarray(fold_table()))


def corr_kernel(pick, slots_ref, panels_ref, lag_ref, stack_ref, out_ref, cross):
    step = pl.program_id(0)
    count, chans = out_ref.shape[0], out_ref.shape[1]
    own = panels_ref[pick(lax.axis_index("row"))].astype(jnp.float32)
    minutes = own.shape[0] // chans
    for j in range(count):
        part = panels_ref[pick(slots_ref[0, step * count + j])].astype(jnp.float32)
        for a in range(0, chans, 2):
            both_re, both_im = [], []
            for channel in (a, a + 1):
                re = im = None
                for m in range(minutes):
                    row = m * chans + channel
                    o_re, o_im = own[row : row + 1, :LANES], own[row : row + 1, LANES:]
                    p_re = part[m * chans : (m + 1) * chans, :LANES]
                    p_im = part[m * chans : (m + 1) * chans, LANES:]
                    r = o_re * p_re + o_im * p_im
                    i = o_im * p_re - o_re * p_im
                    re = r if re is None else re + r
                    im = i if im is None else im + i
                both_re.append(re)
                both_im.append(im)
            rows = slice((j * chans + a) * chans, (j * chans + a + 2) * chans)
            cross[rows, :LANES] = jnp.concatenate(both_re, axis=0).astype(jnp.bfloat16)
            cross[rows, LANES:] = jnp.concatenate(both_im, axis=0).astype(jnp.bfloat16)
    full = jnp.dot(cross[...], lag_ref[...], preferred_element_type=jnp.float32)
    scale = (1.0 / math.sqrt(BINS)) / jnp.maximum(full[:, COLS - 1 :], 1.0)
    corr = (full * scale)[:, :LAGS].reshape(out_ref.shape)
    out_ref[...] = stack_ref[pl.ds(step * count, count)] + corr


def correlate(pick, slots, panels, stack):
    offsets, chans = stack.shape[0], stack.shape[1]
    chunk = max(d for d in range(1, 7) if offsets % d == 0)
    whole = pl.BlockSpec(memory_space=pltpu.VMEM)
    return pl.pallas_call(
        functools.partial(corr_kernel, pick),
        out_shape=jax.ShapeDtypeStruct(stack.shape, jnp.float32),
        grid_spec=pltpu.PrefetchScalarGridSpec(
            num_scalar_prefetch=1,
            grid=(offsets // chunk,),
            in_specs=[whole, whole, whole],
            out_specs=pl.BlockSpec((chunk, chans, chans, LAGS), lambda i, s: (i, 0, 0, 0)),
            scratch_shapes=[pltpu.VMEM((chunk * chans * chans, panels.shape[2]), jnp.bfloat16)],
        ),
        compiler_params=pltpu.CompilerParams(vmem_limit_bytes=CORR_VMEM),
        name="correlate",
    )(slots, panels, jnp.asarray(lag_table()), stack)


def share(own, panel_count, offsets):
    chips = panel_count // 2
    hops = (offsets + 1) // 2
    if panel_count % 2 or hops > 8 or hops + 2 > chips:
        return lax.all_gather(own, "row", axis=0), lambda j: j

    def fetch(far):
        shift = 2 * far
        return lax.ppermute(own, "row", [((i + shift) % panel_count, i) for i in range(panel_count)])

    mine = jnp.stack([own] + [fetch(far) for far in range(1, hops)] + [fetch(-1)])
    both = [[2 * c, 2 * c + 1] for c in range(chips)]
    panels = lax.all_gather(mine, "row", axis=0, tiled=True, axis_index_groups=both)

    def pick(j):
        base = (lax.axis_index("row") // 2) * 2
        ahead = lax.rem(j - base + panel_count, panel_count)
        far = ahead // 2
        place = jnp.where(far == chips - 1, hops, far)
        return lax.rem(ahead, 2) * (hops + 1) + place

    return panels, pick


def shards(traces, valid_mask, pair_table, stack_in):
    own = whiten(traces, valid_mask)
    panels, pick = share(own, lax.axis_size("row"), pair_table.shape[1])
    return correlate(pick, pair_table, panels, stack_in[0])[None]


def solution(mesh):
    in_specs = (
        P(("parts", "row"), None, None),
        P(("parts", "row"), None),
        P(("parts", "row"), None),
        P(("parts", "row"), None, None, None, None),
    )
    out_specs = P(("parts", "row"), None, None, None, None)
    return jax.shard_map(shards, mesh=mesh, in_specs=in_specs, out_specs=out_specs, check_vma=False)
```

time: 27 us -> 22.5 us (0.83)
  Pallas kernels: 9.33 us -> 6.79 us
  local copies, waits for them, and re-layouts: 2.61 us -> 0.85 us
    pallas_call x1, Pallas kernels: 4.92 us -> 3.14 us  [correlate(): pl.pallas_call(functools.partial(corr_kernel, pick), out_shape=jax.ShapeD...]
    transpose x1 -> x0, local copies, waits for them, and re-layouts: 1.77 us -> none  [whiten(): x = jnp.swapaxes(traces, 0, 1).reshape(rows, samples)]
    pallas_call x1, Pallas kernels: 4.41 us -> 3.65 us  [whiten(): pl.pallas_call(whiten_kernel, out_shape=jax.ShapeDtypeStruct((rows, 2 * L...]
    unnamed x5 -> x11, local copies, waits for them, and re-layouts: 0.83 us -> 0.84 us
  transfers between devices with their start and end apart: 5 -> 5, of which waited for: 1 -> 1; matrix products, arithmetic and copies ran while one was open for 3% -> 4% of each run, Pallas kernels for 0% -> 0%
where the time goes in v3:
time: 22.5 us; the launch traced here: 22.3 us
  starting transfers between devices  11 us (49%)
  Pallas kernels  6.79 us (30%)
  blocking collectives  2.16 us (10%)
  waiting for transfers between devices  1.46 us (6%)
  local copies, waits for them, and re-layouts  0.85 us (4%)
    ppermute x5, starting transfers between devices, fetch(): lax.ppermute(own, 'row', [((i + shift) % panel_count, i) for i in range(p...  11 us
    pallas_call x1, Pallas kernels, whiten(): pl.pallas_call(whiten_kernel, out_shape=jax.ShapeDtypeStruct((rows, 2 * L...  3.65 us
    pallas_call x1, Pallas kernels, correlate(): pl.pallas_call(functools.partial(corr_kernel, pick), out_shape=jax.ShapeD...  3.14 us
    all_gather x1, blocking collectives, share(): lax.all_gather(mine, 'row', axis=0, tiled=True, axis_index_groups=both)  2.16 us
    ppermute x5, waiting for transfers between devices, fetch(): lax.ppermute(own, 'row', [((i + shift) % panel_count, i) for i in range(p...  1.46 us
    unnamed x11, local copies, waits for them, and re-layouts  0.84 us
  transfers between devices with their start and end apart: 5, of which 1 were waited for; matrix products, arithmetic and copies ran while one was open for 4% of the time, Pallas kernels for 0%

profile of v3, /device:TPU:0, one launch (start us, length us, event | category | flops | bytes accessed | tf_op | source)
XLA Modules:
  0.0 22.3 jit_solution(17802593869135304519)
XLA Ops:
  0.0 0.0 copy-start
  0.0 0.0 copy-start.1
  0.0 0.0 copy-start.2
  0.0 3.6 %whiten.1 = bf16[16,1280]{1,0:T(8,128)(2,1)} custom-call(bf16[8,2,12000]{2,1,0:T(2,128)(2,1)} %x_hbm.1, s32[2,8]{1,0:T(2,128)} %bitcast.16, bf16[600,1280]{1,0:T(8,128)(2,1)} %constant.4.clone.table_hbm), custom_call_target="tpu_custom_call" | custom-call | tf_op jit(solution)/shard_map/whiten/pallas_call | solution.py:186
  3.7 3.0 %collective-permute-start.4 = (bf16[16,1280]{1,0:T(8,128)(2,1)}, bf16[16,1280]{1,0:T(8,128)(2,1)S(1)}, u32[]{:S(2)}, u32[]{:S(2)}) collective-permute-start(bf16[16,1280]{1,0:T(8,128)(2,1)} %whiten.1), channel_id=1, source_target_pairs={{14,0},{15,1},{0,2},{1,3},{2,4},{3,5},{4,6},{5,7},{6,8},{7,9},{8,1... | collective-permute-start | bytes 122888 | tf_op jit(solution)/shard_map/ppermute | solution.py:261
  6.7 2.6 %collective-permute-start.3 = (bf16[16,1280]{1,0:T(8,128)(2,1)}, bf16[16,1280]{1,0:T(8,128)(2,1)S(1)}, u32[]{:S(2)}, u32[]{:S(2)}) collective-permute-start(bf16[16,1280]{1,0:T(8,128)(2,1)} %whiten.1), channel_id=1, source_target_pairs={{8,0},{9,1},{10,2},{11,3},{12,4},{13,5},{14,6},{15,7},{0,8},{1,9},... | collective-permute-start | bytes 122888 | tf_op jit(solution)/shard_map/ppermute | solution.py:261
  9.3 1.3 %collective-permute-start.2 = (bf16[16,1280]{1,0:T(8,128)(2,1)}, bf16[16,1280]{1,0:T(8,128)(2,1)S(1)}, u32[]{:S(2)}, u32[]{:S(2)}) collective-permute-start(bf16[16,1280]{1,0:T(8,128)(2,1)} %whiten.1), channel_id=1, source_target_pairs={{6,0},{7,1},{8,2},{9,3},{10,4},{11,5},{12,6},{13,7},{14,8},{15,9},... | collective-permute-start | bytes 122888 | tf_op jit(solution)/shard_map/ppermute | solution.py:261
  10.6 2.1 %collective-permute-start.1 = (bf16[16,1280]{1,0:T(8,128)(2,1)}, bf16[16,1280]{1,0:T(8,128)(2,1)S(1)}, u32[]{:S(2)}, u32[]{:S(2)}) collective-permute-start(bf16[16,1280]{1,0:T(8,128)(2,1)} %whiten.1), channel_id=1, source_target_pairs={{4,0},{5,1},{6,2},{7,3},{8,4},{9,5},{10,6},{11,7},{12,8},{13,9},{1... | collective-permute-start | bytes 122888 | tf_op jit(solution)/shard_map/ppermute | solution.py:261
  12.7 1.9 %collective-permute-start = (bf16[16,1280]{1,0:T(8,128)(2,1)}, bf16[16,1280]{1,0:T(8,128)(2,1)S(1)}, u32[]{:S(2)}, u32[]{:S(2)}) collective-permute-start(bf16[16,1280]{1,0:T(8,128)(2,1)} %whiten.1), channel_id=1, source_target_pairs={{2,0},{3,1},{4,2},{5,3},{6,4},{7,5},{8,6},{9,7},{10,8},{11,9},{12,... | collective-permute-start | bytes 122888 | tf_op jit(solution)/shard_map/ppermute | solution.py:261
  14.7 0.8 %bitcast_dynamic-update-slice_fusion.5 = bf16[6,16,1280]{2,1,0:T(8,128)(2,1)S(1)} fusion(bf16[16,1280]{1,0:T(8,128)(2,1)} %whiten.1), kind=kLoop, calls=%fused_computation.5 | loop fusion | bytes 81920
  15.5 1.4 %collective-permute-done = bf16[16,1280]{1,0:T(8,128)(2,1)S(1)} collective-permute-done((bf16[16,1280]{1,0:T(8,128)(2,1)}, bf16[16,1280]{1,0:T(8,128)(2,1)S(1)}, u32[]{:S(2)}, u32[]{:S(2)}) %collective-permute-start) | collective-permute-done | bytes 40992 | tf_op jit(solution)/shard_map/ppermute | solution.py:261
  16.9 0.0 collective-permute-done.1
  16.9 0.0 collective-permute-done.2
  17.0 0.0 collective-permute-done.3
  17.0 0.0 collective-permute-done.4
  17.0 2.2 %all_gather.3.panels_ref = bf16[12,16,1280]{2,1,0:T(8,128)(2,1)S(1)} all-gather(bf16[6,16,1280]{2,1,0:T(8,128)(2,1)S(1)} %bitcast_dynamic-update-slice_fusion), channel_id=1, replica_groups={{0,1},{2,3},{4,5},{6,7},{8,9},{10,11},{12,13},{14,15},{16,17},{18,19},{..., dimensions={0}, use_global_device_ids=true | all-gather | bytes 737280 | tf_op jit(solution)/shard_map/all_gather | solution.py:265
  19.2 0.0 copy-done
  19.2 0.0 copy-done.1
  19.2 0.0 copy-done.2
  19.2 3.1 %correlate.1 = f32[10,8,8,401]{3,2,1,0:T(8,128)} custom-call(s32[1,10]{1,0:T(1,128)S(1)} %copy-done.2, bf16[12,16,1280]{2,1,0:T(8,128)(2,1)S(1)} %all_gather.3.panels_ref, bf16[1280,512]{1,0:T(8,128)(2,1)S(1)} %copy-done.1, f32[10,8,8,401]{3,2,1,0:T(8,128)S(1)} %bitcast.15), custom_call_target="tpu_custom_call" | custom-call | tf_op jit(solution)/shard_map/correlate/pallas_call | solution.py:238
  (5 shorter events, 0.0 us)
Async XLA Ops:
  0.0 19.2 %copy-start = (f32[1,10,8,8,401]{4,3,2,1,0:T(8,128)S(1)}, f32[1,10,8,8,401]{4,3,2,1,0:T(8,128)}, u32[]{:S(2)}) copy-start(f32[1,10,8,8,401]{4,3,2,1,0:T(8,128)} %param.9) | copy-start | bytes 3079684
  0.0 19.2 %copy-start.1 = (bf16[1280,512]{1,0:T(8,128)(2,1)S(1)}, bf16[1280,512]{1,0:T(8,128)(2,1)}, u32[]{:S(2)}) copy-start(bf16[1280,512]{1,0:T(8,128)(2,1)} %constant.5.clone.lag_ref) | copy-start | bytes 3932164
  0.0 19.2 %copy-start.2 = (s32[1,10]{1,0:T(1,128)S(1)}, s32[1,10]{1,0:T(1,128)}, u32[]{:S(2)}) copy-start(s32[1,10]{1,0:T(1,128)} %slots_ref.1) | copy-start | bytes 124
  3.7 13.3 %collective-permute-start.4 = (bf16[16,1280]{1,0:T(8,128)(2,1)}, bf16[16,1280]{1,0:T(8,128)(2,1)S(1)}, u32[]{:S(2)}, u32[]{:S(2)}) collective-permute-start(bf16[16,1280]{1,0:T(8,128)(2,1)} %whiten.1), channel_id=1, source_target_pairs={{14,0},{15,1},{0,2},{1,3},{2,4},{3,5},{4,6},{5,7},{6,8},{7,9},{8,1... | collective-permute-start | bytes 122888 | tf_op jit(solution)/shard_map/ppermute | solution.py:261
  6.7 10.3 %collective-permute-start.3 = (bf16[16,1280]{1,0:T(8,128)(2,1)}, bf16[16,1280]{1,0:T(8,128)(2,1)S(1)}, u32[]{:S(2)}, u32[]{:S(2)}) collective-permute-start(bf16[16,1280]{1,0:T(8,128)(2,1)} %whiten.1), channel_id=1, source_target_pairs={{8,0},{9,1},{10,2},{11,3},{12,4},{13,5},{14,6},{15,7},{0,8},{1,9},... | collective-permute-start | bytes 122888 | tf_op jit(solution)/shard_map/ppermute | solution.py:261
  9.3 7.7 %collective-permute-start.2 = (bf16[16,1280]{1,0:T(8,128)(2,1)}, bf16[16,1280]{1,0:T(8,128)(2,1)S(1)}, u32[]{:S(2)}, u32[]{:S(2)}) collective-permute-start(bf16[16,1280]{1,0:T(8,128)(2,1)} %whiten.1), channel_id=1, source_target_pairs={{6,0},{7,1},{8,2},{9,3},{10,4},{11,5},{12,6},{13,7},{14,8},{15,9},... | collective-permute-start | bytes 122888 | tf_op jit(solution)/shard_map/ppermute | solution.py:261
  10.6 6.4 %collective-permute-start.1 = (bf16[16,1280]{1,0:T(8,128)(2,1)}, bf16[16,1280]{1,0:T(8,128)(2,1)S(1)}, u32[]{:S(2)}, u32[]{:S(2)}) collective-permute-start(bf16[16,1280]{1,0:T(8,128)(2,1)} %whiten.1), channel_id=1, source_target_pairs={{4,0},{5,1},{6,2},{7,3},{8,4},{9,5},{10,6},{11,7},{12,8},{13,9},{1... | collective-permute-start | bytes 122888 | tf_op jit(solution)/shard_map/ppermute | solution.py:261
  12.7 4.2 %collective-permute-start = (bf16[16,1280]{1,0:T(8,128)(2,1)}, bf16[16,1280]{1,0:T(8,128)(2,1)S(1)}, u32[]{:S(2)}, u32[]{:S(2)}) collective-permute-start(bf16[16,1280]{1,0:T(8,128)(2,1)} %whiten.1), channel_id=1, source_target_pairs={{2,0},{3,1},{4,2},{5,3},{6,4},{7,5},{8,6},{9,7},{10,8},{11,9},{12,... | collective-permute-start | bytes 122888 | tf_op jit(solution)/shard_map/ppermute | solution.py:261

commit v4 on v3

--- a/solution.py
+++ b/solution.py
@@ -200,34 +200,42 @@
     )(traces, valid_mask.T, jnp.asarray(fold_table()))
 
 
+def cross_tile(own, part, chans, cross, j):
+    minutes = own.shape[0] // chans
+    for a in range(0, chans, 2):
+        both_re, both_im = [], []
+        for channel in (a, a + 1):
+            re = im = None
+            for m in range(minutes):
+                row = m * chans + channel
+                o_re, o_im = own[row : row + 1, :LANES], own[row : row + 1, LANES:]
+                p_re = part[m * chans : (m + 1) * chans, :LANES]
+                p_im = part[m * chans : (m + 1) * chans, LANES:]
+                r = o_re * p_re + o_im * p_im
+                i = o_im * p_re - o_re * p_im
+                re = r if re is None else re + r
+                im = i if im is None else im + i
+            both_re.append(re)
+            both_im.append(im)
+        rows = slice((j * chans + a) * chans, (j * chans + a + 2) * chans)
+        cross[rows, :LANES] = jnp.concatenate(both_re, axis=0).astype(jnp.bfloat16)
+        cross[rows, LANES:] = jnp.concatenate(both_im, axis=0).astype(jnp.bfloat16)
+
+
+def lag_product(cross, table, shape):
+    full = jnp.dot(cross, table, preferred_element_type=jnp.float32)
+    scale = (1.0 / math.sqrt(BINS)) / jnp.maximum(full[:, COLS - 1 :], 1.0)
+    return (full * scale)[:, :LAGS].reshape(shape)
+
+
 def corr_kernel(pick, slots_ref, panels_ref, lag_ref, stack_ref, out_ref, cross):
     step = pl.program_id(0)
     count, chans = out_ref.shape[0], out_ref.shape[1]
     own = panels_ref[pick(lax.axis_index("row"))].astype(jnp.float32)
-    minutes = own.shape[0] // chans
     for j in range(count):
         part = panels_ref[pick(slots_ref[0, step * count + j])].astype(jnp.float32)
-        for a in range(0, chans, 2):
-            both_re, both_im = [], []
-            for channel in (a, a + 1):
-                re = im = None
-                for m in range(minutes):
-                    row = m * chans + channel
-                    o_re, o_im = own[row : row + 1, :LANES], own[row : row + 1, LANES:]
-                    p_re = part[m * chans : (m + 1) * chans, :LANES]
-                    p_im = part[m * chans : (m + 1) * chans, LANES:]
-                    r = o_re * p_re + o_im * p_im
-                    i = o_im * p_re - o_re * p_im
-                    re = r if re is None else re + r
-                    im = i if im is None else im + i
-                both_re.append(re)
-                both_im.append(im)
-            rows = slice((j * chans + a) * chans, (j * chans + a + 2) * chans)
-            cross[rows, :LANES] = jnp.concatenate(both_re, axis=0).astype(jnp.bfloat16)
-            cross[rows, LANES:] = jnp.concatenate(both_im, axis=0).astype(jnp.bfloat16)
-    full = jnp.dot(cross[...], lag_ref[...], preferred_element_type=jnp.float32)
-    scale = (1.0 / math.sqrt(BINS)) / jnp.maximum(full[:, COLS - 1 :], 1.0)
-    corr = (full * scale)[:, :LAGS].reshape(out_ref.shape)
+        cross_tile(own, part, chans, cross, j)
+    corr = lag_product(cross[...], lag_ref[...], out_ref.shape)
     out_ref[...] = stack_ref[pl.ds(step * count, count)] + corr
 
 
@@ -250,34 +258,129 @@
     )(slots, panels, jnp.asarray(lag_table()), stack)
 
 
-def share(own, panel_count, offsets):
+def gather_all(own, slots, stack):
+    panels = lax.all_gather(own, "row", axis=0)
+    return correlate(lambda j: j, slots, panels, stack)
+
+
+def place(panel_count):
+    me = lax.axis_index("row")
+    return me, me // 2, lax.rem(me, 2), lax.rem(me // 2, 2)
+
+
+def first_hop(panel_count):
+    me, chip, core, odd = place(panel_count)
+    a = jnp.where(core == 0, chip + 1 - 2 * odd, chip + 2)
+    b = jnp.where(core == 0, chip - 1 + 4 * odd, chip + 3 - 2 * odd)
+    return a, b
+
+
+def pair_panels(panel_count):
+    me, chip, core, odd = place(panel_count)
+    return [(0, 2 * chip, True), (1, 2 * chip + 1, True)]
+
+
+def near_panels(panel_count):
+    me, chip, core, odd = place(panel_count)
+    a, b = first_hop(panel_count)
+    return [(0, 2 * a, True), (1, 2 * a + 1, True), (2, 2 * b, True), (3, 2 * b + 1, True), (4, me + 8, True)]
+
+
+def swapped_panels(panel_count):
+    me, chip, core, odd = place(panel_count)
+    low = 2 * odd * core
+    found = []
+    for t in range(2):
+        ahead = jnp.where(core == 0, chip + 2, chip + 1 + 2 * odd)
+        found.append((low + t, 2 * ahead + t, True))
+    for t in range(2):
+        ahead = 2 * (chip + 3 - 2 * odd) + t
+        found.append((jnp.where(core == 0, 2 + t, 4), jnp.where(core == 0, ahead, 2 * chip + 8), (core == 0) | (t == 0)))
+    return found
+
+
+def tiles_kernel(panel_count, which, fresh, *refs):
+    slots_ref, pair_ref, panels_ref, lag_ref, stack_ref = refs[:5]
+    out_ref, cross, result, sem = refs[5 if fresh else 6 :]
+    offsets, chans = stack_ref.shape[0], stack_ref.shape[1]
+    me = lax.axis_index("row")
+    own = pair_ref[lax.rem(me, 2)].astype(jnp.float32)
+    found = which(panel_count)
+    todo = []
+    for j, (at, panel, wanted) in enumerate(found):
+        panel = lax.rem(panel + panel_count, panel_count)
+        valid = (lax.rem(panel - me + 1 + panel_count, panel_count) < offsets) & wanted
+        slot = jnp.int32(0)
+        for o in range(1, offsets):
+            slot = jnp.where(slots_ref[0, o] == panel, o, slot)
+        todo.append((at, slot, valid))
+    copies = []
+    for start in range(0, len(found), 2):
+        some = todo[start : start + 2]
+        for j, (at, slot, valid) in enumerate(some):
+            cross_tile(own, panels_ref[at].astype(jnp.float32), chans, cross, start + j)
+        rows = slice(start * chans * chans, (start + len(some)) * chans * chans)
+        corr = lag_product(cross[rows], lag_ref[...], (len(some), chans, chans, LAGS))
+        for j, (at, slot, valid) in enumerate(some):
+            result[start + j] = stack_ref[slot] + corr[j]
+            copies.append((valid, pltpu.make_async_copy(result.at[start + j], out_ref.at[slot], sem.at[start + j])))
+            pl.when(valid)(copies[-1][1].start)
+    for valid, copy in copies:
+        pl.when(valid)(copy.wait)
+
+
+def tiles(which, count, panel_count, slots, pair, panels, table, stack, out=None):
+    offsets, chans = stack.shape[0], stack.shape[1]
+    whole = pl.BlockSpec(memory_space=pltpu.VMEM)
+    hbm = pl.BlockSpec(memory_space=pltpu.HBM)
+    rows = count * chans * chans
+    return pl.pallas_call(
+        functools.partial(tiles_kernel, panel_count, which, out is None),
+        out_shape=jax.ShapeDtypeStruct(stack.shape, jnp.float32),
+        in_specs=[pl.BlockSpec(memory_space=pltpu.SMEM), whole, whole, whole, whole] + ([] if out is None else [hbm]),
+        out_specs=hbm,
+        scratch_shapes=[
+            pltpu.VMEM((rows, 2 * LANES), jnp.bfloat16),
+            pltpu.VMEM((count, chans, chans, LAGS), jnp.float32),
+            pltpu.SemaphoreType.DMA((count,)),
+        ],
+        input_output_aliases={} if out is None else {5: 0},
+        compiler_params=pltpu.CompilerParams(vmem_limit_bytes=CORR_VMEM),
+        cost_estimate=pl.CostEstimate(flops=4 * rows * LANES * COLS, bytes_accessed=4 * rows * COLS, transcendentals=0),
+        name=which.__name__,
+    )(slots, pair, panels, table, stack, *([] if out is None else [out]))
+
+
+def gather_near(own, slots, stack, panel_count):
     chips = panel_count // 2
-    hops = (offsets + 1) // 2
-    if panel_count % 2 or hops > 8 or hops + 2 > chips:
-        return lax.all_gather(own, "row", axis=0), lambda j: j
-
-    def fetch(far):
-        shift = 2 * far
-        return lax.ppermute(own, "row", [((i + shift) % panel_count, i) for i in range(panel_count)])
-
-    mine = jnp.stack([own] + [fetch(far) for far in range(1, hops)] + [fetch(-1)])
-    both = [[2 * c, 2 * c + 1] for c in range(chips)]
-    panels = lax.all_gather(mine, "row", axis=0, tiled=True, axis_index_groups=both)
-
-    def pick(j):
-        base = (lax.axis_index("row") // 2) * 2
-        ahead = lax.rem(j - base + panel_count, panel_count)
-        far = ahead // 2
-        place = jnp.where(far == chips - 1, hops, far)
-        return lax.rem(ahead, 2) * (hops + 1) + place
-
-    return panels, pick
+    pair = lax.all_gather(own, "row", axis=0, axis_index_groups=[[2 * c, 2 * c + 1] for c in range(chips)])
+
+    def fetch(array, even, odd):
+        ahead = [even, odd]
+        moves = []
+        for i in range(panel_count):
+            c = i // 2
+            moves.append((2 * ((c + ahead[i % 2][c % 2]) % chips) + i % 2, i))
+        return lax.ppermute(array, "row", moves)
+
+    table = jnp.asarray(lag_table())
+    near = fetch(pair, (1, -1), (2, 2))
+    next_near = fetch(pair, (-1, 3), (3, 1))
+    far = fetch(own, (4, 4), (4, 4))
+    out = tiles(pair_panels, 2, panel_count, slots, pair, pair, table, stack)
+    near, next_near, far, out = lax.optimization_barrier((near, next_near, far, out))
+    five = jnp.concatenate([near, next_near, far[None]], axis=0)
+    swapped = lax.ppermute(five, "row", [(i ^ 1, i) for i in range(panel_count)])
+    out = tiles(near_panels, 5, panel_count, slots, pair, five, table, stack, out)
+    return tiles(swapped_panels, 4, panel_count, slots, pair, swapped, table, stack, out)
 
 
 def shards(traces, valid_mask, pair_table, stack_in):
     own = whiten(traces, valid_mask)
-    panels, pick = share(own, lax.axis_size("row"), pair_table.shape[1])
-    return correlate(pick, pair_table, panels, stack_in[0])[None]
+    panel_count = lax.axis_size("row")
+    if pair_table.shape[1] == 10 and panel_count >= 12 and panel_count % 4 == 0:
+        return gather_near(own, pair_table, stack_in[0], panel_count)[None]
+    return gather_all(own, pair_table, stack_in[0])[None]
 
 
 def solution(mesh):

time: 22.5 us -> 21.5 us (0.956)
  the two profiles are of different devices: /device:TPU:0 before, /device:TPU:25 now
where the time goes in v4:
time: 21.5 us; the launch traced here: 21.4 us
  Pallas kernels  9.71 us (45%)
  starting transfers between devices  6.06 us (28%)
  blocking collectives  2.4 us (11%)
  waiting for transfers between devices  1.83 us (9%)
  local copies, waits for them, and re-layouts  1.32 us (6%)
    pallas_call x3, Pallas kernels, tiles(): pl.pallas_call(functools.partial(tiles_kernel, panel_count, which, out is...  6.11 us
    ppermute x3, starting transfers between devices, fetch(): return lax.ppermute(array, 'row', moves)  4.47 us
    pallas_call x1, Pallas kernels, whiten(): pl.pallas_call(whiten_kernel, out_shape=jax.ShapeDtypeStruct((rows, 2 * L...  3.6 us
    all_gather x1, blocking collectives, gather_near(): lax.all_gather(own, 'row', axis=0, axis_index_groups=[[2 * c, 2 * c + 1]...  2.4 us
    ppermute x3, waiting for transfers between devices, fetch(): return lax.ppermute(array, 'row', moves)  1.83 us
    ppermute x1, starting transfers between devices, gather_near(): lax.ppermute(five, 'row', [(i ^ 1, i) for i in range(panel_count)])  1.58 us
    unnamed x6, local copies, waits for them, and re-layouts  1.32 us
  transfers between devices with their start and end apart: 4, of which 1 were waited for; matrix products, arithmetic and copies ran while one was open for 0% of the time, Pallas kernels for 19%

profile of v4, /device:TPU:25, one launch (start us, length us, event | category | flops | bytes accessed | tf_op | source)
XLA Modules:
  0.0 21.4 jit_solution(18387676686564620119)
XLA Ops:
  0.0 0.0 copy-start.2
  0.0 0.0 copy-start
  0.0 3.6 %whiten.1 = bf16[16,1280]{1,0:T(8,128)(2,1)} custom-call(bf16[8,2,12000]{2,1,0:T(2,128)(2,1)} %x_hbm.1, s32[2,8]{1,0:T(2,128)} %bitcast.15, bf16[600,1280]{1,0:T(8,128)(2,1)} %constant.4.clone.table_hbm), custom_call_target="tpu_custom_call" | custom-call | tf_op jit(solution)/shard_map/whiten/pallas_call | solution.py:186
  3.6 2.4 %all-gather = bf16[32,1280]{1,0:T(8,128)(2,1)S(1)} all-gather(bf16[16,1280]{1,0:T(8,128)(2,1)} %whiten.1), channel_id=2, replica_groups={{0,1},{2,3},{4,5},{6,7},{8,9},{10,11},{12,13},{14,15},{16,17},{18,19},{..., dimensions={0}, use_global_device_ids=true | all-gather | bytes 122880 | tf_op jit(solution)/shard_map/all_gather | solution.py:356
  6.0 1.1 %collective-permute-start.1 = (bf16[2,16,1280]{2,1,0:T(8,128)(2,1)S(1)}, bf16[2,16,1280]{2,1,0:T(8,128)(2,1)S(1)}, u32[]{:S(2)}, u32[]{:S(2)}) collective-permute-start(bf16[2,16,1280]{2,1,0:T(8,128)(2,1)S(1)} %bitcast.8), channel_id=1, source_target_pairs={{14,0},{7,1},{8,2},{5,3},{2,4},{11,5},{12,6},{9,7},{6,8},{15,9},{0... | collective-permute-start | bytes 245768 | tf_op jit(solution)/shard_map/ppermute | solution.py:364
  7.1 0.2 collective-permute-start
  7.3 3.2 %collective-permute-start.2 = (bf16[16,1280]{1,0:T(8,128)(2,1)}, bf16[16,1280]{1,0:T(8,128)(2,1)S(1)}, u32[]{:S(2)}, u32[]{:S(2)}) collective-permute-start(bf16[16,1280]{1,0:T(8,128)(2,1)} %whiten.1), channel_id=1, source_target_pairs={{8,0},{9,1},{10,2},{11,3},{12,4},{13,5},{14,6},{15,7},{0,8},{1,9},... | collective-permute-start | bytes 122888 | tf_op jit(solution)/shard_map/ppermute | solution.py:364
  10.5 0.0 copy-done.2
  10.5 0.0 copy-done
  10.5 0.0 copy-start.1
  10.5 1.3 %copy-done.1 = bf16[1280,512]{1,0:T(8,128)(2,1)S(1)} copy-done((bf16[1280,512]{1,0:T(8,128)(2,1)S(1)}, bf16[1280,512]{1,0:T(8,128)(2,1)}, u32[]{:S(2)}) %copy-start.1) | copy-done | bytes 1310744
  11.8 1.8 %pair_panels.1.refs_5_ = f32[10,8,8,401]{3,2,1,0:T(8,128)} custom-call(s32[1,10]{1,0:T(1,128)S(1)} %copy-done.2, bf16[2,16,1280]{2,1,0:T(8,128)(2,1)S(1)} %bitcast.10, bf16[2,16,1280]{2,1,0:T(8,128)(2,1)S(1)} %bitcast.11, bf16[1280,512]{1,0:T(8,128)(2,1)S(1)} %copy-done.1, f32[10,8,8,401]{3,2,1,0:T(8,128)S(1)} %bitcast.5), custom_call_target="tpu_custom_call" | custom-call | flops 167772160 | bytes 262144 | tf_op jit(solution)/shard_map/pair_panels/pallas_call | solution.py:337
  13.6 1.8 %collective-permute-done.2 = bf16[16,1280]{1,0:T(8,128)(2,1)S(1)} collective-permute-done((bf16[16,1280]{1,0:T(8,128)(2,1)}, bf16[16,1280]{1,0:T(8,128)(2,1)S(1)}, u32[]{:S(2)}, u32[]{:S(2)}) %collective-permute-start.2) | collective-permute-done | bytes 40992 | tf_op jit(solution)/shard_map/ppermute | solution.py:364
  15.4 0.0 collective-permute-done.1
  15.4 0.0 collective-permute-done
  15.4 1.6 %collective-permute-start.3 = (bf16[5,16,1280]{2,1,0:T(8,128)(2,1)S(1)}, bf16[5,16,1280]{2,1,0:T(8,128)(2,1)S(1)}, u32[]{:S(2)}, u32[]{:S(2)}) collective-permute-start(bf16[5,16,1280]{2,1,0:T(8,128)(2,1)S(1)} %pad_maximum_fusion.refs_2_), channel_id=1, source_target_pairs={{1,0},{0,1},{3,2},{2,3},{5,4},{4,5},{7,6},{6,7},{9,8},{8,9},{11,10... | collective-permute-start | bytes 614408 | tf_op jit(solution)/shard_map/ppermute | solution.py:373
  17.0 2.3 %near_panels.1.refs_5_ = f32[10,8,8,401]{3,2,1,0:T(8,128)} custom-call(s32[1,10]{1,0:T(1,128)S(1)} %copy-done.2, bf16[2,16,1280]{2,1,0:T(8,128)(2,1)S(1)} %bitcast.12, bf16[5,16,1280]{2,1,0:T(8,128)(2,1)S(1)} %pad_maximum_fusion.refs_2_, bf16[1280,512]{1,0:T(8,128)(2,1)S(1)} %copy-done.1, ...), custom_call_target="tpu_custom_call", output_to_operand_aliasing={{}: (5, {})} | custom-call | flops 419430400 | bytes 655360 | tf_op jit(solution)/shard_map/near_panels/pallas_call | solution.py:337
  19.3 0.0 collective-permute-done.3.refs_2_
  19.4 2.0 %swapped_panels.1 = f32[10,8,8,401]{3,2,1,0:T(8,128)} custom-call(s32[1,10]{1,0:T(1,128)S(1)} %copy-done.2, bf16[2,16,1280]{2,1,0:T(8,128)(2,1)S(1)} %bitcast.13, bf16[5,16,1280]{2,1,0:T(8,128)(2,1)S(1)} %collective-permute-done.3.refs_2_, bf16[1280,512]{1,0:T(8,128)(2,1)S(1)} %copy-done.1, ...), custom_call_target="tpu_custom_call", output_to_operand_aliasing={{}: (5, {})} | custom-call | flops 335544320 | bytes 524288 | tf_op jit(solution)/shard_map/swapped_panels/pallas_call | solution.py:337
  (1 shorter events, 0.0 us)
Async XLA Ops:
  0.0 10.5 %copy-start.2 = (s32[1,10]{1,0:T(1,128)S(1)}, s32[1,10]{1,0:T(1,128)}, u32[]{:S(2)}) copy-start(s32[1,10]{1,0:T(1,128)} %refs_0_.5) | copy-start | bytes 124
  0.0 10.5 %copy-start = (f32[1,10,8,8,401]{4,3,2,1,0:T(8,128)S(1)}, f32[1,10,8,8,401]{4,3,2,1,0:T(8,128)}, u32[]{:S(2)}) copy-start(f32[1,10,8,8,401]{4,3,2,1,0:T(8,128)} %param.9) | copy-start | bytes 3079684
  6.0 9.4 %collective-permute-start.1 = (bf16[2,16,1280]{2,1,0:T(8,128)(2,1)S(1)}, bf16[2,16,1280]{2,1,0:T(8,128)(2,1)S(1)}, u32[]{:S(2)}, u32[]{:S(2)}) collective-permute-start(bf16[2,16,1280]{2,1,0:T(8,128)(2,1)S(1)} %bitcast.8), channel_id=1, source_target_pairs={{14,0},{7,1},{8,2},{5,3},{2,4},{11,5},{12,6},{9,7},{6,8},{15,9},{0... | collective-permute-start | bytes 245768 | tf_op jit(solution)/shard_map/ppermute | solution.py:364
  7.1 8.3 %collective-permute-start = (bf16[2,16,1280]{2,1,0:T(8,128)(2,1)S(1)}, bf16[2,16,1280]{2,1,0:T(8,128)(2,1)S(1)}, u32[]{:S(2)}, u32[]{:S(2)}) collective-permute-start(bf16[2,16,1280]{2,1,0:T(8,128)(2,1)S(1)} %bitcast.9), channel_id=1, source_target_pairs={{2,0},{5,1},{0,2},{7,3},{6,4},{9,5},{4,6},{11,7},{10,8},{13,9},{8,... | collective-permute-start | bytes 245768 | tf_op jit(solution)/shard_map/ppermute | solution.py:364
  7.3 8.1 %collective-permute-start.2 = (bf16[16,1280]{1,0:T(8,128)(2,1)}, bf16[16,1280]{1,0:T(8,128)(2,1)S(1)}, u32[]{:S(2)}, u32[]{:S(2)}) collective-permute-start(bf16[16,1280]{1,0:T(8,128)(2,1)} %whiten.1), channel_id=1, source_target_pairs={{8,0},{9,1},{10,2},{11,3},{12,4},{13,5},{14,6},{15,7},{0,8},{1,9},... | collective-permute-start | bytes 122888 | tf_op jit(solution)/shard_map/ppermute | solution.py:364
  10.5 1.3 %copy-start.1 = (bf16[1280,512]{1,0:T(8,128)(2,1)S(1)}, bf16[1280,512]{1,0:T(8,128)(2,1)}, u32[]{:S(2)}) copy-start(bf16[1280,512]{1,0:T(8,128)(2,1)} %constant.5.clone.refs_3_) | copy-start | bytes 3932164
  15.4 3.9 %collective-permute-start.3 = (bf16[5,16,1280]{2,1,0:T(8,128)(2,1)S(1)}, bf16[5,16,1280]{2,1,0:T(8,128)(2,1)S(1)}, u32[]{:S(2)}, u32[]{:S(2)}) collective-permute-start(bf16[5,16,1280]{2,1,0:T(8,128)(2,1)S(1)} %pad_maximum_fusion.refs_2_), channel_id=1, source_target_pairs={{1,0},{0,1},{3,2},{2,3},{5,4},{4,5},{7,6},{6,7},{9,8},{8,9},{11,10... | collective-permute-start | bytes 614408 | tf_op jit(solution)/shard_map/ppermute | solution.py:373

commit v5 on v4

--- a/solution.py
+++ b/solution.py
@@ -13,6 +13,7 @@
 SAMPLES = 12000
 FLO = 6
 BINS = 595
+SEGS = 2
 HALF = 40
 LAGS = 401
 EPS = 1e-06
@@ -299,56 +300,93 @@
     return found
 
 
-def tiles_kernel(panel_count, which, fresh, *refs):
-    slots_ref, pair_ref, panels_ref, lag_ref, stack_ref = refs[:5]
-    out_ref, cross, result, sem = refs[5 if fresh else 6 :]
-    offsets, chans = stack_ref.shape[0], stack_ref.shape[1]
-    me = lax.axis_index("row")
-    own = pair_ref[lax.rem(me, 2)].astype(jnp.float32)
+def products(which, panel_count, own, panels_ref, table, chans, cross, keep):
     found = which(panel_count)
-    todo = []
-    for j, (at, panel, wanted) in enumerate(found):
-        panel = lax.rem(panel + panel_count, panel_count)
-        valid = (lax.rem(panel - me + 1 + panel_count, panel_count) < offsets) & wanted
-        slot = jnp.int32(0)
-        for o in range(1, offsets):
-            slot = jnp.where(slots_ref[0, o] == panel, o, slot)
-        todo.append((at, slot, valid))
-    copies = []
     for start in range(0, len(found), 2):
-        some = todo[start : start + 2]
-        for j, (at, slot, valid) in enumerate(some):
+        some = found[start : start + 2]
+        for j, (at, panel, wanted) in enumerate(some):
             cross_tile(own, panels_ref[at].astype(jnp.float32), chans, cross, start + j)
         rows = slice(start * chans * chans, (start + len(some)) * chans * chans)
-        corr = lag_product(cross[rows], lag_ref[...], (len(some), chans, chans, LAGS))
-        for j, (at, slot, valid) in enumerate(some):
-            result[start + j] = stack_ref[slot] + corr[j]
-            copies.append((valid, pltpu.make_async_copy(result.at[start + j], out_ref.at[slot], sem.at[start + j])))
-            pl.when(valid)(copies[-1][1].start)
-    for valid, copy in copies:
-        pl.when(valid)(copy.wait)
-
-
-def tiles(which, count, panel_count, slots, pair, panels, table, stack, out=None):
-    offsets, chans = stack.shape[0], stack.shape[1]
+        full = jnp.dot(cross[rows], table, preferred_element_type=jnp.float32)
+        scale = (1.0 / math.sqrt(BINS)) / jnp.maximum(full[:, COLS - 1 :], 1.0)
+        keep(start, (full * scale).reshape(len(some), chans * chans, COLS))
+
+
+def early_kernel(panel_count, which, pair_ref, panels_ref, table_ref, out_ref, cross):
+    own = pair_ref[lax.rem(lax.axis_index("row"), 2)].astype(jnp.float32)
+
+    def keep(start, corr):
+        out_ref[start : start + corr.shape[0]] = corr
+
+    products(which, panel_count, own, panels_ref, table_ref[...], own.shape[0] // SEGS, cross, keep)
+
+
+def early(which, count, panel_count, chans, pair, panels, table):
     whole = pl.BlockSpec(memory_space=pltpu.VMEM)
-    hbm = pl.BlockSpec(memory_space=pltpu.HBM)
     rows = count * chans * chans
     return pl.pallas_call(
-        functools.partial(tiles_kernel, panel_count, which, out is None),
-        out_shape=jax.ShapeDtypeStruct(stack.shape, jnp.float32),
-        in_specs=[pl.BlockSpec(memory_space=pltpu.SMEM), whole, whole, whole, whole] + ([] if out is None else [hbm]),
-        out_specs=hbm,
-        scratch_shapes=[
-            pltpu.VMEM((rows, 2 * LANES), jnp.bfloat16),
-            pltpu.VMEM((count, chans, chans, LAGS), jnp.float32),
-            pltpu.SemaphoreType.DMA((count,)),
-        ],
-        input_output_aliases={} if out is None else {5: 0},
+        functools.partial(early_kernel, panel_count, which),
+        out_shape=jax.ShapeDtypeStruct((count, chans * chans, COLS), jnp.float32),
+        in_specs=[whole] * 3,
+        out_specs=whole,
+        scratch_shapes=[pltpu.VMEM((rows, 2 * LANES), jnp.bfloat16)],
         compiler_params=pltpu.CompilerParams(vmem_limit_bytes=CORR_VMEM),
         cost_estimate=pl.CostEstimate(flops=4 * rows * LANES * COLS, bytes_accessed=4 * rows * COLS, transcendentals=0),
         name=which.__name__,
-    )(slots, pair, panels, table, stack, *([] if out is None else [out]))
+    )(pair, panels, table)
+
+
+def last_kernel(panel_count, lists, slots_ref, pair_ref, panels_ref, table_ref, stack_ref, *refs):
+    done_refs = refs[: len(lists) - 1]
+    out_ref, cross, result, sem = refs[len(lists) - 1 :]
+    offsets, chans = stack_ref.shape[0], stack_ref.shape[1]
+    me = lax.axis_index("row")
+    copies = []
+
+    def finish(found, corr):
+        for j, (at, panel, wanted) in enumerate(found):
+            panel = lax.rem(panel + panel_count, panel_count)
+            valid = (lax.rem(panel - me + 1 + panel_count, panel_count) < offsets) & wanted
+            slot = jnp.int32(0)
+            for o in range(1, offsets):
+                slot = jnp.where(slots_ref[0, o] == panel, o, slot)
+            n = len(copies)
+            result[n] = stack_ref[slot] + corr[j][:, :LAGS].reshape(chans, chans, LAGS)
+            copy = pltpu.make_async_copy(result.at[n], out_ref.at[slot], sem.at[n])
+            copies.append((valid, copy))
+            pl.when(valid)(copy.start)
+
+    for which, done in zip(lists, done_refs):
+        finish(which(panel_count), done)
+    own = pair_ref[lax.rem(me, 2)].astype(jnp.float32)
+    found = lists[-1](panel_count)
+
+    def keep(start, corr):
+        finish(found[start : start + corr.shape[0]], corr)
+
+    products(lists[-1], panel_count, own, panels_ref, table_ref[...], chans, cross, keep)
+    for valid, copy in copies:
+        pl.when(valid)(copy.wait)
+
+
+def last(lists, counts, panel_count, slots, pair, panels, table, stack, *done):
+    offsets, chans = stack.shape[0], stack.shape[1]
+    whole = pl.BlockSpec(memory_space=pltpu.VMEM)
+    rows = counts[-1] * chans * chans
+    return pl.pallas_call(
+        functools.partial(last_kernel, panel_count, lists),
+        out_shape=jax.ShapeDtypeStruct(stack.shape, jnp.float32),
+        in_specs=[pl.BlockSpec(memory_space=pltpu.SMEM)] + [whole] * (4 + len(done)),
+        out_specs=pl.BlockSpec(memory_space=pltpu.HBM),
+        scratch_shapes=[
+            pltpu.VMEM((rows, 2 * LANES), jnp.bfloat16),
+            pltpu.VMEM((sum(counts), chans, chans, LAGS), jnp.float32),
+            pltpu.SemaphoreType.DMA((sum(counts),)),
+        ],
+        compiler_params=pltpu.CompilerParams(vmem_limit_bytes=CORR_VMEM),
+        cost_estimate=pl.CostEstimate(flops=4 * rows * LANES * COLS, bytes_accessed=4 * rows * COLS, transcendentals=0),
+        name=lists[-1].__name__,
+    )(slots, pair, panels, table, stack, *done)
 
 
 def gather_near(own, slots, stack, panel_count):
@@ -367,12 +405,14 @@
     near = fetch(pair, (1, -1), (2, 2))
     next_near = fetch(pair, (-1, 3), (3, 1))
     far = fetch(own, (4, 4), (4, 4))
-    out = tiles(pair_panels, 2, panel_count, slots, pair, pair, table, stack)
-    near, next_near, far, out = lax.optimization_barrier((near, next_near, far, out))
+    chans = stack.shape[1]
+    first = early(pair_panels, 2, panel_count, chans, pair, pair, table)
+    near, next_near, far, first = lax.optimization_barrier((near, next_near, far, first))
     five = jnp.concatenate([near, next_near, far[None]], axis=0)
     swapped = lax.ppermute(five, "row", [(i ^ 1, i) for i in range(panel_count)])
-    out = tiles(near_panels, 5, panel_count, slots, pair, five, table, stack, out)
-    return tiles(swapped_panels, 4, panel_count, slots, pair, swapped, table, stack, out)
+    second = early(near_panels, 5, panel_count, chans, pair, five, table)
+    lists = (pair_panels, near_panels, swapped_panels)
+    return last(lists, (2, 5, 4), panel_count, slots, pair, swapped, table, stack, first, second)
 
 
 def shards(traces, valid_mask, pair_table, stack_in):

time: 21.5 us -> 20.5 us (0.953)
  waiting for transfers between devices: 1.83 us -> 4.52 us
  Pallas kernels: 9.71 us -> 7.29 us
  local copies, waits for them, and re-layouts: 1.32 us -> 0.01 us
    ppermute x3, waiting for transfers between devices: 1.83 us -> 4.41 us  [fetch(): return lax.ppermute(array, 'row', moves)]
    pallas_call x3, Pallas kernels: 6.11 us -> 3.68 us  [the longest x1 2.22 us: last(): pl.pallas_call(functools.partial(last_kernel, panel_count, lists), out_sh...]
    unnamed x6, local copies, waits for them, and re-layouts: 1.32 us -> 0.01 us
  transfers between devices with their start and end apart: 4 -> 4, of which waited for: 1 -> 2; matrix products, arithmetic and copies ran while one was open for 0% -> 0% of each run, Pallas kernels for 19% -> 7%
where the time goes in v5:
time: 20.5 us; the launch traced here: 20.4 us
  Pallas kernels  7.29 us (36%)
  starting transfers between devices  6.06 us (30%)
  waiting for transfers between devices  4.52 us (22%)
  blocking collectives  2.4 us (12%)
    ppermute x3, starting transfers between devices, fetch(): return lax.ppermute(array, 'row', moves)  4.47 us
    ppermute x3, waiting for transfers between devices, fetch(): return lax.ppermute(array, 'row', moves)  4.41 us
    pallas_call x1, Pallas kernels, whiten(): pl.pallas_call(whiten_kernel, out_shape=jax.ShapeDtypeStruct((rows, 2 * L...  3.61 us
    all_gather x1, blocking collectives, gather_near(): lax.all_gather(own, 'row', axis=0, axis_index_groups=[[2 * c, 2 * c + 1]...  2.4 us
    pallas_call x1, Pallas kernels, last(): pl.pallas_call(functools.partial(last_kernel, panel_count, lists), out_sh...  2.22 us
    ppermute x1, starting transfers between devices, gather_near(): lax.ppermute(five, 'row', [(i ^ 1, i) for i in range(panel_count)])  1.58 us
    pallas_call x2, Pallas kernels, early(): pl.pallas_call(functools.partial(early_kernel, panel_count, which), out_s...  1.46 us
  transfers between devices with their start and end apart: 4, of which 2 were waited for; matrix products, arithmetic and copies ran while one was open for 0% of the time, Pallas kernels for 7%

profile of v5, /device:TPU:25, one launch (start us, length us, event | category | flops | bytes accessed | tf_op | source)
XLA Modules:
  0.0 20.4 jit_solution(1230351654590817110)
XLA Ops:
  0.0 0.0 copy-start
  0.0 3.6 %whiten.1 = bf16[16,1280]{1,0:T(8,128)(2,1)} custom-call(bf16[8,2,12000]{2,1,0:T(2,128)(2,1)} %x_hbm.1, s32[2,8]{1,0:T(2,128)} %bitcast.13, bf16[600,1280]{1,0:T(8,128)(2,1)} %constant.4.clone.table_hbm), custom_call_target="tpu_custom_call" | custom-call | tf_op jit(solution)/shard_map/whiten/pallas_call | solution.py:187
  3.6 2.4 %all-gather = bf16[32,1280]{1,0:T(8,128)(2,1)S(1)} all-gather(bf16[16,1280]{1,0:T(8,128)(2,1)} %whiten.1), channel_id=2, replica_groups={{0,1},{2,3},{4,5},{6,7},{8,9},{10,11},{12,13},{14,15},{16,17},{18,19},{..., dimensions={0}, use_global_device_ids=true | all-gather | bytes 122880 | tf_op jit(solution)/shard_map/all_gather | solution.py:394
  6.0 1.1 %collective-permute-start.1 = (bf16[2,16,1280]{2,1,0:T(8,128)(2,1)S(1)}, bf16[2,16,1280]{2,1,0:T(8,128)(2,1)S(1)}, u32[]{:S(2)}, u32[]{:S(2)}) collective-permute-start(bf16[2,16,1280]{2,1,0:T(8,128)(2,1)S(1)} %bitcast.5), channel_id=1, source_target_pairs={{14,0},{7,1},{8,2},{5,3},{2,4},{11,5},{12,6},{9,7},{6,8},{15,9},{0... | collective-permute-start | bytes 245768 | tf_op jit(solution)/shard_map/ppermute | solution.py:402
  7.1 0.2 collective-permute-start
  7.3 3.2 %collective-permute-start.2 = (bf16[16,1280]{1,0:T(8,128)(2,1)}, bf16[16,1280]{1,0:T(8,128)(2,1)S(1)}, u32[]{:S(2)}, u32[]{:S(2)}) collective-permute-start(bf16[16,1280]{1,0:T(8,128)(2,1)} %whiten.1), channel_id=1, source_target_pairs={{8,0},{9,1},{10,2},{11,3},{12,4},{13,5},{14,6},{15,7},{0,8},{1,9},... | collective-permute-start | bytes 122888 | tf_op jit(solution)/shard_map/ppermute | solution.py:402
  10.5 0.0 copy-done
  10.5 0.5 %pair_panels.1.refs_0_ = f32[2,64,512]{2,1,0:T(8,128)S(1)} custom-call(bf16[2,16,1280]{2,1,0:T(8,128)(2,1)S(1)} %bitcast.7, bf16[2,16,1280]{2,1,0:T(8,128)(2,1)S(1)} %bitcast.8, bf16[1280,512]{1,0:T(8,128)(2,1)S(1)} %copy-done), custom_call_target="tpu_custom_call" | custom-call | flops 167772160 | bytes 262144 | tf_op jit(solution)/shard_map/pair_panels/pallas_call | solution.py:327
  11.0 4.4 %collective-permute-done.2 = bf16[16,1280]{1,0:T(8,128)(2,1)S(1)} collective-permute-done((bf16[16,1280]{1,0:T(8,128)(2,1)}, bf16[16,1280]{1,0:T(8,128)(2,1)S(1)}, u32[]{:S(2)}, u32[]{:S(2)}) %collective-permute-start.2) | collective-permute-done | bytes 40992 | tf_op jit(solution)/shard_map/ppermute | solution.py:402
  15.4 0.0 collective-permute-done.1
  15.4 0.0 collective-permute-done
  15.4 0.0 copy-start.1
  15.4 0.0 copy-start.2
  15.5 1.6 %collective-permute-start.3 = (bf16[5,16,1280]{2,1,0:T(8,128)(2,1)S(1)}, bf16[5,16,1280]{2,1,0:T(8,128)(2,1)S(1)}, u32[]{:S(2)}, u32[]{:S(2)}) collective-permute-start(bf16[5,16,1280]{2,1,0:T(8,128)(2,1)S(1)} %pad_maximum_fusion.panels_ref), channel_id=1, source_target_pairs={{1,0},{0,1},{3,2},{2,3},{5,4},{4,5},{7,6},{6,7},{9,8},{8,9},{11,10... | collective-permute-start | bytes 614408 | tf_op jit(solution)/shard_map/ppermute | solution.py:412
  17.0 1.0 %near_panels.1.refs_1_ = f32[5,64,512]{2,1,0:T(8,128)S(1)} custom-call(bf16[2,16,1280]{2,1,0:T(8,128)(2,1)S(1)} %bitcast.9, bf16[5,16,1280]{2,1,0:T(8,128)(2,1)S(1)} %pad_maximum_fusion.panels_ref, bf16[1280,512]{1,0:T(8,128)(2,1)S(1)} %copy-done), custom_call_target="tpu_custom_call" | custom-call | flops 419430400 | bytes 655360 | tf_op jit(solution)/shard_map/near_panels/pallas_call | solution.py:327
  18.0 0.1 collective-permute-done.3.panels_ref
  18.1 0.0 copy-done.1
  18.1 0.0 copy-done.2
  18.1 2.2 %swapped_panels.1 = f32[10,8,8,401]{3,2,1,0:T(8,128)} custom-call(s32[1,10]{1,0:T(1,128)S(1)} %copy-done.2, bf16[2,16,1280]{2,1,0:T(8,128)(2,1)S(1)} %bitcast.10, bf16[5,16,1280]{2,1,0:T(8,128)(2,1)S(1)} %collective-permute-done.3.panels_ref, bf16[1280,512]{1,0:T(8,128)(2,1)S(1)} %copy-done, f32[10,8,8,401]{3,2,1,0:T(8,128)S(1)} %bitcast.11, ...), custom_call_target="tpu_custom_call" | custom-call | flops 335544320 | bytes 524288 | tf_op jit(solution)/shard_map/swapped_panels/pallas_call | solution.py:376
  (1 shorter events, 0.0 us)
Async XLA Ops:
  0.0 10.5 %copy-start = (bf16[1280,512]{1,0:T(8,128)(2,1)S(1)}, bf16[1280,512]{1,0:T(8,128)(2,1)}, u32[]{:S(2)}) copy-start(bf16[1280,512]{1,0:T(8,128)(2,1)} %constant.5.clone.table_ref) | copy-start | bytes 3932164
  6.0 9.4 %collective-permute-start.1 = (bf16[2,16,1280]{2,1,0:T(8,128)(2,1)S(1)}, bf16[2,16,1280]{2,1,0:T(8,128)(2,1)S(1)}, u32[]{:S(2)}, u32[]{:S(2)}) collective-permute-start(bf16[2,16,1280]{2,1,0:T(8,128)(2,1)S(1)} %bitcast.5), channel_id=1, source_target_pairs={{14,0},{7,1},{8,2},{5,3},{2,4},{11,5},{12,6},{9,7},{6,8},{15,9},{0... | collective-permute-start | bytes 245768 | tf_op jit(solution)/shard_map/ppermute | solution.py:402
  7.1 8.3 %collective-permute-start = (bf16[2,16,1280]{2,1,0:T(8,128)(2,1)S(1)}, bf16[2,16,1280]{2,1,0:T(8,128)(2,1)S(1)}, u32[]{:S(2)}, u32[]{:S(2)}) collective-permute-start(bf16[2,16,1280]{2,1,0:T(8,128)(2,1)S(1)} %bitcast.6), channel_id=1, source_target_pairs={{2,0},{5,1},{0,2},{7,3},{6,4},{9,5},{4,6},{11,7},{10,8},{13,9},{8,... | collective-permute-start | bytes 245768 | tf_op jit(solution)/shard_map/ppermute | solution.py:402
  7.3 8.1 %collective-permute-start.2 = (bf16[16,1280]{1,0:T(8,128)(2,1)}, bf16[16,1280]{1,0:T(8,128)(2,1)S(1)}, u32[]{:S(2)}, u32[]{:S(2)}) collective-permute-start(bf16[16,1280]{1,0:T(8,128)(2,1)} %whiten.1), channel_id=1, source_target_pairs={{8,0},{9,1},{10,2},{11,3},{12,4},{13,5},{14,6},{15,7},{0,8},{1,9},... | collective-permute-start | bytes 122888 | tf_op jit(solution)/shard_map/ppermute | solution.py:402
  15.4 2.7 %copy-start.1 = (f32[1,10,8,8,401]{4,3,2,1,0:T(8,128)S(1)}, f32[1,10,8,8,401]{4,3,2,1,0:T(8,128)}, u32[]{:S(2)}) copy-start(f32[1,10,8,8,401]{4,3,2,1,0:T(8,128)} %param.9) | copy-start | bytes 3079684
  15.4 2.7 %copy-start.2 = (s32[1,10]{1,0:T(1,128)S(1)}, s32[1,10]{1,0:T(1,128)}, u32[]{:S(2)}) copy-start(s32[1,10]{1,0:T(1,128)} %slots_ref.1) | copy-start | bytes 124
  15.5 2.7 %collective-permute-start.3 = (bf16[5,16,1280]{2,1,0:T(8,128)(2,1)S(1)}, bf16[5,16,1280]{2,1,0:T(8,128)(2,1)S(1)}, u32[]{:S(2)}, u32[]{:S(2)}) collective-permute-start(bf16[5,16,1280]{2,1,0:T(8,128)(2,1)S(1)} %pad_maximum_fusion.panels_ref), channel_id=1, source_target_pairs={{1,0},{0,1},{3,2},{2,3},{5,4},{4,5},{7,6},{6,7},{9,8},{8,9},{11,10... | collective-permute-start | bytes 614408 | tf_op jit(solution)/shard_map/ppermute | solution.py:412

commit v6 on v5

--- a/solution.py
+++ b/solution.py
@@ -278,24 +278,24 @@
 
 def pair_panels(panel_count):
     me, chip, core, odd = place(panel_count)
-    return [(0, 2 * chip, True), (1, 2 * chip + 1, True)]
+    return [(0, me, True), (1, me + 1 - 2 * core, True)]
 
 
 def near_panels(panel_count):
     me, chip, core, odd = place(panel_count)
     a, b = first_hop(panel_count)
-    return [(0, 2 * a, True), (1, 2 * a + 1, True), (2, 2 * b, True), (3, 2 * b + 1, True), (4, me + 8, True)]
+    pairs = [(2 * i + t, 2 * c + (core if t == 0 else 1 - core), True) for i, c in enumerate((a, b)) for t in range(2)]
+    return pairs + [(4, me + 8, True)]
 
 
 def swapped_panels(panel_count):
     me, chip, core, odd = place(panel_count)
-    low = 2 * odd * core
     found = []
     for t in range(2):
         ahead = jnp.where(core == 0, chip + 2, chip + 1 + 2 * odd)
-        found.append((low + t, 2 * ahead + t, True))
+        found.append((2 * odd * core + t, 2 * ahead + (1 - core if t == 0 else core), True))
     for t in range(2):
-        ahead = 2 * (chip + 3 - 2 * odd) + t
+        ahead = 2 * (chip + 3 - 2 * odd) + 1 - t
         found.append((jnp.where(core == 0, 2 + t, 4), jnp.where(core == 0, ahead, 2 * chip + 8), (core == 0) | (t == 0)))
     return found
 
@@ -313,7 +313,7 @@
 
 
 def early_kernel(panel_count, which, pair_ref, panels_ref, table_ref, out_ref, cross):
-    own = pair_ref[lax.rem(lax.axis_index("row"), 2)].astype(jnp.float32)
+    own = pair_ref[0].astype(jnp.float32)
 
     def keep(start, corr):
         out_ref[start : start + corr.shape[0]] = corr
@@ -358,7 +358,7 @@
 
     for which, done in zip(lists, done_refs):
         finish(which(panel_count), done)
-    own = pair_ref[lax.rem(me, 2)].astype(jnp.float32)
+    own = pair_ref[0].astype(jnp.float32)
     found = lists[-1](panel_count)
 
     def keep(start, corr):
@@ -391,7 +391,8 @@
 
 def gather_near(own, slots, stack, panel_count):
     chips = panel_count // 2
-    pair = lax.all_gather(own, "row", axis=0, axis_index_groups=[[2 * c, 2 * c + 1] for c in range(chips)])
+    def swap(array):
+        return lax.ppermute(array, "row", [(i ^ 1, i) for i in range(panel_count)])
 
     def fetch(array, even, odd):
         ahead = [even, odd]
@@ -402,6 +403,8 @@
         return lax.ppermute(array, "row", moves)
 
     table = jnp.asarray(lag_table())
+    twice = jnp.stack([own, own])
+    pair, own = lax.optimization_barrier((lax.dynamic_update_slice(twice, swap(own)[None], (1, 0, 0)), own))
     near = fetch(pair, (1, -1), (2, 2))
     next_near = fetch(pair, (-1, 3), (3, 1))
     far = fetch(own, (4, 4), (4, 4))
@@ -409,7 +412,7 @@
     first = early(pair_panels, 2, panel_count, chans, pair, pair, table)
     near, next_near, far, first = lax.optimization_barrier((near, next_near, far, first))
     five = jnp.concatenate([near, next_near, far[None]], axis=0)
-    swapped = lax.ppermute(five, "row", [(i ^ 1, i) for i in range(panel_count)])
+    swapped = swap(five)
     second = early(near_panels, 5, panel_count, chans, pair, five, table)
     lists = (pair_panels, near_panels, swapped_panels)
     return last(lists, (2, 5, 4), panel_count, slots, pair, swapped, table, stack, first, second)

time: 20.5 us -> 20 us (0.976)
  blocking collectives: 2.4 us -> 0 us
  other arithmetic: 0.03 us -> 0.89 us
  starting transfers between devices: 6.06 us -> 6.8 us
    all_gather x1 -> x0, blocking collectives: 2.4 us -> none  [gather_near(): lax.all_gather(own, 'row', axis=0, axis_index_groups=[[2 * c, 2 * c + 1]...]
    another operation x0 -> x1, other arithmetic: none -> 0.86 us  [gather_near(): twice = jnp.stack([own, own])]
    ppermute x1 -> x2, starting transfers between devices: 1.58 us -> 2.32 us  [swap(): return lax.ppermute(array, 'row', [(i ^ 1, i) for i in range(panel_count)])]
    ppermute x1 -> x2, waiting for transfers between devices: 0.1 us -> 0.32 us  [swap(): return lax.ppermute(array, 'row', [(i ^ 1, i) for i in range(panel_count)])]
  transfers between devices with their start and end apart: 4 -> 5, of which waited for: 2 -> 3; matrix products, arithmetic and copies ran while one was open for 0% -> 4% of each run, Pallas kernels for 7% -> 7%
where the time goes in v6:
time: 20 us; the launch traced here: 19.8 us
  Pallas kernels  7.31 us (37%)
  starting transfers between devices  6.8 us (34%)
  waiting for transfers between devices  4.72 us (24%)
  other arithmetic  0.89 us (4%)
    ppermute x3, starting transfers between devices, fetch(): return lax.ppermute(array, 'row', moves)  4.47 us
    ppermute x3, waiting for transfers between devices, fetch(): return lax.ppermute(array, 'row', moves)  4.4 us
    pallas_call x1, Pallas kernels, whiten(): pl.pallas_call(whiten_kernel, out_shape=jax.ShapeDtypeStruct((rows, 2 * L...  3.61 us
    ppermute x2, starting transfers between devices, swap(): return lax.ppermute(array, 'row', [(i ^ 1, i) for i in range(panel_count)])  2.32 us
    pallas_call x1, Pallas kernels, last(): pl.pallas_call(functools.partial(last_kernel, panel_count, lists), out_sh...  2.24 us
    pallas_call x2, Pallas kernels, early(): pl.pallas_call(functools.partial(early_kernel, panel_count, which), out_s...  1.46 us
    another operation x1, other arithmetic, gather_near(): twice = jnp.stack([own, own])  0.86 us
  transfers between devices with their start and end apart: 5, of which 3 were waited for; matrix products, arithmetic and copies ran while one was open for 4% of the time, Pallas kernels for 7%

profile of v6, /device:TPU:25, one launch (start us, length us, event | category | flops | bytes accessed | tf_op | source)
XLA Modules:
  0.0 19.8 jit_solution(11776615800367370246)
XLA Ops:
  0.0 0.0 copy-start
  0.0 3.6 %whiten.1 = bf16[16,1280]{1,0:T(8,128)(2,1)} custom-call(bf16[8,2,12000]{2,1,0:T(2,128)(2,1)} %x_hbm.1, s32[2,8]{1,0:T(2,128)} %bitcast.10, bf16[600,1280]{1,0:T(8,128)(2,1)} %constant.8.clone.table_hbm), custom_call_target="tpu_custom_call" | custom-call | tf_op jit(solution)/shard_map/whiten/pallas_call | solution.py:187
  3.6 0.7 %collective-permute-start = (bf16[16,1280]{1,0:T(8,128)(2,1)}, bf16[16,1280]{1,0:T(8,128)(2,1)S(1)}, u32[]{:S(2)}, u32[]{:S(2)}) collective-permute-start(bf16[16,1280]{1,0:T(8,128)(2,1)} %whiten.1), channel_id=1, source_target_pairs={{1,0},{0,1},{3,2},{2,3},{5,4},{4,5},{7,6},{6,7},{9,8},{8,9},{11,10... | collective-permute-start | bytes 122888 | tf_op jit(solution)/shard_map/ppermute | solution.py:395
  4.4 0.9 %pad_maximum_fusion.1 = bf16[2,16,1280]{2,1,0:T(8,128)(2,1)S(1)} fusion(bf16[1,16,1280]{2,1,0:T(8,128)(2,1)} %bitcast.8), kind=kLoop, calls=%fused_computation.1 | loop fusion | flops 40960 | bytes 122880 | tf_op jit(solution)/shard_map/stack | solution.py:406
  5.2 0.2 %collective-permute-done = bf16[16,1280]{1,0:T(8,128)(2,1)S(1)} collective-permute-done((bf16[16,1280]{1,0:T(8,128)(2,1)}, bf16[16,1280]{1,0:T(8,128)(2,1)S(1)}, u32[]{:S(2)}, u32[]{:S(2)}) %collective-permute-start) | collective-permute-done | bytes 40992 | tf_op jit(solution)/shard_map/ppermute | solution.py:395
  5.4 1.1 %collective-permute-start.2 = (bf16[2,16,1280]{2,1,0:T(8,128)(2,1)S(1)}, bf16[2,16,1280]{2,1,0:T(8,128)(2,1)S(1)}, u32[]{:S(2)}, u32[]{:S(2)}) collective-permute-start(bf16[2,16,1280]{2,1,0:T(8,128)(2,1)S(1)} %bitcast_dynamic-update-slice_fusion.pair_ref.panels_ref), channel_id=1, source_target_pairs={{14,0},{7,1},{8,2},{5,3},{2,4},{11,5},{12,6},{9,7},{6,8},{15,9},{0... | collective-permute-start | bytes 245768 | tf_op jit(solution)/shard_map/ppermute | solution.py:403
  6.5 0.2 collective-permute-start.1
  6.7 3.2 %collective-permute-start.3 = (bf16[16,1280]{1,0:T(8,128)(2,1)}, bf16[16,1280]{1,0:T(8,128)(2,1)S(1)}, u32[]{:S(2)}, u32[]{:S(2)}) collective-permute-start(bf16[16,1280]{1,0:T(8,128)(2,1)} %whiten.1), channel_id=1, source_target_pairs={{8,0},{9,1},{10,2},{11,3},{12,4},{13,5},{14,6},{15,7},{0,8},{1,9},... | collective-permute-start | bytes 122888 | tf_op jit(solution)/shard_map/ppermute | solution.py:403
  9.9 0.0 copy-done
  9.9 0.5 %pair_panels.1.refs_0_ = f32[2,64,512]{2,1,0:T(8,128)S(1)} custom-call(bf16[2,16,1280]{2,1,0:T(8,128)(2,1)S(1)} %bitcast_dynamic-update-slice_fusion.pair_ref.panels_ref, bf16[2,16,1280]{2,1,0:T(8,128)(2,1)S(1)} %bitcast_dynamic-update-slice_fusion.pair_ref.panels_ref, bf16[1280,512]{1,0:T(8,128)(2,1)S(1)} %copy-done), custom_call_target="tpu_custom_call" | custom-call | flops 167772160 | bytes 262144 | tf_op jit(solution)/shard_map/pair_panels/pallas_call | solution.py:327
  10.4 4.4 %collective-permute-done.3 = bf16[16,1280]{1,0:T(8,128)(2,1)S(1)} collective-permute-done((bf16[16,1280]{1,0:T(8,128)(2,1)}, bf16[16,1280]{1,0:T(8,128)(2,1)S(1)}, u32[]{:S(2)}, u32[]{:S(2)}) %collective-permute-start.3) | collective-permute-done | bytes 40992 | tf_op jit(solution)/shard_map/ppermute | solution.py:403
  14.8 0.0 collective-permute-done.2
  14.8 0.0 collective-permute-done.1
  14.8 0.0 copy-start.1
  14.8 0.0 copy-start.2
  14.9 1.6 %collective-permute-start.4 = (bf16[5,16,1280]{2,1,0:T(8,128)(2,1)S(1)}, bf16[5,16,1280]{2,1,0:T(8,128)(2,1)S(1)}, u32[]{:S(2)}, u32[]{:S(2)}) collective-permute-start(bf16[5,16,1280]{2,1,0:T(8,128)(2,1)S(1)} %pad_maximum_fusion.panels_ref), channel_id=1, source_target_pairs={{1,0},{0,1},{3,2},{2,3},{5,4},{4,5},{7,6},{6,7},{9,8},{8,9},{11,10... | collective-permute-start | bytes 614408 | tf_op jit(solution)/shard_map/ppermute | solution.py:395
  16.5 1.0 %near_panels.1.refs_1_ = f32[5,64,512]{2,1,0:T(8,128)S(1)} custom-call(bf16[2,16,1280]{2,1,0:T(8,128)(2,1)S(1)} %bitcast_dynamic-update-slice_fusion.pair_ref.panels_ref, bf16[5,16,1280]{2,1,0:T(8,128)(2,1)S(1)} %pad_maximum_fusion.panels_ref, bf16[1280,512]{1,0:T(8,128)(2,1)S(1)} %copy-done), custom_call_target="tpu_custom_call" | custom-call | flops 419430400 | bytes 655360 | tf_op jit(solution)/shard_map/near_panels/pallas_call | solution.py:327
  17.4 0.1 collective-permute-done.4.panels_ref
  17.5 0.0 copy-done.1
  17.5 0.0 copy-done.2
  17.5 2.2 %swapped_panels.1 = f32[10,8,8,401]{3,2,1,0:T(8,128)} custom-call(s32[1,10]{1,0:T(1,128)S(1)} %copy-done.2, bf16[2,16,1280]{2,1,0:T(8,128)(2,1)S(1)} %bitcast_dynamic-update-slice_fusion.pair_ref.panels_ref, bf16[5,16,1280]{2,1,0:T(8,128)(2,1)S(1)} %collective-permute-done.4.panels_ref, bf16[1280,512]{1,0:T(8,128)(2,1)S(1)} %copy-done, ...), custom_call_target="tpu_custom_call" | custom-call | flops 335544320 | bytes 524288 | tf_op jit(solution)/shard_map/swapped_panels/pallas_call | solution.py:376
  (2 shorter events, 0.0 us)
Async XLA Ops:
  0.0 9.9 %copy-start = (bf16[1280,512]{1,0:T(8,128)(2,1)S(1)}, bf16[1280,512]{1,0:T(8,128)(2,1)}, u32[]{:S(2)}) copy-start(bf16[1280,512]{1,0:T(8,128)(2,1)} %constant.9.clone.table_ref) | copy-start | bytes 3932164
  3.6 1.8 %collective-permute-start = (bf16[16,1280]{1,0:T(8,128)(2,1)}, bf16[16,1280]{1,0:T(8,128)(2,1)S(1)}, u32[]{:S(2)}, u32[]{:S(2)}) collective-permute-start(bf16[16,1280]{1,0:T(8,128)(2,1)} %whiten.1), channel_id=1, source_target_pairs={{1,0},{0,1},{3,2},{2,3},{5,4},{4,5},{7,6},{6,7},{9,8},{8,9},{11,10... | collective-permute-start | bytes 122888 | tf_op jit(solution)/shard_map/ppermute | solution.py:395
  5.4 9.4 %collective-permute-start.2 = (bf16[2,16,1280]{2,1,0:T(8,128)(2,1)S(1)}, bf16[2,16,1280]{2,1,0:T(8,128)(2,1)S(1)}, u32[]{:S(2)}, u32[]{:S(2)}) collective-permute-start(bf16[2,16,1280]{2,1,0:T(8,128)(2,1)S(1)} %bitcast_dynamic-update-slice_fusion.pair_ref.panels_ref), channel_id=1, source_target_pairs={{14,0},{7,1},{8,2},{5,3},{2,4},{11,5},{12,6},{9,7},{6,8},{15,9},{0... | collective-permute-start | bytes 245768 | tf_op jit(solution)/shard_map/ppermute | solution.py:403
  6.5 8.3 %collective-permute-start.1 = (bf16[2,16,1280]{2,1,0:T(8,128)(2,1)S(1)}, bf16[2,16,1280]{2,1,0:T(8,128)(2,1)S(1)}, u32[]{:S(2)}, u32[]{:S(2)}) collective-permute-start(bf16[2,16,1280]{2,1,0:T(8,128)(2,1)S(1)} %bitcast_dynamic-update-slice_fusion.pair_ref.panels_ref), channel_id=1, source_target_pairs={{2,0},{5,1},{0,2},{7,3},{6,4},{9,5},{4,6},{11,7},{10,8},{13,9},{8,... | collective-permute-start | bytes 245768 | tf_op jit(solution)/shard_map/ppermute | solution.py:403
  6.7 8.1 %collective-permute-start.3 = (bf16[16,1280]{1,0:T(8,128)(2,1)}, bf16[16,1280]{1,0:T(8,128)(2,1)S(1)}, u32[]{:S(2)}, u32[]{:S(2)}) collective-permute-start(bf16[16,1280]{1,0:T(8,128)(2,1)} %whiten.1), channel_id=1, source_target_pairs={{8,0},{9,1},{10,2},{11,3},{12,4},{13,5},{14,6},{15,7},{0,8},{1,9},... | collective-permute-start | bytes 122888 | tf_op jit(solution)/shard_map/ppermute | solution.py:403
  14.8 2.7 %copy-start.1 = (f32[1,10,8,8,401]{4,3,2,1,0:T(8,128)S(1)}, f32[1,10,8,8,401]{4,3,2,1,0:T(8,128)}, u32[]{:S(2)}) copy-start(f32[1,10,8,8,401]{4,3,2,1,0:T(8,128)} %param.9) | copy-start | bytes 3079684
  14.8 2.7 %copy-start.2 = (s32[1,10]{1,0:T(1,128)S(1)}, s32[1,10]{1,0:T(1,128)}, u32[]{:S(2)}) copy-start(s32[1,10]{1,0:T(1,128)} %slots_ref.1) | copy-start | bytes 124
  14.9 2.7 %collective-permute-start.4 = (bf16[5,16,1280]{2,1,0:T(8,128)(2,1)S(1)}, bf16[5,16,1280]{2,1,0:T(8,128)(2,1)S(1)}, u32[]{:S(2)}, u32[]{:S(2)}) collective-permute-start(bf16[5,16,1280]{2,1,0:T(8,128)(2,1)S(1)} %pad_maximum_fusion.panels_ref), channel_id=1, source_target_pairs={{1,0},{0,1},{3,2},{2,3},{5,4},{4,5},{7,6},{6,7},{9,8},{8,9},{11,10... | collective-permute-start | bytes 614408 | tf_op jit(solution)/shard_map/ppermute | solution.py:395

commit v7 on v6

--- a/solution.py
+++ b/solution.py
@@ -77,10 +77,10 @@
     e14, e23, f14, f23 = e[1] + e[4], e[2] + e[3], e[1] - e[4], e[2] - e[3]
     d14, d23, g14, g23 = d[1] + d[4], d[2] + d[3], d[1] - d[4], d[2] - d[3]
     y0 = (e[0] + e14 + e23, None)
-    y2 = (e[0] + c2 * e14 - c1 * e23, -(s2 * f14 + s1 * f23))
-    y4 = (e[0] - c1 * e14 + c2 * e23, -(s1 * f14 - s2 * f23))
-    y1 = (d[0] + c1 * g14 + c2 * g23, -(s1 * d14 + s2 * d23))
-    y3 = (d[0] - c2 * g14 - c1 * g23, -(s2 * d14 - s1 * d23))
+    y2 = (e[0] + c2 * e14 - c1 * e23, s2 * f14 + s1 * f23)
+    y4 = (e[0] - c1 * e14 + c2 * e23, s1 * f14 - s2 * f23)
+    y1 = (d[0] + c1 * g14 + c2 * g23, s1 * d14 + s2 * d23)
+    y3 = (d[0] - c2 * g14 - c1 * g23, s2 * d14 - s1 * d23)
     y5 = (d[0] - g14 + g23, None)
     return [y0, y1, y2, y3, y4, y5]
 
@@ -89,14 +89,16 @@
     y = [None] * 11
     y[0::2] = ten_point([s[n] + s[n + 10] for n in range(10)])
     d = [s[n] - s[n + 10] for n in range(10)]
-    g = [d[n] - d[10 - n] for n in range(1, 5)]
-    h = [d[n] + d[10 - n] for n in range(1, 5)]
-    for k in (1, 3, 5, 7, 9):
-        real, imag = d[0], -sine(5 * k, 20) * d[5]
-        for n in range(1, 5):
-            real = real + cosine(n * k % 20, 20) * g[n - 1]
-            imag = imag - sine(n * k % 20, 20) * h[n - 1]
-        y[k] = (real, imag)
+    g1, g2, g3, g4 = (d[n] - d[10 - n] for n in range(1, 5))
+    h1, h2, h3, h4 = (d[n] + d[10 - n] for n in range(1, 5))
+    for k, turn in ((1, d[5]), (3, -d[5])):
+        even = d[0] + cosine(2 * k, 20) * g2 + cosine(4 * k, 20) * g4
+        odd = cosine(k, 20) * g1 + cosine(3 * k, 20) * g3
+        even_sin = sine(2 * k, 20) * h2 + sine(4 * k, 20) * h4
+        odd_sin = sine(k, 20) * h1 + sine(3 * k, 20) * h3 + turn
+        y[k] = (even + odd, odd_sin + even_sin)
+        y[10 - k] = (even - odd, odd_sin - even_sin)
+    y[5] = (d[0] - g2 + g4, h1 - h3 + d[5])
     return y
 
 
@@ -140,11 +142,12 @@
     for part, groups in enumerate(GROUPS):
         wanted = sorted({min(k, SPLIT - k) for g in groups for k in range(g, SPLIT, 5)})
         pieces = [(k, i) for k in wanted for i in range(2) if y[k][i] is not None]
-        left = jnp.concatenate([p for k, i in pieces for p in hi_lo(y[k][i])], axis=0)
+        halves = [hi_lo(y[k][i]) for k, i in pieces]
+        left = jnp.concatenate([half[j] for j in range(2) for half in halves], axis=0)
         at = starts[part]
         full = jnp.dot(left, table[:, at : starts[part + 1]], preferred_element_type=jnp.float32)
         got = {
-            p: full[2 * rows * i : 2 * rows * i + rows] + full[2 * rows * i + rows : 2 * rows * (i + 1)]
+            p: full[rows * i : rows * (i + 1)] + full[rows * (len(pieces) + i) : rows * (len(pieces) + i + 1)]
             for i, p in enumerate(pieces)
         }
         for place, group in enumerate(groups):
@@ -157,8 +160,11 @@
                 a = got[(same, 0)]
                 r, i = a[:, cos], a[:, sin]
                 if (same, 1) in got:
-                    b = got[(same, 1)] if k == same else -got[(same, 1)]
-                    r, i = r - b[:, sin], i + b[:, cos]
+                    b = got[(same, 1)]
+                    if k == same:
+                        r, i = r + b[:, sin], i - b[:, cos]
+                    else:
+                        r, i = r - b[:, sin], i + b[:, cos]
                 re = r if re is None else jnp.where(run == q, r, re)
                 im = i if im is None else jnp.where(run == q, i, im)
             real[group], imag[group] = re, im
@@ -336,11 +342,14 @@
     )(pair, panels, table)
 
 
-def last_kernel(panel_count, lists, slots_ref, pair_ref, panels_ref, table_ref, stack_ref, *refs):
+def last_kernel(panel_count, lists, slots_any, pair_ref, panels_ref, table_ref, stack_ref, *refs):
     done_refs = refs[: len(lists) - 1]
-    out_ref, cross, result, sem = refs[len(lists) - 1 :]
+    out_ref, slots_ref, cross, result, sem = refs[len(lists) - 1 :]
     offsets, chans = stack_ref.shape[0], stack_ref.shape[1]
+    fetch_slots = pltpu.make_async_copy(slots_any, slots_ref, sem.at[sem.shape[0] - 1])
+    fetch_slots.start()
     me = lax.axis_index("row")
+    own = pair_ref[0].astype(jnp.float32)
     copies = []
 
     def finish(found, corr):
@@ -356,12 +365,13 @@
             copies.append((valid, copy))
             pl.when(valid)(copy.start)
 
-    for which, done in zip(lists, done_refs):
-        finish(which(panel_count), done)
-    own = pair_ref[0].astype(jnp.float32)
     found = lists[-1](panel_count)
 
     def keep(start, corr):
+        if start == 0:
+            fetch_slots.wait()
+            for which, done in zip(lists, done_refs):
+                finish(which(panel_count), done)
         finish(found[start : start + corr.shape[0]], corr)
 
     products(lists[-1], panel_count, own, panels_ref, table_ref[...], chans, cross, keep)
@@ -376,12 +386,13 @@
     return pl.pallas_call(
         functools.partial(last_kernel, panel_count, lists),
         out_shape=jax.ShapeDtypeStruct(stack.shape, jnp.float32),
-        in_specs=[pl.BlockSpec(memory_space=pltpu.SMEM)] + [whole] * (4 + len(done)),
+        in_specs=[pl.BlockSpec(memory_space=pl.ANY)] + [whole] * (4 + len(done)),
         out_specs=pl.BlockSpec(memory_space=pltpu.HBM),
         scratch_shapes=[
+            pltpu.SMEM(slots.shape, jnp.int32),
             pltpu.VMEM((rows, 2 * LANES), jnp.bfloat16),
             pltpu.VMEM((sum(counts), chans, chans, LAGS), jnp.float32),
-            pltpu.SemaphoreType.DMA((sum(counts),)),
+            pltpu.SemaphoreType.DMA((sum(counts) + 1,)),
         ],
         compiler_params=pltpu.CompilerParams(vmem_limit_bytes=CORR_VMEM),
         cost_estimate=pl.CostEstimate(flops=4 * rows * LANES * COLS, bytes_accessed=4 * rows * COLS, transcendentals=0),

time: 20 us -> 19.7 us (0.985)
  Pallas kernels: 7.31 us -> 7.04 us
    pallas_call x1, Pallas kernels: 3.61 us -> 3.38 us  [whiten(): pl.pallas_call(whiten_kernel, out_shape=jax.ShapeDtypeStruct((rows, 2 * L...]
where the time goes in v7:
time: 19.7 us; the launch traced here: 19.5 us
  Pallas kernels  7.04 us (36%)
  starting transfers between devices  6.8 us (35%)
  waiting for transfers between devices  4.73 us (24%)
  other arithmetic  0.89 us (5%)
    ppermute x3, starting transfers between devices, fetch(): return lax.ppermute(array, 'row', moves)  4.48 us
    ppermute x3, waiting for transfers between devices, fetch(): return lax.ppermute(array, 'row', moves)  4.4 us
    pallas_call x1, Pallas kernels, whiten(): pl.pallas_call(whiten_kernel, out_shape=jax.ShapeDtypeStruct((rows, 2 * L...  3.38 us
    ppermute x2, starting transfers between devices, swap(): return lax.ppermute(array, 'row', [(i ^ 1, i) for i in range(panel_count)])  2.32 us
    pallas_call x1, Pallas kernels, last(): pl.pallas_call(functools.partial(last_kernel, panel_count, lists), out_sh...  2.21 us
    pallas_call x2, Pallas kernels, early(): pl.pallas_call(functools.partial(early_kernel, panel_count, which), out_s...  1.45 us
    another operation x1, other arithmetic, gather_near(): twice = jnp.stack([own, own])  0.86 us
  transfers between devices with their start and end apart: 5, of which 3 were waited for; matrix products, arithmetic and copies ran while one was open for 4% of the time, Pallas kernels for 7%

profile of v7, /device:TPU:25, one launch (start us, length us, event | category | flops | bytes accessed | tf_op | source)
XLA Modules:
  0.0 19.5 jit_solution(9836963730508650612)
XLA Ops:
  0.0 0.0 copy-start
  0.0 3.4 %whiten.1 = bf16[16,1280]{1,0:T(8,128)(2,1)} custom-call(bf16[8,2,12000]{2,1,0:T(2,128)(2,1)} %x_hbm.1, s32[2,8]{1,0:T(2,128)} %bitcast.10, bf16[600,1280]{1,0:T(8,128)(2,1)} %constant.8.clone.table_hbm), custom_call_target="tpu_custom_call" | custom-call | tf_op jit(solution)/shard_map/whiten/pallas_call | solution.py:193
  3.4 0.7 %collective-permute-start = (bf16[16,1280]{1,0:T(8,128)(2,1)}, bf16[16,1280]{1,0:T(8,128)(2,1)S(1)}, u32[]{:S(2)}, u32[]{:S(2)}) collective-permute-start(bf16[16,1280]{1,0:T(8,128)(2,1)} %whiten.1), channel_id=1, source_target_pairs={{1,0},{0,1},{3,2},{2,3},{5,4},{4,5},{7,6},{6,7},{9,8},{8,9},{11,10... | collective-permute-start | bytes 122888 | tf_op jit(solution)/shard_map/ppermute | solution.py:406
  4.1 0.9 %pad_maximum_fusion.1 = bf16[2,16,1280]{2,1,0:T(8,128)(2,1)S(1)} fusion(bf16[1,16,1280]{2,1,0:T(8,128)(2,1)} %bitcast.8), kind=kLoop, calls=%fused_computation.1 | loop fusion | flops 40960 | bytes 122880 | tf_op jit(solution)/shard_map/stack | solution.py:417
  5.0 0.2 %collective-permute-done = bf16[16,1280]{1,0:T(8,128)(2,1)S(1)} collective-permute-done((bf16[16,1280]{1,0:T(8,128)(2,1)}, bf16[16,1280]{1,0:T(8,128)(2,1)S(1)}, u32[]{:S(2)}, u32[]{:S(2)}) %collective-permute-start) | collective-permute-done | bytes 40992 | tf_op jit(solution)/shard_map/ppermute | solution.py:406
  5.2 1.1 %collective-permute-start.2 = (bf16[2,16,1280]{2,1,0:T(8,128)(2,1)S(1)}, bf16[2,16,1280]{2,1,0:T(8,128)(2,1)S(1)}, u32[]{:S(2)}, u32[]{:S(2)}) collective-permute-start(bf16[2,16,1280]{2,1,0:T(8,128)(2,1)S(1)} %bitcast_dynamic-update-slice_fusion.pair_ref.panels_ref), channel_id=1, source_target_pairs={{14,0},{7,1},{8,2},{5,3},{2,4},{11,5},{12,6},{9,7},{6,8},{15,9},{0... | collective-permute-start | bytes 245768 | tf_op jit(solution)/shard_map/ppermute | solution.py:414
  6.3 0.2 collective-permute-start.1
  6.5 3.2 %collective-permute-start.3 = (bf16[16,1280]{1,0:T(8,128)(2,1)}, bf16[16,1280]{1,0:T(8,128)(2,1)S(1)}, u32[]{:S(2)}, u32[]{:S(2)}) collective-permute-start(bf16[16,1280]{1,0:T(8,128)(2,1)} %whiten.1), channel_id=1, source_target_pairs={{8,0},{9,1},{10,2},{11,3},{12,4},{13,5},{14,6},{15,7},{0,8},{1,9},... | collective-permute-start | bytes 122888 | tf_op jit(solution)/shard_map/ppermute | solution.py:414
  9.7 0.0 copy-done
  9.7 0.5 %pair_panels.1.refs_0_ = f32[2,64,512]{2,1,0:T(8,128)S(1)} custom-call(bf16[2,16,1280]{2,1,0:T(8,128)(2,1)S(1)} %bitcast_dynamic-update-slice_fusion.pair_ref.panels_ref, bf16[2,16,1280]{2,1,0:T(8,128)(2,1)S(1)} %bitcast_dynamic-update-slice_fusion.pair_ref.panels_ref, bf16[1280,512]{1,0:T(8,128)(2,1)S(1)} %copy-done), custom_call_target="tpu_custom_call" | custom-call | flops 167772160 | bytes 262144 | tf_op jit(solution)/shard_map/pair_panels/pallas_call | solution.py:333
  10.2 4.4 %collective-permute-done.3 = bf16[16,1280]{1,0:T(8,128)(2,1)S(1)} collective-permute-done((bf16[16,1280]{1,0:T(8,128)(2,1)}, bf16[16,1280]{1,0:T(8,128)(2,1)S(1)}, u32[]{:S(2)}, u32[]{:S(2)}) %collective-permute-start.3) | collective-permute-done | bytes 40992 | tf_op jit(solution)/shard_map/ppermute | solution.py:414
  14.6 0.0 collective-permute-done.2
  14.6 0.0 collective-permute-done.1
  14.6 0.0 copy-start.1
  14.6 0.0 copy-start.2
  14.6 1.6 %collective-permute-start.4 = (bf16[5,16,1280]{2,1,0:T(8,128)(2,1)S(1)}, bf16[5,16,1280]{2,1,0:T(8,128)(2,1)S(1)}, u32[]{:S(2)}, u32[]{:S(2)}) collective-permute-start(bf16[5,16,1280]{2,1,0:T(8,128)(2,1)S(1)} %pad_maximum_fusion.panels_ref), channel_id=1, source_target_pairs={{1,0},{0,1},{3,2},{2,3},{5,4},{4,5},{7,6},{6,7},{9,8},{8,9},{11,10... | collective-permute-start | bytes 614408 | tf_op jit(solution)/shard_map/ppermute | solution.py:406
  16.2 1.0 %near_panels.1.refs_1_ = f32[5,64,512]{2,1,0:T(8,128)S(1)} custom-call(bf16[2,16,1280]{2,1,0:T(8,128)(2,1)S(1)} %bitcast_dynamic-update-slice_fusion.pair_ref.panels_ref, bf16[5,16,1280]{2,1,0:T(8,128)(2,1)S(1)} %pad_maximum_fusion.panels_ref, bf16[1280,512]{1,0:T(8,128)(2,1)S(1)} %copy-done), custom_call_target="tpu_custom_call" | custom-call | flops 419430400 | bytes 655360 | tf_op jit(solution)/shard_map/near_panels/pallas_call | solution.py:333
  17.2 0.1 collective-permute-done.4.panels_ref
  17.3 0.0 copy-done.1
  17.3 0.0 copy-done.2
  17.3 2.2 %swapped_panels.1 = f32[10,8,8,401]{3,2,1,0:T(8,128)} custom-call(s32[1,10]{1,0:T(1,128)S(1)} %copy-done.2, bf16[2,16,1280]{2,1,0:T(8,128)(2,1)S(1)} %bitcast_dynamic-update-slice_fusion.pair_ref.panels_ref, bf16[5,16,1280]{2,1,0:T(8,128)(2,1)S(1)} %collective-permute-done.4.panels_ref, bf16[1280,512]{1,0:T(8,128)(2,1)S(1)} %copy-done, ...), custom_call_target="tpu_custom_call" | custom-call | flops 335544320 | bytes 524288 | tf_op jit(solution)/shard_map/swapped_panels/pallas_call | solution.py:386
  (2 shorter events, 0.0 us)
Async XLA Ops:
  0.0 9.7 %copy-start = (bf16[1280,512]{1,0:T(8,128)(2,1)S(1)}, bf16[1280,512]{1,0:T(8,128)(2,1)}, u32[]{:S(2)}) copy-start(bf16[1280,512]{1,0:T(8,128)(2,1)} %constant.9.clone.table_ref) | copy-start | bytes 3932164
  3.4 1.8 %collective-permute-start = (bf16[16,1280]{1,0:T(8,128)(2,1)}, bf16[16,1280]{1,0:T(8,128)(2,1)S(1)}, u32[]{:S(2)}, u32[]{:S(2)}) collective-permute-start(bf16[16,1280]{1,0:T(8,128)(2,1)} %whiten.1), channel_id=1, source_target_pairs={{1,0},{0,1},{3,2},{2,3},{5,4},{4,5},{7,6},{6,7},{9,8},{8,9},{11,10... | collective-permute-start | bytes 122888 | tf_op jit(solution)/shard_map/ppermute | solution.py:406
  5.2 9.4 %collective-permute-start.2 = (bf16[2,16,1280]{2,1,0:T(8,128)(2,1)S(1)}, bf16[2,16,1280]{2,1,0:T(8,128)(2,1)S(1)}, u32[]{:S(2)}, u32[]{:S(2)}) collective-permute-start(bf16[2,16,1280]{2,1,0:T(8,128)(2,1)S(1)} %bitcast_dynamic-update-slice_fusion.pair_ref.panels_ref), channel_id=1, source_target_pairs={{14,0},{7,1},{8,2},{5,3},{2,4},{11,5},{12,6},{9,7},{6,8},{15,9},{0... | collective-permute-start | bytes 245768 | tf_op jit(solution)/shard_map/ppermute | solution.py:414
  6.3 8.3 %collective-permute-start.1 = (bf16[2,16,1280]{2,1,0:T(8,128)(2,1)S(1)}, bf16[2,16,1280]{2,1,0:T(8,128)(2,1)S(1)}, u32[]{:S(2)}, u32[]{:S(2)}) collective-permute-start(bf16[2,16,1280]{2,1,0:T(8,128)(2,1)S(1)} %bitcast_dynamic-update-slice_fusion.pair_ref.panels_ref), channel_id=1, source_target_pairs={{2,0},{5,1},{0,2},{7,3},{6,4},{9,5},{4,6},{11,7},{10,8},{13,9},{8,... | collective-permute-start | bytes 245768 | tf_op jit(solution)/shard_map/ppermute | solution.py:414
  6.5 8.1 %collective-permute-start.3 = (bf16[16,1280]{1,0:T(8,128)(2,1)}, bf16[16,1280]{1,0:T(8,128)(2,1)S(1)}, u32[]{:S(2)}, u32[]{:S(2)}) collective-permute-start(bf16[16,1280]{1,0:T(8,128)(2,1)} %whiten.1), channel_id=1, source_target_pairs={{8,0},{9,1},{10,2},{11,3},{12,4},{13,5},{14,6},{15,7},{0,8},{1,9},... | collective-permute-start | bytes 122888 | tf_op jit(solution)/shard_map/ppermute | solution.py:414
  14.6 2.7 %copy-start.1 = (f32[1,10,8,8,401]{4,3,2,1,0:T(8,128)S(1)}, f32[1,10,8,8,401]{4,3,2,1,0:T(8,128)}, u32[]{:S(2)}) copy-start(f32[1,10,8,8,401]{4,3,2,1,0:T(8,128)} %param.9) | copy-start | bytes 3079684
  14.6 2.7 %copy-start.2 = (s32[1,10]{1,0:T(1,128)S(1)}, s32[1,10]{1,0:T(1,128)}, u32[]{:S(2)}) copy-start(s32[1,10]{1,0:T(1,128)} %slots_any.1) | copy-start | bytes 124
  14.6 2.7 %collective-permute-start.4 = (bf16[5,16,1280]{2,1,0:T(8,128)(2,1)S(1)}, bf16[5,16,1280]{2,1,0:T(8,128)(2,1)S(1)}, u32[]{:S(2)}, u32[]{:S(2)}) collective-permute-start(bf16[5,16,1280]{2,1,0:T(8,128)(2,1)S(1)} %pad_maximum_fusion.panels_ref), channel_id=1, source_target_pairs={{1,0},{0,1},{3,2},{2,3},{5,4},{4,5},{7,6},{6,7},{9,8},{8,9},{11,10... | collective-permute-start | bytes 614408 | tf_op jit(solution)/shard_map/ppermute | solution.py:406

commit v8 on v7

--- a/solution.py
+++ b/solution.py
@@ -291,6 +291,8 @@
     me, chip, core, odd = place(panel_count)
     a, b = first_hop(panel_count)
     pairs = [(2 * i + t, 2 * c + (core if t == 0 else 1 - core), True) for i, c in enumerate((a, b)) for t in range(2)]
+    for i, here in ((0, odd == 1), (2, odd == 0)):
+        pairs[i] = (i, pairs[i][1], (core == 1) | jnp.logical_not(here))
     return pairs + [(4, me + 8, True)]
 
 
@@ -302,7 +304,8 @@
         found.append((2 * odd * core + t, 2 * ahead + (1 - core if t == 0 else core), True))
     for t in range(2):
         ahead = 2 * (chip + 3 - 2 * odd) + 1 - t
-        found.append((jnp.where(core == 0, 2 + t, 4), jnp.where(core == 0, ahead, 2 * chip + 8), (core == 0) | (t == 0)))
+        wanted = True if t == 0 else core == 0
+        found.append((jnp.where(core == 0, 2 + t, 4), jnp.where(core == 0, ahead, 2 * chip + 8), wanted))
     return found
 
 
@@ -348,22 +351,26 @@
     offsets, chans = stack_ref.shape[0], stack_ref.shape[1]
     fetch_slots = pltpu.make_async_copy(slots_any, slots_ref, sem.at[sem.shape[0] - 1])
     fetch_slots.start()
-    me = lax.axis_index("row")
     own = pair_ref[0].astype(jnp.float32)
     copies = []
+
+    def only(wanted, act):
+        if wanted is True:
+            act()
+        else:
+            pl.when(wanted)(act)
 
     def finish(found, corr):
         for j, (at, panel, wanted) in enumerate(found):
             panel = lax.rem(panel + panel_count, panel_count)
-            valid = (lax.rem(panel - me + 1 + panel_count, panel_count) < offsets) & wanted
             slot = jnp.int32(0)
             for o in range(1, offsets):
                 slot = jnp.where(slots_ref[0, o] == panel, o, slot)
             n = len(copies)
             result[n] = stack_ref[slot] + corr[j][:, :LAGS].reshape(chans, chans, LAGS)
             copy = pltpu.make_async_copy(result.at[n], out_ref.at[slot], sem.at[n])
-            copies.append((valid, copy))
-            pl.when(valid)(copy.start)
+            copies.append((wanted, copy))
+            only(wanted, copy.start)
 
     found = lists[-1](panel_count)
 
@@ -375,8 +382,8 @@
         finish(found[start : start + corr.shape[0]], corr)
 
     products(lists[-1], panel_count, own, panels_ref, table_ref[...], chans, cross, keep)
-    for valid, copy in copies:
-        pl.when(valid)(copy.wait)
+    for wanted, copy in copies:
+        only(wanted, copy.wait)
 
 
 def last(lists, counts, panel_count, slots, pair, panels, table, stack, *done):
@@ -386,7 +393,7 @@
     return pl.pallas_call(
         functools.partial(last_kernel, panel_count, lists),
         out_shape=jax.ShapeDtypeStruct(stack.shape, jnp.float32),
-        in_specs=[pl.BlockSpec(memory_space=pl.ANY)] + [whole] * (4 + len(done)),
+        in_specs=[whole] * (5 + len(done)),
         out_specs=pl.BlockSpec(memory_space=pltpu.HBM),
         scratch_shapes=[
             pltpu.SMEM(slots.shape, jnp.int32),
@@ -415,10 +422,10 @@
 
     table = jnp.asarray(lag_table())
     twice = jnp.stack([own, own])
-    pair, own = lax.optimization_barrier((lax.dynamic_update_slice(twice, swap(own)[None], (1, 0, 0)), own))
+    pair = lax.optimization_barrier(lax.dynamic_update_slice(twice, swap(own)[None], (1, 0, 0)))
     near = fetch(pair, (1, -1), (2, 2))
     next_near = fetch(pair, (-1, 3), (3, 1))
-    far = fetch(own, (4, 4), (4, 4))
+    far = fetch(pair[0], (4, 4), (4, 4))
     chans = stack.shape[1]
     first = early(pair_panels, 2, panel_count, chans, pair, pair, table)
     near, next_near, far, first = lax.optimization_barrier((near, next_near, far, first))

time: 19.7 us -> 19.7 us (level)
  no operation moved by 1% of the time
where the time goes in v8:
time: 19.7 us; the launch traced here: 19.5 us
  Pallas kernels  7.03 us (36%)
  starting transfers between devices  6.82 us (35%)
  waiting for transfers between devices  4.7 us (24%)
  other arithmetic  0.89 us (5%)
    ppermute x3, starting transfers between devices, fetch(): return lax.ppermute(array, 'row', moves)  4.48 us
    ppermute x3, waiting for transfers between devices, fetch(): return lax.ppermute(array, 'row', moves)  4.37 us
    pallas_call x1, Pallas kernels, whiten(): pl.pallas_call(whiten_kernel, out_shape=jax.ShapeDtypeStruct((rows, 2 * L...  3.38 us
    ppermute x2, starting transfers between devices, swap(): return lax.ppermute(array, 'row', [(i ^ 1, i) for i in range(panel_count)])  2.34 us
    pallas_call x1, Pallas kernels, last(): pl.pallas_call(functools.partial(last_kernel, panel_count, lists), out_sh...  2.2 us
    pallas_call x2, Pallas kernels, early(): pl.pallas_call(functools.partial(early_kernel, panel_count, which), out_s...  1.46 us
    another operation x1, other arithmetic, gather_near(): twice = jnp.stack([own, own])  0.86 us
  transfers between devices with their start and end apart: 5, of which 3 were waited for; matrix products, arithmetic and copies ran while one was open for 4% of the time, Pallas kernels for 7%

profile of v8, /device:TPU:25, one launch (start us, length us, event | category | flops | bytes accessed | tf_op | source)
XLA Modules:
  0.0 19.5 jit_solution(12876144250163824420)
XLA Ops:
  0.0 0.0 copy-start
  0.0 3.4 %whiten.1 = bf16[16,1280]{1,0:T(8,128)(2,1)} custom-call(bf16[8,2,12000]{2,1,0:T(2,128)(2,1)} %x_hbm.1, s32[2,8]{1,0:T(2,128)} %bitcast.12, bf16[600,1280]{1,0:T(8,128)(2,1)} %constant.8.clone.table_hbm), custom_call_target="tpu_custom_call" | custom-call | tf_op jit(solution)/shard_map/whiten/pallas_call | solution.py:193
  3.4 0.7 %collective-permute-start = (bf16[16,1280]{1,0:T(8,128)(2,1)}, bf16[16,1280]{1,0:T(8,128)(2,1)S(1)}, u32[]{:S(2)}, u32[]{:S(2)}) collective-permute-start(bf16[16,1280]{1,0:T(8,128)(2,1)} %whiten.1), channel_id=1, source_target_pairs={{1,0},{0,1},{3,2},{2,3},{5,4},{4,5},{7,6},{6,7},{9,8},{8,9},{11,10... | collective-permute-start | bytes 122888 | tf_op jit(solution)/shard_map/ppermute | solution.py:413
  4.1 0.9 %pad_maximum_fusion.1 = bf16[2,16,1280]{2,1,0:T(8,128)(2,1)S(1)} fusion(bf16[1,16,1280]{2,1,0:T(8,128)(2,1)} %bitcast.10), kind=kLoop, calls=%fused_computation.1 | loop fusion | flops 40960 | bytes 122880 | tf_op jit(solution)/shard_map/stack | solution.py:424
  5.0 0.2 %collective-permute-done = bf16[16,1280]{1,0:T(8,128)(2,1)S(1)} collective-permute-done((bf16[16,1280]{1,0:T(8,128)(2,1)}, bf16[16,1280]{1,0:T(8,128)(2,1)S(1)}, u32[]{:S(2)}, u32[]{:S(2)}) %collective-permute-start) | collective-permute-done | bytes 40992 | tf_op jit(solution)/shard_map/ppermute | solution.py:413
  5.2 1.1 %collective-permute-start.2 = (bf16[2,16,1280]{2,1,0:T(8,128)(2,1)S(1)}, bf16[2,16,1280]{2,1,0:T(8,128)(2,1)S(1)}, u32[]{:S(2)}, u32[]{:S(2)}) collective-permute-start(bf16[2,16,1280]{2,1,0:T(8,128)(2,1)S(1)} %bitcast_dynamic-update-slice_fusion.pair_ref.panels_ref), channel_id=1, source_target_pairs={{14,0},{7,1},{8,2},{5,3},{2,4},{11,5},{12,6},{9,7},{6,8},{15,9},{0... | collective-permute-start | bytes 245768 | tf_op jit(solution)/shard_map/ppermute | solution.py:421
  6.3 0.2 collective-permute-start.1
  6.5 3.2 %collective-permute-start.3 = (bf16[16,1280]{1,0:T(8,128)(2,1)S(1)}, bf16[16,1280]{1,0:T(8,128)(2,1)S(1)}, u32[]{:S(2)}, u32[]{:S(2)}) collective-permute-start(bf16[16,1280]{1,0:T(8,128)(2,1)S(1)} %slice_bitcast_fusion), channel_id=1, source_target_pairs={{8,0},{9,1},{10,2},{11,3},{12,4},{13,5},{14,6},{15,7},{0,8},{1,9},... | collective-permute-start | bytes 122888 | tf_op jit(solution)/shard_map/ppermute | solution.py:421
  9.7 0.0 copy-done
  9.7 0.5 %pair_panels.1.refs_0_ = f32[2,64,512]{2,1,0:T(8,128)S(1)} custom-call(bf16[2,16,1280]{2,1,0:T(8,128)(2,1)S(1)} %bitcast_dynamic-update-slice_fusion.pair_ref.panels_ref, bf16[2,16,1280]{2,1,0:T(8,128)(2,1)S(1)} %bitcast_dynamic-update-slice_fusion.pair_ref.panels_ref, bf16[1280,512]{1,0:T(8,128)(2,1)S(1)} %copy-done), custom_call_target="tpu_custom_call" | custom-call | flops 167772160 | bytes 262144 | tf_op jit(solution)/shard_map/pair_panels/pallas_call | solution.py:336
  10.2 4.4 %collective-permute-done.3 = bf16[16,1280]{1,0:T(8,128)(2,1)S(1)} collective-permute-done((bf16[16,1280]{1,0:T(8,128)(2,1)S(1)}, bf16[16,1280]{1,0:T(8,128)(2,1)S(1)}, u32[]{:S(2)}, u32[]{:S(2)}) %collective-permute-start.3) | collective-permute-done | bytes 40992 | tf_op jit(solution)/shard_map/ppermute | solution.py:421
  14.6 0.0 collective-permute-done.2
  14.6 0.0 collective-permute-done.1
  14.6 0.0 copy-start.1
  14.6 0.0 copy-start.2
  14.6 1.6 %collective-permute-start.4 = (bf16[5,16,1280]{2,1,0:T(8,128)(2,1)S(1)}, bf16[5,16,1280]{2,1,0:T(8,128)(2,1)S(1)}, u32[]{:S(2)}, u32[]{:S(2)}) collective-permute-start(bf16[5,16,1280]{2,1,0:T(8,128)(2,1)S(1)} %pad_maximum_fusion.panels_ref), channel_id=1, source_target_pairs={{1,0},{0,1},{3,2},{2,3},{5,4},{4,5},{7,6},{6,7},{9,8},{8,9},{11,10... | collective-permute-start | bytes 614408 | tf_op jit(solution)/shard_map/ppermute | solution.py:413
  16.2 1.0 %near_panels.1.refs_1_ = f32[5,64,512]{2,1,0:T(8,128)S(1)} custom-call(bf16[2,16,1280]{2,1,0:T(8,128)(2,1)S(1)} %bitcast_dynamic-update-slice_fusion.pair_ref.panels_ref, bf16[5,16,1280]{2,1,0:T(8,128)(2,1)S(1)} %pad_maximum_fusion.panels_ref, bf16[1280,512]{1,0:T(8,128)(2,1)S(1)} %copy-done), custom_call_target="tpu_custom_call" | custom-call | flops 419430400 | bytes 655360 | tf_op jit(solution)/shard_map/near_panels/pallas_call | solution.py:336
  17.2 0.1 collective-permute-done.4.panels_ref
  17.3 0.0 copy-done.1
  17.3 0.0 copy-done.2
  17.3 2.2 %swapped_panels.1 = f32[10,8,8,401]{3,2,1,0:T(8,128)} custom-call(s32[1,10]{1,0:T(1,128)S(1)} %copy-done.2, bf16[2,16,1280]{2,1,0:T(8,128)(2,1)S(1)} %bitcast_dynamic-update-slice_fusion.pair_ref.panels_ref, bf16[5,16,1280]{2,1,0:T(8,128)(2,1)S(1)} %collective-permute-done.4.panels_ref, bf16[1280,512]{1,0:T(8,128)(2,1)S(1)} %copy-done, ...), custom_call_target="tpu_custom_call" | custom-call | flops 335544320 | bytes 524288 | tf_op jit(solution)/shard_map/swapped_panels/pallas_call | solution.py:393
  (3 shorter events, 0.0 us)
Async XLA Ops:
  0.0 9.7 %copy-start = (bf16[1280,512]{1,0:T(8,128)(2,1)S(1)}, bf16[1280,512]{1,0:T(8,128)(2,1)}, u32[]{:S(2)}) copy-start(bf16[1280,512]{1,0:T(8,128)(2,1)} %constant.9.clone.table_ref) | copy-start | bytes 3932164
  3.4 1.8 %collective-permute-start = (bf16[16,1280]{1,0:T(8,128)(2,1)}, bf16[16,1280]{1,0:T(8,128)(2,1)S(1)}, u32[]{:S(2)}, u32[]{:S(2)}) collective-permute-start(bf16[16,1280]{1,0:T(8,128)(2,1)} %whiten.1), channel_id=1, source_target_pairs={{1,0},{0,1},{3,2},{2,3},{5,4},{4,5},{7,6},{6,7},{9,8},{8,9},{11,10... | collective-permute-start | bytes 122888 | tf_op jit(solution)/shard_map/ppermute | solution.py:413
  5.2 9.4 %collective-permute-start.2 = (bf16[2,16,1280]{2,1,0:T(8,128)(2,1)S(1)}, bf16[2,16,1280]{2,1,0:T(8,128)(2,1)S(1)}, u32[]{:S(2)}, u32[]{:S(2)}) collective-permute-start(bf16[2,16,1280]{2,1,0:T(8,128)(2,1)S(1)} %bitcast_dynamic-update-slice_fusion.pair_ref.panels_ref), channel_id=1, source_target_pairs={{14,0},{7,1},{8,2},{5,3},{2,4},{11,5},{12,6},{9,7},{6,8},{15,9},{0... | collective-permute-start | bytes 245768 | tf_op jit(solution)/shard_map/ppermute | solution.py:421
  6.3 8.3 %collective-permute-start.1 = (bf16[2,16,1280]{2,1,0:T(8,128)(2,1)S(1)}, bf16[2,16,1280]{2,1,0:T(8,128)(2,1)S(1)}, u32[]{:S(2)}, u32[]{:S(2)}) collective-permute-start(bf16[2,16,1280]{2,1,0:T(8,128)(2,1)S(1)} %bitcast_dynamic-update-slice_fusion.pair_ref.panels_ref), channel_id=1, source_target_pairs={{2,0},{5,1},{0,2},{7,3},{6,4},{9,5},{4,6},{11,7},{10,8},{13,9},{8,... | collective-permute-start | bytes 245768 | tf_op jit(solution)/shard_map/ppermute | solution.py:421
  6.5 8.1 %collective-permute-start.3 = (bf16[16,1280]{1,0:T(8,128)(2,1)S(1)}, bf16[16,1280]{1,0:T(8,128)(2,1)S(1)}, u32[]{:S(2)}, u32[]{:S(2)}) collective-permute-start(bf16[16,1280]{1,0:T(8,128)(2,1)S(1)} %slice_bitcast_fusion), channel_id=1, source_target_pairs={{8,0},{9,1},{10,2},{11,3},{12,4},{13,5},{14,6},{15,7},{0,8},{1,9},... | collective-permute-start | bytes 122888 | tf_op jit(solution)/shard_map/ppermute | solution.py:421
  14.6 2.7 %copy-start.1 = (f32[1,10,8,8,401]{4,3,2,1,0:T(8,128)S(1)}, f32[1,10,8,8,401]{4,3,2,1,0:T(8,128)}, u32[]{:S(2)}) copy-start(f32[1,10,8,8,401]{4,3,2,1,0:T(8,128)} %param.9) | copy-start | bytes 3079684
  14.6 2.7 %copy-start.2 = (s32[1,10]{1,0:T(1,128)S(1)}, s32[1,10]{1,0:T(1,128)}, u32[]{:S(2)}) copy-start(s32[1,10]{1,0:T(1,128)} %slots_any.1) | copy-start | bytes 124
  14.6 2.7 %collective-permute-start.4 = (bf16[5,16,1280]{2,1,0:T(8,128)(2,1)S(1)}, bf16[5,16,1280]{2,1,0:T(8,128)(2,1)S(1)}, u32[]{:S(2)}, u32[]{:S(2)}) collective-permute-start(bf16[5,16,1280]{2,1,0:T(8,128)(2,1)S(1)} %pad_maximum_fusion.panels_ref), channel_id=1, source_target_pairs={{1,0},{0,1},{3,2},{2,3},{5,4},{4,5},{7,6},{6,7},{9,8},{8,9},{11,10... | collective-permute-start | bytes 614408 | tf_op jit(solution)/shard_map/ppermute | solution.py:413

commit v9 on v8

--- a/solution.py
+++ b/solution.py
@@ -192,7 +192,7 @@
     anywhere = pl.BlockSpec(memory_space=pltpu.HBM)
     return pl.pallas_call(
         whiten_kernel,
-        out_shape=jax.ShapeDtypeStruct((rows, 2 * LANES), jnp.bfloat16),
+        out_shape=pltpu.VMEM((rows, 2 * LANES), jnp.bfloat16),
         in_specs=[anywhere] * 3,
         out_specs=pl.BlockSpec(memory_space=pltpu.VMEM),
         scratch_shapes=[

time: 19.7 us -> 18.8 us (0.954)
  other arithmetic: 0.89 us -> 0.04 us
  waiting for transfers between devices: 4.7 us -> 5.36 us
  Pallas kernels: 7.03 us -> 6.39 us
    another operation x1, other arithmetic: 0.86 us -> 0.01 us  [gather_near(): twice = jnp.stack([own, own])]
    ppermute x2, waiting for transfers between devices: 0.32 us -> 1 us  [swap(): return lax.ppermute(array, 'row', [(i ^ 1, i) for i in range(panel_count)])]
    pallas_call x1, Pallas kernels: 3.38 us -> 2.76 us  [whiten(): pl.pallas_call(whiten_kernel, out_shape=pltpu.VMEM((rows, 2 * LANES), jnp...]
  transfers between devices with their start and end apart: 5 -> 5, of which waited for: 3 -> 3; matrix products, arithmetic and copies ran while one was open for 4% -> 0% of each run, Pallas kernels for 7% -> 8%
where the time goes in v9:
time: 18.8 us; the launch traced here: 18.7 us
  starting transfers between devices  6.83 us (36%)
  Pallas kernels  6.39 us (34%)
  waiting for transfers between devices  5.36 us (29%)
    ppermute x3, starting transfers between devices, fetch(): return lax.ppermute(array, 'row', moves)  4.48 us
    ppermute x3, waiting for transfers between devices, fetch(): return lax.ppermute(array, 'row', moves)  4.36 us
    pallas_call x1, Pallas kernels, whiten(): pl.pallas_call(whiten_kernel, out_shape=pltpu.VMEM((rows, 2 * LANES), jnp...  2.76 us
    ppermute x2, starting transfers between devices, swap(): return lax.ppermute(array, 'row', [(i ^ 1, i) for i in range(panel_count)])  2.34 us
    pallas_call x1, Pallas kernels, last(): pl.pallas_call(functools.partial(last_kernel, panel_count, lists), out_sh...  2.2 us
    pallas_call x2, Pallas kernels, early(): pl.pallas_call(functools.partial(early_kernel, panel_count, which), out_s...  1.43 us
    ppermute x2, waiting for transfers between devices, swap(): return lax.ppermute(array, 'row', [(i ^ 1, i) for i in range(panel_count)])  1 us
  transfers between devices with their start and end apart: 5, of which 3 were waited for; matrix products, arithmetic and copies ran while one was open for 0% of the time, Pallas kernels for 8%

profile of v9, /device:TPU:25, one launch (start us, length us, event | category | flops | bytes accessed | tf_op | source)
XLA Modules:
  0.0 18.7 jit_solution(8239904837172672802)
XLA Ops:
  0.0 0.0 copy-start
  0.0 2.8 %whiten.1 = bf16[16,1280]{1,0:T(8,128)(2,1)S(1)} custom-call(bf16[8,2,12000]{2,1,0:T(2,128)(2,1)} %x_hbm.1, s32[2,8]{1,0:T(2,128)} %bitcast.12, bf16[600,1280]{1,0:T(8,128)(2,1)} %constant.8.clone.table_hbm), custom_call_target="tpu_custom_call" | custom-call | tf_op jit(solution)/shard_map/whiten/pallas_call | solution.py:193
  2.8 0.7 %collective-permute-start = (bf16[16,1280]{1,0:T(8,128)(2,1)S(1)}, bf16[16,1280]{1,0:T(8,128)(2,1)S(1)}, u32[]{:S(2)}, u32[]{:S(2)}) collective-permute-start(bf16[16,1280]{1,0:T(8,128)(2,1)S(1)} %whiten.1), channel_id=1, source_target_pairs={{1,0},{0,1},{3,2},{2,3},{5,4},{4,5},{7,6},{6,7},{9,8},{8,9},{11,10... | collective-permute-start | bytes 122888 | tf_op jit(solution)/shard_map/ppermute | solution.py:413
  3.5 0.9 %collective-permute-done = bf16[16,1280]{1,0:T(8,128)(2,1)S(1)} collective-permute-done((bf16[16,1280]{1,0:T(8,128)(2,1)S(1)}, bf16[16,1280]{1,0:T(8,128)(2,1)S(1)}, u32[]{:S(2)}, u32[]{:S(2)}) %collective-permute-start) | collective-permute-done | bytes 40992 | tf_op jit(solution)/shard_map/ppermute | solution.py:413
  4.4 1.1 %collective-permute-start.2 = (bf16[2,16,1280]{2,1,0:T(8,128)(2,1)S(1)}, bf16[2,16,1280]{2,1,0:T(8,128)(2,1)S(1)}, u32[]{:S(2)}, u32[]{:S(2)}) collective-permute-start(bf16[2,16,1280]{2,1,0:T(8,128)(2,1)S(1)} %bitcast_dynamic-update-slice_fusion.pair_ref.panels_ref), channel_id=1, source_target_pairs={{14,0},{7,1},{8,2},{5,3},{2,4},{11,5},{12,6},{9,7},{6,8},{15,9},{0... | collective-permute-start | bytes 245768 | tf_op jit(solution)/shard_map/ppermute | solution.py:421
  5.5 0.2 collective-permute-start.1
  5.7 3.2 %collective-permute-start.3 = (bf16[16,1280]{1,0:T(8,128)(2,1)S(1)}, bf16[16,1280]{1,0:T(8,128)(2,1)S(1)}, u32[]{:S(2)}, u32[]{:S(2)}) collective-permute-start(bf16[16,1280]{1,0:T(8,128)(2,1)S(1)} %slice_bitcast_fusion), channel_id=1, source_target_pairs={{8,0},{9,1},{10,2},{11,3},{12,4},{13,5},{14,6},{15,7},{0,8},{1,9},... | collective-permute-start | bytes 122888 | tf_op jit(solution)/shard_map/ppermute | solution.py:421
  8.9 0.0 copy-done
  8.9 0.5 %pair_panels.1.refs_0_ = f32[2,64,512]{2,1,0:T(8,128)S(1)} custom-call(bf16[2,16,1280]{2,1,0:T(8,128)(2,1)S(1)} %bitcast_dynamic-update-slice_fusion.pair_ref.panels_ref, bf16[2,16,1280]{2,1,0:T(8,128)(2,1)S(1)} %bitcast_dynamic-update-slice_fusion.pair_ref.panels_ref, bf16[1280,512]{1,0:T(8,128)(2,1)S(1)} %copy-done), custom_call_target="tpu_custom_call" | custom-call | flops 167772160 | bytes 262144 | tf_op jit(solution)/shard_map/pair_panels/pallas_call | solution.py:336
  9.4 4.4 %collective-permute-done.3 = bf16[16,1280]{1,0:T(8,128)(2,1)S(1)} collective-permute-done((bf16[16,1280]{1,0:T(8,128)(2,1)S(1)}, bf16[16,1280]{1,0:T(8,128)(2,1)S(1)}, u32[]{:S(2)}, u32[]{:S(2)}) %collective-permute-start.3) | collective-permute-done | bytes 40992 | tf_op jit(solution)/shard_map/ppermute | solution.py:421
  13.7 0.0 collective-permute-done.2
  13.7 0.0 collective-permute-done.1
  13.7 0.0 copy-start.1
  13.7 0.0 copy-start.2
  13.8 1.6 %collective-permute-start.4 = (bf16[5,16,1280]{2,1,0:T(8,128)(2,1)S(1)}, bf16[5,16,1280]{2,1,0:T(8,128)(2,1)S(1)}, u32[]{:S(2)}, u32[]{:S(2)}) collective-permute-start(bf16[5,16,1280]{2,1,0:T(8,128)(2,1)S(1)} %pad_maximum_fusion.panels_ref), channel_id=1, source_target_pairs={{1,0},{0,1},{3,2},{2,3},{5,4},{4,5},{7,6},{6,7},{9,8},{8,9},{11,10... | collective-permute-start | bytes 614408 | tf_op jit(solution)/shard_map/ppermute | solution.py:413
  15.4 0.9 %near_panels.1.refs_1_ = f32[5,64,512]{2,1,0:T(8,128)S(1)} custom-call(bf16[2,16,1280]{2,1,0:T(8,128)(2,1)S(1)} %bitcast_dynamic-update-slice_fusion.pair_ref.panels_ref, bf16[5,16,1280]{2,1,0:T(8,128)(2,1)S(1)} %pad_maximum_fusion.panels_ref, bf16[1280,512]{1,0:T(8,128)(2,1)S(1)} %copy-done), custom_call_target="tpu_custom_call" | custom-call | flops 419430400 | bytes 655360 | tf_op jit(solution)/shard_map/near_panels/pallas_call | solution.py:336
  16.3 0.1 collective-permute-done.4.panels_ref
  16.5 0.0 copy-done.1
  16.5 0.0 copy-done.2
  16.5 2.2 %swapped_panels.1 = f32[10,8,8,401]{3,2,1,0:T(8,128)} custom-call(s32[1,10]{1,0:T(1,128)S(1)} %copy-done.2, bf16[2,16,1280]{2,1,0:T(8,128)(2,1)S(1)} %bitcast_dynamic-update-slice_fusion.pair_ref.panels_ref, bf16[5,16,1280]{2,1,0:T(8,128)(2,1)S(1)} %collective-permute-done.4.panels_ref, bf16[1280,512]{1,0:T(8,128)(2,1)S(1)} %copy-done, ...), custom_call_target="tpu_custom_call" | custom-call | flops 335544320 | bytes 524288 | tf_op jit(solution)/shard_map/swapped_panels/pallas_call | solution.py:393
  (4 shorter events, 0.0 us)
Async XLA Ops:
  0.0 8.9 %copy-start = (bf16[1280,512]{1,0:T(8,128)(2,1)S(1)}, bf16[1280,512]{1,0:T(8,128)(2,1)}, u32[]{:S(2)}) copy-start(bf16[1280,512]{1,0:T(8,128)(2,1)} %constant.9.clone.table_ref) | copy-start | bytes 3932164
  2.8 1.6 %collective-permute-start = (bf16[16,1280]{1,0:T(8,128)(2,1)S(1)}, bf16[16,1280]{1,0:T(8,128)(2,1)S(1)}, u32[]{:S(2)}, u32[]{:S(2)}) collective-permute-start(bf16[16,1280]{1,0:T(8,128)(2,1)S(1)} %whiten.1), channel_id=1, source_target_pairs={{1,0},{0,1},{3,2},{2,3},{5,4},{4,5},{7,6},{6,7},{9,8},{8,9},{11,10... | collective-permute-start | bytes 122888 | tf_op jit(solution)/shard_map/ppermute | solution.py:413
  4.4 9.3 %collective-permute-start.2 = (bf16[2,16,1280]{2,1,0:T(8,128)(2,1)S(1)}, bf16[2,16,1280]{2,1,0:T(8,128)(2,1)S(1)}, u32[]{:S(2)}, u32[]{:S(2)}) collective-permute-start(bf16[2,16,1280]{2,1,0:T(8,128)(2,1)S(1)} %bitcast_dynamic-update-slice_fusion.pair_ref.panels_ref), channel_id=1, source_target_pairs={{14,0},{7,1},{8,2},{5,3},{2,4},{11,5},{12,6},{9,7},{6,8},{15,9},{0... | collective-permute-start | bytes 245768 | tf_op jit(solution)/shard_map/ppermute | solution.py:421
  5.5 8.3 %collective-permute-start.1 = (bf16[2,16,1280]{2,1,0:T(8,128)(2,1)S(1)}, bf16[2,16,1280]{2,1,0:T(8,128)(2,1)S(1)}, u32[]{:S(2)}, u32[]{:S(2)}) collective-permute-start(bf16[2,16,1280]{2,1,0:T(8,128)(2,1)S(1)} %bitcast_dynamic-update-slice_fusion.pair_ref.panels_ref), channel_id=1, source_target_pairs={{2,0},{5,1},{0,2},{7,3},{6,4},{9,5},{4,6},{11,7},{10,8},{13,9},{8,... | collective-permute-start | bytes 245768 | tf_op jit(solution)/shard_map/ppermute | solution.py:421
  5.7 8.1 %collective-permute-start.3 = (bf16[16,1280]{1,0:T(8,128)(2,1)S(1)}, bf16[16,1280]{1,0:T(8,128)(2,1)S(1)}, u32[]{:S(2)}, u32[]{:S(2)}) collective-permute-start(bf16[16,1280]{1,0:T(8,128)(2,1)S(1)} %slice_bitcast_fusion), channel_id=1, source_target_pairs={{8,0},{9,1},{10,2},{11,3},{12,4},{13,5},{14,6},{15,7},{0,8},{1,9},... | collective-permute-start | bytes 122888 | tf_op jit(solution)/shard_map/ppermute | solution.py:421
  13.7 2.7 %copy-start.1 = (f32[1,10,8,8,401]{4,3,2,1,0:T(8,128)S(1)}, f32[1,10,8,8,401]{4,3,2,1,0:T(8,128)}, u32[]{:S(2)}) copy-start(f32[1,10,8,8,401]{4,3,2,1,0:T(8,128)} %param.9) | copy-start | bytes 3079684
  13.7 2.7 %copy-start.2 = (s32[1,10]{1,0:T(1,128)S(1)}, s32[1,10]{1,0:T(1,128)}, u32[]{:S(2)}) copy-start(s32[1,10]{1,0:T(1,128)} %slots_any.1) | copy-start | bytes 124
  13.8 2.7 %collective-permute-start.4 = (bf16[5,16,1280]{2,1,0:T(8,128)(2,1)S(1)}, bf16[5,16,1280]{2,1,0:T(8,128)(2,1)S(1)}, u32[]{:S(2)}, u32[]{:S(2)}) collective-permute-start(bf16[5,16,1280]{2,1,0:T(8,128)(2,1)S(1)} %pad_maximum_fusion.panels_ref), channel_id=1, source_target_pairs={{1,0},{0,1},{3,2},{2,3},{5,4},{4,5},{7,6},{6,7},{9,8},{8,9},{11,10... | collective-permute-start | bytes 614408 | tf_op jit(solution)/shard_map/ppermute | solution.py:413

commit v10 on v9

--- a/solution.py
+++ b/solution.py
@@ -301,11 +301,11 @@
     found = []
     for t in range(2):
         ahead = jnp.where(core == 0, chip + 2, chip + 1 + 2 * odd)
-        found.append((2 * odd * core + t, 2 * ahead + (1 - core if t == 0 else core), True))
+        found.append((t, 2 * ahead + (1 - core if t == 0 else core), True))
     for t in range(2):
         ahead = 2 * (chip + 3 - 2 * odd) + 1 - t
         wanted = True if t == 0 else core == 0
-        found.append((jnp.where(core == 0, 2 + t, 4), jnp.where(core == 0, ahead, 2 * chip + 8), wanted))
+        found.append((2 + t, jnp.where(core == 0, ahead, 2 * chip + 8), wanted))
     return found
 
 
@@ -430,7 +430,10 @@
     first = early(pair_panels, 2, panel_count, chans, pair, pair, table)
     near, next_near, far, first = lax.optimization_barrier((near, next_near, far, first))
     five = jnp.concatenate([near, next_near, far[None]], axis=0)
-    swapped = swap(five)
+    me, chip, core, odd = place(panel_count)
+    low = jnp.where((core == 0) & (odd == 1), next_near, near)
+    high = jnp.where(core == 0, far[None], next_near)
+    swapped = swap(jnp.concatenate([low, high], axis=0))
     second = early(near_panels, 5, panel_count, chans, pair, five, table)
     lists = (pair_panels, near_panels, swapped_panels)
     return last(lists, (2, 5, 4), panel_count, slots, pair, swapped, table, stack, first, second)

time: 18.8 us -> 18.9 us (level)
  local copies, waits for them, and re-layouts: 0.02 us -> 0.3 us
    unnamed x6, local copies, waits for them, and re-layouts: 0.01 us -> 0.3 us
  transfers between devices with their start and end apart: 5 -> 5, of which waited for: 3 -> 2; matrix products, arithmetic and copies ran while one was open for 0% -> 0% of each run, Pallas kernels for 8% -> 8%
where the time goes in v10:
time: 18.9 us; the launch traced here: 18.7 us
  starting transfers between devices  6.83 us (36%)
  Pallas kernels  6.22 us (33%)
  waiting for transfers between devices  5.27 us (28%)
  local copies, waits for them, and re-layouts  0.3 us (2%)
    ppermute x3, starting transfers between devices, fetch(): return lax.ppermute(array, 'row', moves)  4.48 us
    ppermute x3, waiting for transfers between devices, fetch(): return lax.ppermute(array, 'row', moves)  4.36 us
    pallas_call x1, Pallas kernels, whiten(): pl.pallas_call(whiten_kernel, out_shape=pltpu.VMEM((rows, 2 * LANES), jnp...  2.76 us
    ppermute x2, starting transfers between devices, swap(): return lax.ppermute(array, 'row', [(i ^ 1, i) for i in range(panel_count)])  2.34 us
    pallas_call x1, Pallas kernels, last(): pl.pallas_call(functools.partial(last_kernel, panel_count, lists), out_sh...  2.03 us
    pallas_call x2, Pallas kernels, early(): pl.pallas_call(functools.partial(early_kernel, panel_count, which), out_s...  1.43 us
    ppermute x2, waiting for transfers between devices, swap(): return lax.ppermute(array, 'row', [(i ^ 1, i) for i in range(panel_count)])  0.91 us
  transfers between devices with their start and end apart: 5, of which 2 were waited for; matrix products, arithmetic and copies ran while one was open for 0% of the time, Pallas kernels for 8%

profile of v10, /device:TPU:25, one launch (start us, length us, event | category | flops | bytes accessed | tf_op | source)
XLA Modules:
  0.0 18.7 jit_solution(7400031793846030177)
XLA Ops:
  0.0 0.0 copy-start
  0.0 2.8 %whiten.1 = bf16[16,1280]{1,0:T(8,128)(2,1)S(1)} custom-call(bf16[8,2,12000]{2,1,0:T(2,128)(2,1)} %x_hbm.1, s32[2,8]{1,0:T(2,128)} %bitcast.12, bf16[600,1280]{1,0:T(8,128)(2,1)} %constant.26.clone.table_hbm), custom_call_target="tpu_custom_call" | custom-call | tf_op jit(solution)/shard_map/whiten/pallas_call | solution.py:193
  2.8 0.7 %collective-permute-start = (bf16[16,1280]{1,0:T(8,128)(2,1)S(1)}, bf16[16,1280]{1,0:T(8,128)(2,1)S(1)}, u32[]{:S(2)}, u32[]{:S(2)}) collective-permute-start(bf16[16,1280]{1,0:T(8,128)(2,1)S(1)} %whiten.1), channel_id=1, source_target_pairs={{1,0},{0,1},{3,2},{2,3},{5,4},{4,5},{7,6},{6,7},{9,8},{8,9},{11,10... | collective-permute-start | bytes 122888 | tf_op jit(solution)/shard_map/ppermute | solution.py:413
  3.5 0.9 %collective-permute-done = bf16[16,1280]{1,0:T(8,128)(2,1)S(1)} collective-permute-done((bf16[16,1280]{1,0:T(8,128)(2,1)S(1)}, bf16[16,1280]{1,0:T(8,128)(2,1)S(1)}, u32[]{:S(2)}, u32[]{:S(2)}) %collective-permute-start) | collective-permute-done | bytes 40992 | tf_op jit(solution)/shard_map/ppermute | solution.py:413
  4.4 1.1 %collective-permute-start.2 = (bf16[2,16,1280]{2,1,0:T(8,128)(2,1)S(1)}, bf16[2,16,1280]{2,1,0:T(8,128)(2,1)S(1)}, u32[]{:S(2)}, u32[]{:S(2)}) collective-permute-start(bf16[2,16,1280]{2,1,0:T(8,128)(2,1)S(1)} %bitcast_dynamic-update-slice_fusion.pair_ref.panels_ref), channel_id=1, source_target_pairs={{14,0},{7,1},{8,2},{5,3},{2,4},{11,5},{12,6},{9,7},{6,8},{15,9},{0... | collective-permute-start | bytes 245768 | tf_op jit(solution)/shard_map/ppermute | solution.py:421
  5.5 0.2 collective-permute-start.1
  5.7 3.2 %collective-permute-start.3 = (bf16[16,1280]{1,0:T(8,128)(2,1)S(1)}, bf16[16,1280]{1,0:T(8,128)(2,1)S(1)}, u32[]{:S(2)}, u32[]{:S(2)}) collective-permute-start(bf16[16,1280]{1,0:T(8,128)(2,1)S(1)} %slice_bitcast_fusion), channel_id=1, source_target_pairs={{8,0},{9,1},{10,2},{11,3},{12,4},{13,5},{14,6},{15,7},{0,8},{1,9},... | collective-permute-start | bytes 122888 | tf_op jit(solution)/shard_map/ppermute | solution.py:421
  8.9 0.0 copy-done
  8.9 0.5 %pair_panels.1.refs_0_ = f32[2,64,512]{2,1,0:T(8,128)S(1)} custom-call(bf16[2,16,1280]{2,1,0:T(8,128)(2,1)S(1)} %bitcast_dynamic-update-slice_fusion.pair_ref.panels_ref, bf16[2,16,1280]{2,1,0:T(8,128)(2,1)S(1)} %bitcast_dynamic-update-slice_fusion.pair_ref.panels_ref, bf16[1280,512]{1,0:T(8,128)(2,1)S(1)} %copy-done), custom_call_target="tpu_custom_call" | custom-call | flops 167772160 | bytes 262144 | tf_op jit(solution)/shard_map/pair_panels/pallas_call | solution.py:336
  9.4 4.4 %collective-permute-done.3 = bf16[16,1280]{1,0:T(8,128)(2,1)S(1)} collective-permute-done((bf16[16,1280]{1,0:T(8,128)(2,1)S(1)}, bf16[16,1280]{1,0:T(8,128)(2,1)S(1)}, u32[]{:S(2)}, u32[]{:S(2)}) %collective-permute-start.3) | collective-permute-done | bytes 40992 | tf_op jit(solution)/shard_map/ppermute | solution.py:421
  13.7 0.0 collective-permute-done.2
  13.7 0.0 collective-permute-done.1
  13.8 1.6 %collective-permute-start.4 = (bf16[4,16,1280]{2,1,0:T(8,128)(2,1)S(1)}, bf16[4,16,1280]{2,1,0:T(8,128)(2,1)S(1)}, u32[]{:S(2)}, u32[]{:S(2)}) collective-permute-start(bf16[4,16,1280]{2,1,0:T(8,128)(2,1)S(1)} %pad_maximum_fusion.1), channel_id=1, source_target_pairs={{1,0},{0,1},{3,2},{2,3},{5,4},{4,5},{7,6},{6,7},{9,8},{8,9},{11,10... | collective-permute-start | bytes 491528 | tf_op jit(solution)/shard_map/ppermute | solution.py:413
  15.4 0.0 copy-start.1
  15.4 0.0 copy-start.2
  15.4 0.9 %near_panels.1.refs_1_ = f32[5,64,512]{2,1,0:T(8,128)S(1)} custom-call(bf16[2,16,1280]{2,1,0:T(8,128)(2,1)S(1)} %bitcast_dynamic-update-slice_fusion.pair_ref.panels_ref, bf16[5,16,1280]{2,1,0:T(8,128)(2,1)S(1)} %pad_maximum_fusion.panels_ref, bf16[1280,512]{1,0:T(8,128)(2,1)S(1)} %copy-done), custom_call_target="tpu_custom_call" | custom-call | flops 419430400 | bytes 655360 | tf_op jit(solution)/shard_map/near_panels/pallas_call | solution.py:336
  16.4 0.0 collective-permute-done.4.panels_ref
  16.4 0.3 %copy-done.1 = f32[1,10,8,8,401]{4,3,2,1,0:T(8,128)S(1)} copy-done((f32[1,10,8,8,401]{4,3,2,1,0:T(8,128)S(1)}, f32[1,10,8,8,401]{4,3,2,1,0:T(8,128)}, u32[]{:S(2)}) %copy-start.1) | copy-done | bytes 1026584
  16.7 0.0 copy-done.2
  16.7 2.0 %swapped_panels.1 = f32[10,8,8,401]{3,2,1,0:T(8,128)} custom-call(s32[1,10]{1,0:T(1,128)S(1)} %copy-done.2, bf16[2,16,1280]{2,1,0:T(8,128)(2,1)S(1)} %bitcast_dynamic-update-slice_fusion.pair_ref.panels_ref, bf16[4,16,1280]{2,1,0:T(8,128)(2,1)S(1)} %collective-permute-done.4.panels_ref, bf16[1280,512]{1,0:T(8,128)(2,1)S(1)} %copy-done, ...), custom_call_target="tpu_custom_call" | custom-call | flops 335544320 | bytes 524288 | tf_op jit(solution)/shard_map/swapped_panels/pallas_call | solution.py:393
  (6 shorter events, 0.1 us)
Async XLA Ops:
  0.0 8.9 %copy-start = (bf16[1280,512]{1,0:T(8,128)(2,1)S(1)}, bf16[1280,512]{1,0:T(8,128)(2,1)}, u32[]{:S(2)}) copy-start(bf16[1280,512]{1,0:T(8,128)(2,1)} %constant.27.clone.table_ref) | copy-start | bytes 3932164
  2.8 1.6 %collective-permute-start = (bf16[16,1280]{1,0:T(8,128)(2,1)S(1)}, bf16[16,1280]{1,0:T(8,128)(2,1)S(1)}, u32[]{:S(2)}, u32[]{:S(2)}) collective-permute-start(bf16[16,1280]{1,0:T(8,128)(2,1)S(1)} %whiten.1), channel_id=1, source_target_pairs={{1,0},{0,1},{3,2},{2,3},{5,4},{4,5},{7,6},{6,7},{9,8},{8,9},{11,10... | collective-permute-start | bytes 122888 | tf_op jit(solution)/shard_map/ppermute | solution.py:413
  4.4 9.3 %collective-permute-start.2 = (bf16[2,16,1280]{2,1,0:T(8,128)(2,1)S(1)}, bf16[2,16,1280]{2,1,0:T(8,128)(2,1)S(1)}, u32[]{:S(2)}, u32[]{:S(2)}) collective-permute-start(bf16[2,16,1280]{2,1,0:T(8,128)(2,1)S(1)} %bitcast_dynamic-update-slice_fusion.pair_ref.panels_ref), channel_id=1, source_target_pairs={{14,0},{7,1},{8,2},{5,3},{2,4},{11,5},{12,6},{9,7},{6,8},{15,9},{0... | collective-permute-start | bytes 245768 | tf_op jit(solution)/shard_map/ppermute | solution.py:421
  5.5 8.3 %collective-permute-start.1 = (bf16[2,16,1280]{2,1,0:T(8,128)(2,1)S(1)}, bf16[2,16,1280]{2,1,0:T(8,128)(2,1)S(1)}, u32[]{:S(2)}, u32[]{:S(2)}) collective-permute-start(bf16[2,16,1280]{2,1,0:T(8,128)(2,1)S(1)} %bitcast_dynamic-update-slice_fusion.pair_ref.panels_ref), channel_id=1, source_target_pairs={{2,0},{5,1},{0,2},{7,3},{6,4},{9,5},{4,6},{11,7},{10,8},{13,9},{8,... | collective-permute-start | bytes 245768 | tf_op jit(solution)/shard_map/ppermute | solution.py:421
  5.7 8.1 %collective-permute-start.3 = (bf16[16,1280]{1,0:T(8,128)(2,1)S(1)}, bf16[16,1280]{1,0:T(8,128)(2,1)S(1)}, u32[]{:S(2)}, u32[]{:S(2)}) collective-permute-start(bf16[16,1280]{1,0:T(8,128)(2,1)S(1)} %slice_bitcast_fusion), channel_id=1, source_target_pairs={{8,0},{9,1},{10,2},{11,3},{12,4},{13,5},{14,6},{15,7},{0,8},{1,9},... | collective-permute-start | bytes 122888 | tf_op jit(solution)/shard_map/ppermute | solution.py:421
  13.8 2.6 %collective-permute-start.4 = (bf16[4,16,1280]{2,1,0:T(8,128)(2,1)S(1)}, bf16[4,16,1280]{2,1,0:T(8,128)(2,1)S(1)}, u32[]{:S(2)}, u32[]{:S(2)}) collective-permute-start(bf16[4,16,1280]{2,1,0:T(8,128)(2,1)S(1)} %pad_maximum_fusion.1), channel_id=1, source_target_pairs={{1,0},{0,1},{3,2},{2,3},{5,4},{4,5},{7,6},{6,7},{9,8},{8,9},{11,10... | collective-permute-start | bytes 491528 | tf_op jit(solution)/shard_map/ppermute | solution.py:413
  15.4 1.3 %copy-start.1 = (f32[1,10,8,8,401]{4,3,2,1,0:T(8,128)S(1)}, f32[1,10,8,8,401]{4,3,2,1,0:T(8,128)}, u32[]{:S(2)}) copy-start(f32[1,10,8,8,401]{4,3,2,1,0:T(8,128)} %param.9) | copy-start | bytes 3079684
  15.4 1.3 %copy-start.2 = (s32[1,10]{1,0:T(1,128)S(1)}, s32[1,10]{1,0:T(1,128)}, u32[]{:S(2)}) copy-start(s32[1,10]{1,0:T(1,128)} %slots_any.1) | copy-start | bytes 124

commit v11 on v10

--- a/solution.py
+++ b/solution.py
@@ -321,7 +321,8 @@
         keep(start, (full * scale).reshape(len(some), chans * chans, COLS))
 
 
-def early_kernel(panel_count, which, pair_ref, panels_ref, table_ref, out_ref, cross):
+def early_kernel(panel_count, which, pair_ref, panels_ref, table_ref, *refs):
+    out_ref, cross = refs[-2:]
     own = pair_ref[0].astype(jnp.float32)
 
     def keep(start, corr):
@@ -330,19 +331,19 @@
     products(which, panel_count, own, panels_ref, table_ref[...], own.shape[0] // SEGS, cross, keep)
 
 
-def early(which, count, panel_count, chans, pair, panels, table):
+def early(which, count, panel_count, chans, pair, panels, table, *held):
     whole = pl.BlockSpec(memory_space=pltpu.VMEM)
     rows = count * chans * chans
     return pl.pallas_call(
         functools.partial(early_kernel, panel_count, which),
         out_shape=jax.ShapeDtypeStruct((count, chans * chans, COLS), jnp.float32),
-        in_specs=[whole] * 3,
+        in_specs=[whole] * (3 + len(held)),
         out_specs=whole,
         scratch_shapes=[pltpu.VMEM((rows, 2 * LANES), jnp.bfloat16)],
         compiler_params=pltpu.CompilerParams(vmem_limit_bytes=CORR_VMEM),
         cost_estimate=pl.CostEstimate(flops=4 * rows * LANES * COLS, bytes_accessed=4 * rows * COLS, transcendentals=0),
         name=which.__name__,
-    )(pair, panels, table)
+    )(pair, panels, table, *held)
 
 
 def last_kernel(panel_count, lists, slots_any, pair_ref, panels_ref, table_ref, stack_ref, *refs):
@@ -434,7 +435,7 @@
     low = jnp.where((core == 0) & (odd == 1), next_near, near)
     high = jnp.where(core == 0, far[None], next_near)
     swapped = swap(jnp.concatenate([low, high], axis=0))
-    second = early(near_panels, 5, panel_count, chans, pair, five, table)
+    second = early(near_panels, 5, panel_count, chans, pair, five, table, stack)
     lists = (pair_panels, near_panels, swapped_panels)
     return last(lists, (2, 5, 4), panel_count, slots, pair, swapped, table, stack, first, second)
 

time: 18.9 us -> 18.6 us (0.984)
  local copies, waits for them, and re-layouts: 0.3 us -> 0.02 us
    unnamed x6, local copies, waits for them, and re-layouts: 0.3 us -> 0.01 us
where the time goes in v11:
time: 18.6 us; the launch traced here: 18.5 us
  starting transfers between devices  6.83 us (37%)
  Pallas kernels  6.22 us (33%)
  waiting for transfers between devices  5.25 us (28%)
    ppermute x3, starting transfers between devices, fetch(): return lax.ppermute(array, 'row', moves)  4.48 us
    ppermute x3, waiting for transfers between devices, fetch(): return lax.ppermute(array, 'row', moves)  4.36 us
    pallas_call x1, Pallas kernels, whiten(): pl.pallas_call(whiten_kernel, out_shape=pltpu.VMEM((rows, 2 * LANES), jnp...  2.76 us
    ppermute x2, starting transfers between devices, swap(): return lax.ppermute(array, 'row', [(i ^ 1, i) for i in range(panel_count)])  2.34 us
    pallas_call x1, Pallas kernels, last(): pl.pallas_call(functools.partial(last_kernel, panel_count, lists), out_sh...  2.03 us
    pallas_call x2, Pallas kernels, early(): pl.pallas_call(functools.partial(early_kernel, panel_count, which), out_s...  1.43 us
    ppermute x2, waiting for transfers between devices, swap(): return lax.ppermute(array, 'row', [(i ^ 1, i) for i in range(panel_count)])  0.89 us
  transfers between devices with their start and end apart: 5, of which 2 were waited for; matrix products, arithmetic and copies ran while one was open for 0% of the time, Pallas kernels for 8%

profile of v11, /device:TPU:25, one launch (start us, length us, event | category | flops | bytes accessed | tf_op | source)
XLA Modules:
  0.0 18.5 jit_solution(15753554404382508384)
XLA Ops:
  0.0 0.0 copy-start
  0.0 2.8 %whiten.1 = bf16[16,1280]{1,0:T(8,128)(2,1)S(1)} custom-call(bf16[8,2,12000]{2,1,0:T(2,128)(2,1)} %x_hbm.1, s32[2,8]{1,0:T(2,128)} %bitcast.13, bf16[600,1280]{1,0:T(8,128)(2,1)} %constant.26.clone.table_hbm), custom_call_target="tpu_custom_call" | custom-call | tf_op jit(solution)/shard_map/whiten/pallas_call | solution.py:193
  2.8 0.7 %collective-permute-start = (bf16[16,1280]{1,0:T(8,128)(2,1)S(1)}, bf16[16,1280]{1,0:T(8,128)(2,1)S(1)}, u32[]{:S(2)}, u32[]{:S(2)}) collective-permute-start(bf16[16,1280]{1,0:T(8,128)(2,1)S(1)} %whiten.1), channel_id=1, source_target_pairs={{1,0},{0,1},{3,2},{2,3},{5,4},{4,5},{7,6},{6,7},{9,8},{8,9},{11,10... | collective-permute-start | bytes 122888 | tf_op jit(solution)/shard_map/ppermute | solution.py:414
  3.5 0.9 %collective-permute-done = bf16[16,1280]{1,0:T(8,128)(2,1)S(1)} collective-permute-done((bf16[16,1280]{1,0:T(8,128)(2,1)S(1)}, bf16[16,1280]{1,0:T(8,128)(2,1)S(1)}, u32[]{:S(2)}, u32[]{:S(2)}) %collective-permute-start) | collective-permute-done | bytes 40992 | tf_op jit(solution)/shard_map/ppermute | solution.py:414
  4.4 1.1 %collective-permute-start.2 = (bf16[2,16,1280]{2,1,0:T(8,128)(2,1)S(1)}, bf16[2,16,1280]{2,1,0:T(8,128)(2,1)S(1)}, u32[]{:S(2)}, u32[]{:S(2)}) collective-permute-start(bf16[2,16,1280]{2,1,0:T(8,128)(2,1)S(1)} %bitcast_dynamic-update-slice_fusion.pair_ref.panels_ref), channel_id=1, source_target_pairs={{14,0},{7,1},{8,2},{5,3},{2,4},{11,5},{12,6},{9,7},{6,8},{15,9},{0... | collective-permute-start | bytes 245768 | tf_op jit(solution)/shard_map/ppermute | solution.py:422
  5.5 0.2 collective-permute-start.1
  5.7 3.2 %collective-permute-start.3 = (bf16[16,1280]{1,0:T(8,128)(2,1)S(1)}, bf16[16,1280]{1,0:T(8,128)(2,1)S(1)}, u32[]{:S(2)}, u32[]{:S(2)}) collective-permute-start(bf16[16,1280]{1,0:T(8,128)(2,1)S(1)} %slice_bitcast_fusion), channel_id=1, source_target_pairs={{8,0},{9,1},{10,2},{11,3},{12,4},{13,5},{14,6},{15,7},{0,8},{1,9},... | collective-permute-start | bytes 122888 | tf_op jit(solution)/shard_map/ppermute | solution.py:422
  8.9 0.0 copy-done
  8.9 0.0 copy-start.1
  8.9 0.5 %pair_panels.1.refs_0_ = f32[2,64,512]{2,1,0:T(8,128)S(1)} custom-call(bf16[2,16,1280]{2,1,0:T(8,128)(2,1)S(1)} %bitcast_dynamic-update-slice_fusion.pair_ref.panels_ref, bf16[2,16,1280]{2,1,0:T(8,128)(2,1)S(1)} %bitcast_dynamic-update-slice_fusion.pair_ref.panels_ref, bf16[1280,512]{1,0:T(8,128)(2,1)S(1)} %copy-done), custom_call_target="tpu_custom_call" | custom-call | flops 167772160 | bytes 262144 | tf_op jit(solution)/shard_map/pair_panels/pallas_call | solution.py:337
  9.4 4.4 %collective-permute-done.3 = bf16[16,1280]{1,0:T(8,128)(2,1)S(1)} collective-permute-done((bf16[16,1280]{1,0:T(8,128)(2,1)S(1)}, bf16[16,1280]{1,0:T(8,128)(2,1)S(1)}, u32[]{:S(2)}, u32[]{:S(2)}) %collective-permute-start.3) | collective-permute-done | bytes 40992 | tf_op jit(solution)/shard_map/ppermute | solution.py:422
  13.7 0.0 collective-permute-done.2
  13.7 0.0 collective-permute-done.1
  13.8 1.6 %collective-permute-start.4 = (bf16[4,16,1280]{2,1,0:T(8,128)(2,1)S(1)}, bf16[4,16,1280]{2,1,0:T(8,128)(2,1)S(1)}, u32[]{:S(2)}, u32[]{:S(2)}) collective-permute-start(bf16[4,16,1280]{2,1,0:T(8,128)(2,1)S(1)} %pad_maximum_fusion.1), channel_id=1, source_target_pairs={{1,0},{0,1},{3,2},{2,3},{5,4},{4,5},{7,6},{6,7},{9,8},{8,9},{11,10... | collective-permute-start | bytes 491528 | tf_op jit(solution)/shard_map/ppermute | solution.py:414
  15.4 0.0 copy-done.1
  15.4 0.0 copy-start.2
  15.4 0.9 %near_panels.1.refs_1_ = f32[5,64,512]{2,1,0:T(8,128)S(1)} custom-call(bf16[2,16,1280]{2,1,0:T(8,128)(2,1)S(1)} %bitcast_dynamic-update-slice_fusion.pair_ref.panels_ref, bf16[5,16,1280]{2,1,0:T(8,128)(2,1)S(1)} %pad_maximum_fusion.panels_ref, bf16[1280,512]{1,0:T(8,128)(2,1)S(1)} %copy-done, f32[10,8,8,401]{3,2,1,0:T(8,128)S(1)} %bitcast.9), custom_call_target="tpu_custom_call" | custom-call | flops 419430400 | bytes 655360 | tf_op jit(solution)/shard_map/near_panels/pallas_call | solution.py:337
  16.4 0.0 collective-permute-done.4.panels_ref
  16.4 0.0 copy-done.2
  16.4 2.0 %swapped_panels.1 = f32[10,8,8,401]{3,2,1,0:T(8,128)} custom-call(s32[1,10]{1,0:T(1,128)S(1)} %copy-done.2, bf16[2,16,1280]{2,1,0:T(8,128)(2,1)S(1)} %bitcast_dynamic-update-slice_fusion.pair_ref.panels_ref, bf16[4,16,1280]{2,1,0:T(8,128)(2,1)S(1)} %collective-permute-done.4.panels_ref, bf16[1280,512]{1,0:T(8,128)(2,1)S(1)} %copy-done, ...), custom_call_target="tpu_custom_call" | custom-call | flops 335544320 | bytes 524288 | tf_op jit(solution)/shard_map/swapped_panels/pallas_call | solution.py:394
  (6 shorter events, 0.1 us)
Async XLA Ops:
  0.0 8.9 %copy-start = (bf16[1280,512]{1,0:T(8,128)(2,1)S(1)}, bf16[1280,512]{1,0:T(8,128)(2,1)}, u32[]{:S(2)}) copy-start(bf16[1280,512]{1,0:T(8,128)(2,1)} %constant.27.clone.table_ref) | copy-start | bytes 3932164
  2.8 1.6 %collective-permute-start = (bf16[16,1280]{1,0:T(8,128)(2,1)S(1)}, bf16[16,1280]{1,0:T(8,128)(2,1)S(1)}, u32[]{:S(2)}, u32[]{:S(2)}) collective-permute-start(bf16[16,1280]{1,0:T(8,128)(2,1)S(1)} %whiten.1), channel_id=1, source_target_pairs={{1,0},{0,1},{3,2},{2,3},{5,4},{4,5},{7,6},{6,7},{9,8},{8,9},{11,10... | collective-permute-start | bytes 122888 | tf_op jit(solution)/shard_map/ppermute | solution.py:414
  4.4 9.3 %collective-permute-start.2 = (bf16[2,16,1280]{2,1,0:T(8,128)(2,1)S(1)}, bf16[2,16,1280]{2,1,0:T(8,128)(2,1)S(1)}, u32[]{:S(2)}, u32[]{:S(2)}) collective-permute-start(bf16[2,16,1280]{2,1,0:T(8,128)(2,1)S(1)} %bitcast_dynamic-update-slice_fusion.pair_ref.panels_ref), channel_id=1, source_target_pairs={{14,0},{7,1},{8,2},{5,3},{2,4},{11,5},{12,6},{9,7},{6,8},{15,9},{0... | collective-permute-start | bytes 245768 | tf_op jit(solution)/shard_map/ppermute | solution.py:422
  5.5 8.3 %collective-permute-start.1 = (bf16[2,16,1280]{2,1,0:T(8,128)(2,1)S(1)}, bf16[2,16,1280]{2,1,0:T(8,128)(2,1)S(1)}, u32[]{:S(2)}, u32[]{:S(2)}) collective-permute-start(bf16[2,16,1280]{2,1,0:T(8,128)(2,1)S(1)} %bitcast_dynamic-update-slice_fusion.pair_ref.panels_ref), channel_id=1, source_target_pairs={{2,0},{5,1},{0,2},{7,3},{6,4},{9,5},{4,6},{11,7},{10,8},{13,9},{8,... | collective-permute-start | bytes 245768 | tf_op jit(solution)/shard_map/ppermute | solution.py:422
  5.7 8.1 %collective-permute-start.3 = (bf16[16,1280]{1,0:T(8,128)(2,1)S(1)}, bf16[16,1280]{1,0:T(8,128)(2,1)S(1)}, u32[]{:S(2)}, u32[]{:S(2)}) collective-permute-start(bf16[16,1280]{1,0:T(8,128)(2,1)S(1)} %slice_bitcast_fusion), channel_id=1, source_target_pairs={{8,0},{9,1},{10,2},{11,3},{12,4},{13,5},{14,6},{15,7},{0,8},{1,9},... | collective-permute-start | bytes 122888 | tf_op jit(solution)/shard_map/ppermute | solution.py:422
  8.9 6.5 %copy-start.1 = (f32[1,10,8,8,401]{4,3,2,1,0:T(8,128)S(1)}, f32[1,10,8,8,401]{4,3,2,1,0:T(8,128)}, u32[]{:S(2)}) copy-start(f32[1,10,8,8,401]{4,3,2,1,0:T(8,128)} %param.9) | copy-start | bytes 3079684
  13.8 2.6 %collective-permute-start.4 = (bf16[4,16,1280]{2,1,0:T(8,128)(2,1)S(1)}, bf16[4,16,1280]{2,1,0:T(8,128)(2,1)S(1)}, u32[]{:S(2)}, u32[]{:S(2)}) collective-permute-start(bf16[4,16,1280]{2,1,0:T(8,128)(2,1)S(1)} %pad_maximum_fusion.1), channel_id=1, source_target_pairs={{1,0},{0,1},{3,2},{2,3},{5,4},{4,5},{7,6},{6,7},{9,8},{8,9},{11,10... | collective-permute-start | bytes 491528 | tf_op jit(solution)/shard_map/ppermute | solution.py:414
  15.4 1.0 %copy-start.2 = (s32[1,10]{1,0:T(1,128)S(1)}, s32[1,10]{1,0:T(1,128)}, u32[]{:S(2)}) copy-start(s32[1,10]{1,0:T(1,128)} %slots_any.1) | copy-start | bytes 124

commit v12 on v11

--- a/solution.py
+++ b/solution.py
@@ -19,6 +19,7 @@
 EPS = 1e-06
 WHITEN_VMEM = 60 << 20
 CORR_VMEM = 24 << 20
+TOGETHER = 5
 
 SPLIT = 20
 FOLD = SAMPLES // SPLIT
@@ -311,8 +312,8 @@
 
 def products(which, panel_count, own, panels_ref, table, chans, cross, keep):
     found = which(panel_count)
-    for start in range(0, len(found), 2):
-        some = found[start : start + 2]
+    for start in range(0, len(found), TOGETHER):
+        some = found[start : start + TOGETHER]
         for j, (at, panel, wanted) in enumerate(some):
             cross_tile(own, panels_ref[at].astype(jnp.float32), chans, cross, start + j)
         rows = slice(start * chans * chans, (start + len(some)) * chans * chans)

time: 18.6 us -> 18.5 us (level)
  Pallas kernels: 6.22 us -> 5.97 us
  transfers between devices with their start and end apart: 5 -> 5, of which waited for: 2 -> 3; matrix products, arithmetic and copies ran while one was open for 0% -> 0% of each run, Pallas kernels for 8% -> 7%
where the time goes in v12:
time: 18.5 us; the launch traced here: 18.3 us
  starting transfers between devices  6.83 us (37%)
  Pallas kernels  5.97 us (32%)
  waiting for transfers between devices  5.37 us (29%)
    ppermute x3, starting transfers between devices, fetch(): return lax.ppermute(array, 'row', moves)  4.48 us
    ppermute x3, waiting for transfers between devices, fetch(): return lax.ppermute(array, 'row', moves)  4.36 us
    pallas_call x1, Pallas kernels, whiten(): pl.pallas_call(whiten_kernel, out_shape=pltpu.VMEM((rows, 2 * LANES), jnp...  2.76 us
    ppermute x2, starting transfers between devices, swap(): return lax.ppermute(array, 'row', [(i ^ 1, i) for i in range(panel_count)])  2.34 us
    pallas_call x1, Pallas kernels, last(): pl.pallas_call(functools.partial(last_kernel, panel_count, lists), out_sh...  1.89 us
    pallas_call x2, Pallas kernels, early(): pl.pallas_call(functools.partial(early_kernel, panel_count, which), out_s...  1.31 us
    ppermute x2, waiting for transfers between devices, swap(): return lax.ppermute(array, 'row', [(i ^ 1, i) for i in range(panel_count)])  1.01 us
  transfers between devices with their start and end apart: 5, of which 3 were waited for; matrix products, arithmetic and copies ran while one was open for 0% of the time, Pallas kernels for 7%

profile of v12, /device:TPU:25, one launch (start us, length us, event | category | flops | bytes accessed | tf_op | source)
XLA Modules:
  0.0 18.3 jit_solution(17217488004720958649)
XLA Ops:
  0.0 0.0 copy-start
  0.0 2.8 %whiten.1 = bf16[16,1280]{1,0:T(8,128)(2,1)S(1)} custom-call(bf16[8,2,12000]{2,1,0:T(2,128)(2,1)} %x_hbm.1, s32[2,8]{1,0:T(2,128)} %bitcast.13, bf16[600,1280]{1,0:T(8,128)(2,1)} %constant.26.clone.table_hbm), custom_call_target="tpu_custom_call" | custom-call | tf_op jit(solution)/shard_map/whiten/pallas_call | solution.py:194
  2.8 0.7 %collective-permute-start = (bf16[16,1280]{1,0:T(8,128)(2,1)S(1)}, bf16[16,1280]{1,0:T(8,128)(2,1)S(1)}, u32[]{:S(2)}, u32[]{:S(2)}) collective-permute-start(bf16[16,1280]{1,0:T(8,128)(2,1)S(1)} %whiten.1), channel_id=1, source_target_pairs={{1,0},{0,1},{3,2},{2,3},{5,4},{4,5},{7,6},{6,7},{9,8},{8,9},{11,10... | collective-permute-start | bytes 122888 | tf_op jit(solution)/shard_map/ppermute | solution.py:415
  3.5 0.9 %collective-permute-done = bf16[16,1280]{1,0:T(8,128)(2,1)S(1)} collective-permute-done((bf16[16,1280]{1,0:T(8,128)(2,1)S(1)}, bf16[16,1280]{1,0:T(8,128)(2,1)S(1)}, u32[]{:S(2)}, u32[]{:S(2)}) %collective-permute-start) | collective-permute-done | bytes 40992 | tf_op jit(solution)/shard_map/ppermute | solution.py:415
  4.4 1.1 %collective-permute-start.2 = (bf16[2,16,1280]{2,1,0:T(8,128)(2,1)S(1)}, bf16[2,16,1280]{2,1,0:T(8,128)(2,1)S(1)}, u32[]{:S(2)}, u32[]{:S(2)}) collective-permute-start(bf16[2,16,1280]{2,1,0:T(8,128)(2,1)S(1)} %bitcast_dynamic-update-slice_fusion.pair_ref.panels_ref), channel_id=1, source_target_pairs={{14,0},{7,1},{8,2},{5,3},{2,4},{11,5},{12,6},{9,7},{6,8},{15,9},{0... | collective-permute-start | bytes 245768 | tf_op jit(solution)/shard_map/ppermute | solution.py:423
  5.5 0.2 collective-permute-start.1
  5.7 3.2 %collective-permute-start.3 = (bf16[16,1280]{1,0:T(8,128)(2,1)S(1)}, bf16[16,1280]{1,0:T(8,128)(2,1)S(1)}, u32[]{:S(2)}, u32[]{:S(2)}) collective-permute-start(bf16[16,1280]{1,0:T(8,128)(2,1)S(1)} %slice_bitcast_fusion), channel_id=1, source_target_pairs={{8,0},{9,1},{10,2},{11,3},{12,4},{13,5},{14,6},{15,7},{0,8},{1,9},... | collective-permute-start | bytes 122888 | tf_op jit(solution)/shard_map/ppermute | solution.py:423
  8.9 0.0 copy-done
  8.9 0.0 copy-start.1
  8.9 0.5 %pair_panels.1.refs_0_ = f32[2,64,512]{2,1,0:T(8,128)S(1)} custom-call(bf16[2,16,1280]{2,1,0:T(8,128)(2,1)S(1)} %bitcast_dynamic-update-slice_fusion.pair_ref.panels_ref, bf16[2,16,1280]{2,1,0:T(8,128)(2,1)S(1)} %bitcast_dynamic-update-slice_fusion.pair_ref.panels_ref, bf16[1280,512]{1,0:T(8,128)(2,1)S(1)} %copy-done), custom_call_target="tpu_custom_call" | custom-call | flops 167772160 | bytes 262144 | tf_op jit(solution)/shard_map/pair_panels/pallas_call | solution.py:338
  9.4 4.4 %collective-permute-done.3 = bf16[16,1280]{1,0:T(8,128)(2,1)S(1)} collective-permute-done((bf16[16,1280]{1,0:T(8,128)(2,1)S(1)}, bf16[16,1280]{1,0:T(8,128)(2,1)S(1)}, u32[]{:S(2)}, u32[]{:S(2)}) %collective-permute-start.3) | collective-permute-done | bytes 40992 | tf_op jit(solution)/shard_map/ppermute | solution.py:423
  13.7 0.0 collective-permute-done.2
  13.7 0.0 collective-permute-done.1
  13.8 1.6 %collective-permute-start.4 = (bf16[4,16,1280]{2,1,0:T(8,128)(2,1)S(1)}, bf16[4,16,1280]{2,1,0:T(8,128)(2,1)S(1)}, u32[]{:S(2)}, u32[]{:S(2)}) collective-permute-start(bf16[4,16,1280]{2,1,0:T(8,128)(2,1)S(1)} %pad_maximum_fusion.1), channel_id=1, source_target_pairs={{1,0},{0,1},{3,2},{2,3},{5,4},{4,5},{7,6},{6,7},{9,8},{8,9},{11,10... | collective-permute-start | bytes 491528 | tf_op jit(solution)/shard_map/ppermute | solution.py:415
  15.4 0.0 copy-done.1
  15.4 0.0 copy-start.2
  15.4 0.8 %near_panels.1.refs_1_ = f32[5,64,512]{2,1,0:T(8,128)S(1)} custom-call(bf16[2,16,1280]{2,1,0:T(8,128)(2,1)S(1)} %bitcast_dynamic-update-slice_fusion.pair_ref.panels_ref, bf16[5,16,1280]{2,1,0:T(8,128)(2,1)S(1)} %pad_maximum_fusion.panels_ref, bf16[1280,512]{1,0:T(8,128)(2,1)S(1)} %copy-done, f32[10,8,8,401]{3,2,1,0:T(8,128)S(1)} %bitcast.9), custom_call_target="tpu_custom_call" | custom-call | flops 419430400 | bytes 655360 | tf_op jit(solution)/shard_map/near_panels/pallas_call | solution.py:338
  16.3 0.1 collective-permute-done.4.panels_ref
  16.4 0.0 copy-done.2
  16.4 1.9 %swapped_panels.1 = f32[10,8,8,401]{3,2,1,0:T(8,128)} custom-call(s32[1,10]{1,0:T(1,128)S(1)} %copy-done.2, bf16[2,16,1280]{2,1,0:T(8,128)(2,1)S(1)} %bitcast_dynamic-update-slice_fusion.pair_ref.panels_ref, bf16[4,16,1280]{2,1,0:T(8,128)(2,1)S(1)} %collective-permute-done.4.panels_ref, bf16[1280,512]{1,0:T(8,128)(2,1)S(1)} %copy-done, ...), custom_call_target="tpu_custom_call" | custom-call | flops 335544320 | bytes 524288 | tf_op jit(solution)/shard_map/swapped_panels/pallas_call | solution.py:395
  (6 shorter events, 0.1 us)
Async XLA Ops:
  0.0 8.9 %copy-start = (bf16[1280,512]{1,0:T(8,128)(2,1)S(1)}, bf16[1280,512]{1,0:T(8,128)(2,1)}, u32[]{:S(2)}) copy-start(bf16[1280,512]{1,0:T(8,128)(2,1)} %constant.27.clone.table_ref) | copy-start | bytes 3932164
  2.8 1.6 %collective-permute-start = (bf16[16,1280]{1,0:T(8,128)(2,1)S(1)}, bf16[16,1280]{1,0:T(8,128)(2,1)S(1)}, u32[]{:S(2)}, u32[]{:S(2)}) collective-permute-start(bf16[16,1280]{1,0:T(8,128)(2,1)S(1)} %whiten.1), channel_id=1, source_target_pairs={{1,0},{0,1},{3,2},{2,3},{5,4},{4,5},{7,6},{6,7},{9,8},{8,9},{11,10... | collective-permute-start | bytes 122888 | tf_op jit(solution)/shard_map/ppermute | solution.py:415
  4.4 9.3 %collective-permute-start.2 = (bf16[2,16,1280]{2,1,0:T(8,128)(2,1)S(1)}, bf16[2,16,1280]{2,1,0:T(8,128)(2,1)S(1)}, u32[]{:S(2)}, u32[]{:S(2)}) collective-permute-start(bf16[2,16,1280]{2,1,0:T(8,128)(2,1)S(1)} %bitcast_dynamic-update-slice_fusion.pair_ref.panels_ref), channel_id=1, source_target_pairs={{14,0},{7,1},{8,2},{5,3},{2,4},{11,5},{12,6},{9,7},{6,8},{15,9},{0... | collective-permute-start | bytes 245768 | tf_op jit(solution)/shard_map/ppermute | solution.py:423
  5.5 8.3 %collective-permute-start.1 = (bf16[2,16,1280]{2,1,0:T(8,128)(2,1)S(1)}, bf16[2,16,1280]{2,1,0:T(8,128)(2,1)S(1)}, u32[]{:S(2)}, u32[]{:S(2)}) collective-permute-start(bf16[2,16,1280]{2,1,0:T(8,128)(2,1)S(1)} %bitcast_dynamic-update-slice_fusion.pair_ref.panels_ref), channel_id=1, source_target_pairs={{2,0},{5,1},{0,2},{7,3},{6,4},{9,5},{4,6},{11,7},{10,8},{13,9},{8,... | collective-permute-start | bytes 245768 | tf_op jit(solution)/shard_map/ppermute | solution.py:423
  5.7 8.1 %collective-permute-start.3 = (bf16[16,1280]{1,0:T(8,128)(2,1)S(1)}, bf16[16,1280]{1,0:T(8,128)(2,1)S(1)}, u32[]{:S(2)}, u32[]{:S(2)}) collective-permute-start(bf16[16,1280]{1,0:T(8,128)(2,1)S(1)} %slice_bitcast_fusion), channel_id=1, source_target_pairs={{8,0},{9,1},{10,2},{11,3},{12,4},{13,5},{14,6},{15,7},{0,8},{1,9},... | collective-permute-start | bytes 122888 | tf_op jit(solution)/shard_map/ppermute | solution.py:423
  8.9 6.5 %copy-start.1 = (f32[1,10,8,8,401]{4,3,2,1,0:T(8,128)S(1)}, f32[1,10,8,8,401]{4,3,2,1,0:T(8,128)}, u32[]{:S(2)}) copy-start(f32[1,10,8,8,401]{4,3,2,1,0:T(8,128)} %param.9) | copy-start | bytes 3079684
  13.8 2.6 %collective-permute-start.4 = (bf16[4,16,1280]{2,1,0:T(8,128)(2,1)S(1)}, bf16[4,16,1280]{2,1,0:T(8,128)(2,1)S(1)}, u32[]{:S(2)}, u32[]{:S(2)}) collective-permute-start(bf16[4,16,1280]{2,1,0:T(8,128)(2,1)S(1)} %pad_maximum_fusion.1), channel_id=1, source_target_pairs={{1,0},{0,1},{3,2},{2,3},{5,4},{4,5},{7,6},{6,7},{9,8},{8,9},{11,10... | collective-permute-start | bytes 491528 | tf_op jit(solution)/shard_map/ppermute | solution.py:415
  15.4 1.0 %copy-start.2 = (s32[1,10]{1,0:T(1,128)S(1)}, s32[1,10]{1,0:T(1,128)}, u32[]{:S(2)}) copy-start(s32[1,10]{1,0:T(1,128)} %slots_any.1) | copy-start | bytes 124

commit v13 on v12

--- a/solution.py
+++ b/solution.py
@@ -424,10 +424,10 @@
 
     table = jnp.asarray(lag_table())
     twice = jnp.stack([own, own])
-    pair = lax.optimization_barrier(lax.dynamic_update_slice(twice, swap(own)[None], (1, 0, 0)))
+    pair, own = lax.optimization_barrier((lax.dynamic_update_slice(twice, swap(own)[None], (1, 0, 0)), own))
     near = fetch(pair, (1, -1), (2, 2))
     next_near = fetch(pair, (-1, 3), (3, 1))
-    far = fetch(pair[0], (4, 4), (4, 4))
+    far = fetch(own, (4, 4), (4, 4))
     chans = stack.shape[1]
     first = early(pair_panels, 2, panel_count, chans, pair, pair, table)
     near, next_near, far, first = lax.optimization_barrier((near, next_near, far, first))

time: 18.5 us -> 18.5 us (level)
  no operation moved by 1% of the time
where the time goes in v13:
time: 18.5 us; the launch traced here: 18.3 us
  starting transfers between devices  6.83 us (37%)
  Pallas kernels  5.97 us (32%)
  waiting for transfers between devices  5.37 us (29%)
    ppermute x3, starting transfers between devices, fetch(): return lax.ppermute(array, 'row', moves)  4.48 us
    ppermute x3, waiting for transfers between devices, fetch(): return lax.ppermute(array, 'row', moves)  4.36 us
    pallas_call x1, Pallas kernels, whiten(): pl.pallas_call(whiten_kernel, out_shape=pltpu.VMEM((rows, 2 * LANES), jnp...  2.76 us
    ppermute x2, starting transfers between devices, swap(): return lax.ppermute(array, 'row', [(i ^ 1, i) for i in range(panel_count)])  2.34 us
    pallas_call x1, Pallas kernels, last(): pl.pallas_call(functools.partial(last_kernel, panel_count, lists), out_sh...  1.89 us
    pallas_call x2, Pallas kernels, early(): pl.pallas_call(functools.partial(early_kernel, panel_count, which), out_s...  1.31 us
    ppermute x2, waiting for transfers between devices, swap(): return lax.ppermute(array, 'row', [(i ^ 1, i) for i in range(panel_count)])  1.01 us
  transfers between devices with their start and end apart: 5, of which 3 were waited for; matrix products, arithmetic and copies ran while one was open for 0% of the time, Pallas kernels for 7%

profile of v13, /device:TPU:25, one launch (start us, length us, event | category | flops | bytes accessed | tf_op | source)
XLA Modules:
  0.0 18.3 jit_solution(4437619620066870242)
XLA Ops:
  0.0 0.0 copy-start
  0.0 2.8 %whiten.1 = bf16[16,1280]{1,0:T(8,128)(2,1)S(1)} custom-call(bf16[8,2,12000]{2,1,0:T(2,128)(2,1)} %x_hbm.1, s32[2,8]{1,0:T(2,128)} %bitcast.11, bf16[600,1280]{1,0:T(8,128)(2,1)} %constant.26.clone.table_hbm), custom_call_target="tpu_custom_call" | custom-call | tf_op jit(solution)/shard_map/whiten/pallas_call | solution.py:194
  2.8 0.7 %collective-permute-start = (bf16[16,1280]{1,0:T(8,128)(2,1)S(1)}, bf16[16,1280]{1,0:T(8,128)(2,1)S(1)}, u32[]{:S(2)}, u32[]{:S(2)}) collective-permute-start(bf16[16,1280]{1,0:T(8,128)(2,1)S(1)} %whiten.1), channel_id=1, source_target_pairs={{1,0},{0,1},{3,2},{2,3},{5,4},{4,5},{7,6},{6,7},{9,8},{8,9},{11,10... | collective-permute-start | bytes 122888 | tf_op jit(solution)/shard_map/ppermute | solution.py:415
  3.5 0.9 %collective-permute-done = bf16[16,1280]{1,0:T(8,128)(2,1)S(1)} collective-permute-done((bf16[16,1280]{1,0:T(8,128)(2,1)S(1)}, bf16[16,1280]{1,0:T(8,128)(2,1)S(1)}, u32[]{:S(2)}, u32[]{:S(2)}) %collective-permute-start) | collective-permute-done | bytes 40992 | tf_op jit(solution)/shard_map/ppermute | solution.py:415
  4.4 1.1 %collective-permute-start.2 = (bf16[2,16,1280]{2,1,0:T(8,128)(2,1)S(1)}, bf16[2,16,1280]{2,1,0:T(8,128)(2,1)S(1)}, u32[]{:S(2)}, u32[]{:S(2)}) collective-permute-start(bf16[2,16,1280]{2,1,0:T(8,128)(2,1)S(1)} %bitcast_dynamic-update-slice_fusion.pair_ref.panels_ref), channel_id=1, source_target_pairs={{14,0},{7,1},{8,2},{5,3},{2,4},{11,5},{12,6},{9,7},{6,8},{15,9},{0... | collective-permute-start | bytes 245768 | tf_op jit(solution)/shard_map/ppermute | solution.py:423
  5.5 0.2 collective-permute-start.1
  5.7 3.2 %collective-permute-start.3 = (bf16[16,1280]{1,0:T(8,128)(2,1)S(1)}, bf16[16,1280]{1,0:T(8,128)(2,1)S(1)}, u32[]{:S(2)}, u32[]{:S(2)}) collective-permute-start(bf16[16,1280]{1,0:T(8,128)(2,1)S(1)} %whiten.1), channel_id=1, source_target_pairs={{8,0},{9,1},{10,2},{11,3},{12,4},{13,5},{14,6},{15,7},{0,8},{1,9},... | collective-permute-start | bytes 122888 | tf_op jit(solution)/shard_map/ppermute | solution.py:423
  8.9 0.0 copy-done
  8.9 0.0 copy-start.1
  8.9 0.5 %pair_panels.1.refs_0_ = f32[2,64,512]{2,1,0:T(8,128)S(1)} custom-call(bf16[2,16,1280]{2,1,0:T(8,128)(2,1)S(1)} %bitcast_dynamic-update-slice_fusion.pair_ref.panels_ref, bf16[2,16,1280]{2,1,0:T(8,128)(2,1)S(1)} %bitcast_dynamic-update-slice_fusion.pair_ref.panels_ref, bf16[1280,512]{1,0:T(8,128)(2,1)S(1)} %copy-done), custom_call_target="tpu_custom_call" | custom-call | flops 167772160 | bytes 262144 | tf_op jit(solution)/shard_map/pair_panels/pallas_call | solution.py:338
  9.4 4.4 %collective-permute-done.3 = bf16[16,1280]{1,0:T(8,128)(2,1)S(1)} collective-permute-done((bf16[16,1280]{1,0:T(8,128)(2,1)S(1)}, bf16[16,1280]{1,0:T(8,128)(2,1)S(1)}, u32[]{:S(2)}, u32[]{:S(2)}) %collective-permute-start.3) | collective-permute-done | bytes 40992 | tf_op jit(solution)/shard_map/ppermute | solution.py:423
  13.7 0.0 collective-permute-done.2
  13.7 0.0 collective-permute-done.1
  13.8 1.6 %collective-permute-start.4 = (bf16[4,16,1280]{2,1,0:T(8,128)(2,1)S(1)}, bf16[4,16,1280]{2,1,0:T(8,128)(2,1)S(1)}, u32[]{:S(2)}, u32[]{:S(2)}) collective-permute-start(bf16[4,16,1280]{2,1,0:T(8,128)(2,1)S(1)} %pad_maximum_fusion.1), channel_id=1, source_target_pairs={{1,0},{0,1},{3,2},{2,3},{5,4},{4,5},{7,6},{6,7},{9,8},{8,9},{11,10... | collective-permute-start | bytes 491528 | tf_op jit(solution)/shard_map/ppermute | solution.py:415
  15.4 0.0 copy-done.1
  15.4 0.0 copy-start.2
  15.4 0.8 %near_panels.1.refs_1_ = f32[5,64,512]{2,1,0:T(8,128)S(1)} custom-call(bf16[2,16,1280]{2,1,0:T(8,128)(2,1)S(1)} %bitcast_dynamic-update-slice_fusion.pair_ref.panels_ref, bf16[5,16,1280]{2,1,0:T(8,128)(2,1)S(1)} %pad_maximum_fusion.panels_ref, bf16[1280,512]{1,0:T(8,128)(2,1)S(1)} %copy-done, f32[10,8,8,401]{3,2,1,0:T(8,128)S(1)} %bitcast.7), custom_call_target="tpu_custom_call" | custom-call | flops 419430400 | bytes 655360 | tf_op jit(solution)/shard_map/near_panels/pallas_call | solution.py:338
  16.3 0.1 collective-permute-done.4.panels_ref
  16.4 0.0 copy-done.2
  16.4 1.9 %swapped_panels.1 = f32[10,8,8,401]{3,2,1,0:T(8,128)} custom-call(s32[1,10]{1,0:T(1,128)S(1)} %copy-done.2, bf16[2,16,1280]{2,1,0:T(8,128)(2,1)S(1)} %bitcast_dynamic-update-slice_fusion.pair_ref.panels_ref, bf16[4,16,1280]{2,1,0:T(8,128)(2,1)S(1)} %collective-permute-done.4.panels_ref, bf16[1280,512]{1,0:T(8,128)(2,1)S(1)} %copy-done, ...), custom_call_target="tpu_custom_call" | custom-call | flops 335544320 | bytes 524288 | tf_op jit(solution)/shard_map/swapped_panels/pallas_call | solution.py:395
  (5 shorter events, 0.1 us)
Async XLA Ops:
  0.0 8.9 %copy-start = (bf16[1280,512]{1,0:T(8,128)(2,1)S(1)}, bf16[1280,512]{1,0:T(8,128)(2,1)}, u32[]{:S(2)}) copy-start(bf16[1280,512]{1,0:T(8,128)(2,1)} %constant.27.clone.table_ref) | copy-start | bytes 3932164
  2.8 1.6 %collective-permute-start = (bf16[16,1280]{1,0:T(8,128)(2,1)S(1)}, bf16[16,1280]{1,0:T(8,128)(2,1)S(1)}, u32[]{:S(2)}, u32[]{:S(2)}) collective-permute-start(bf16[16,1280]{1,0:T(8,128)(2,1)S(1)} %whiten.1), channel_id=1, source_target_pairs={{1,0},{0,1},{3,2},{2,3},{5,4},{4,5},{7,6},{6,7},{9,8},{8,9},{11,10... | collective-permute-start | bytes 122888 | tf_op jit(solution)/shard_map/ppermute | solution.py:415
  4.4 9.3 %collective-permute-start.2 = (bf16[2,16,1280]{2,1,0:T(8,128)(2,1)S(1)}, bf16[2,16,1280]{2,1,0:T(8,128)(2,1)S(1)}, u32[]{:S(2)}, u32[]{:S(2)}) collective-permute-start(bf16[2,16,1280]{2,1,0:T(8,128)(2,1)S(1)} %bitcast_dynamic-update-slice_fusion.pair_ref.panels_ref), channel_id=1, source_target_pairs={{14,0},{7,1},{8,2},{5,3},{2,4},{11,5},{12,6},{9,7},{6,8},{15,9},{0... | collective-permute-start | bytes 245768 | tf_op jit(solution)/shard_map/ppermute | solution.py:423
  5.5 8.3 %collective-permute-start.1 = (bf16[2,16,1280]{2,1,0:T(8,128)(2,1)S(1)}, bf16[2,16,1280]{2,1,0:T(8,128)(2,1)S(1)}, u32[]{:S(2)}, u32[]{:S(2)}) collective-permute-start(bf16[2,16,1280]{2,1,0:T(8,128)(2,1)S(1)} %bitcast_dynamic-update-slice_fusion.pair_ref.panels_ref), channel_id=1, source_target_pairs={{2,0},{5,1},{0,2},{7,3},{6,4},{9,5},{4,6},{11,7},{10,8},{13,9},{8,... | collective-permute-start | bytes 245768 | tf_op jit(solution)/shard_map/ppermute | solution.py:423
  5.7 8.1 %collective-permute-start.3 = (bf16[16,1280]{1,0:T(8,128)(2,1)S(1)}, bf16[16,1280]{1,0:T(8,128)(2,1)S(1)}, u32[]{:S(2)}, u32[]{:S(2)}) collective-permute-start(bf16[16,1280]{1,0:T(8,128)(2,1)S(1)} %whiten.1), channel_id=1, source_target_pairs={{8,0},{9,1},{10,2},{11,3},{12,4},{13,5},{14,6},{15,7},{0,8},{1,9},... | collective-permute-start | bytes 122888 | tf_op jit(solution)/shard_map/ppermute | solution.py:423
  8.9 6.6 %copy-start.1 = (f32[1,10,8,8,401]{4,3,2,1,0:T(8,128)S(1)}, f32[1,10,8,8,401]{4,3,2,1,0:T(8,128)}, u32[]{:S(2)}) copy-start(f32[1,10,8,8,401]{4,3,2,1,0:T(8,128)} %param.9) | copy-start | bytes 3079684
  13.8 2.6 %collective-permute-start.4 = (bf16[4,16,1280]{2,1,0:T(8,128)(2,1)S(1)}, bf16[4,16,1280]{2,1,0:T(8,128)(2,1)S(1)}, u32[]{:S(2)}, u32[]{:S(2)}) collective-permute-start(bf16[4,16,1280]{2,1,0:T(8,128)(2,1)S(1)} %pad_maximum_fusion.1), channel_id=1, source_target_pairs={{1,0},{0,1},{3,2},{2,3},{5,4},{4,5},{7,6},{6,7},{9,8},{8,9},{11,10... | collective-permute-start | bytes 491528 | tf_op jit(solution)/shard_map/ppermute | solution.py:415
  15.4 1.0 %copy-start.2 = (s32[1,10]{1,0:T(1,128)S(1)}, s32[1,10]{1,0:T(1,128)}, u32[]{:S(2)}) copy-start(s32[1,10]{1,0:T(1,128)} %slots_any.1) | copy-start | bytes 124
